TPU v7x, 512 devices: a whole 4x8x8 slice. The times are simulated.
512 devices in a mesh: mem: 4 (over x), lat: 4 (over y_hi, core), lon: 32 (over z, y_lo).
Axes of the slice: x: 4, y: 8 (y_hi: 2, y_lo: 4; y = y_hi * 4 + y_lo), z: 8, core: 2. Of those that a mesh axis runs over, the one named last changes fastest.
Arguments:
- initial_temp: float32 [100, 128, 512], P(None, 'lon', 'lat'), may hold values from -6 to 6
- land_mask: int32 [128, 512], P('lon', 'lat'), may hold values 0 or 1
- pert_table: float32 [16, 100], replicated, may hold values from 0.03 to 0.24
- pert_index: int32 [8], P('mem'), may hold values from 0 to 15
- base_kh: float32 [100], replicated, may hold values from 0.03 to 0.24
- member_mix: bfloat16 [8, 100, 100], P('mem'), may hold values from -0.15625 to 0.15625
- base_mix: bfloat16 [100, 100], replicated, may hold values from -0.15625 to 0.15625
- owner: int32 [32768, 1], P(('lat', 'lon')), may hold values from 0 to 127; in each aligned block of 256 rows (0 to 255, 256 to 511, ...) at most 4 rows name the same one
- column: int32 [32768], P(('lat', 'lon')), may hold values from 0 to 511
- interp_w: float32 [32768, 100], P(('lat', 'lon')), may hold values from 0 to 1
- obs_inv_var: float32 [32768, 100], P(('lat', 'lon')), may hold values from 1 to 16
- observed: float32 [32768, 100], P(('lat', 'lon')), may hold values from -6 to 6
Outputs:
- member_temp: bfloat16 [8, 100, 128, 512], P('mem', None, 'lon', 'lat')
- base_temp: bfloat16 [100, 128, 512], P(None, 'lon', 'lat')
- gram_block: float32 [8, 8], replicated
- projection: float32 [8], replicated
- misfit: float32 [32768, 100], P(('lat', 'lon'))
Inputs may be any that keep to these rules, and one draw needn't show every extreme that they name: Within the records of one device no owner is named more than 4 times, and in every draw some owner is named exactly 4 times by some device's records. The column within the owner's block is the longitude offset times 128 plus the latitude offset.
All inputs are finite; a program needn't handle non-finite values. No bound on the sum of `land_mask` on one device may be relied on, other than what follows from the above.
Results may differ from a plain program's by a relative error of at most 0.012.
Values may be sent and summed in bfloat16 or wider, within the bound.
No kernel may reach another device: no remote copies, remote signals or barrier semaphores. Data moves between devices by JAX's collectives and lax.ppermute only.
A program may use at most 64 MiB of HBM per device.

v0:
```python
import jax
import jax.numpy as jnp
from jax import lax
from jax.sharding import PartitionSpec as P

STEPS = 5


def padded_2(cells, sides, width, closed):
    for axis, dim in sides:
        count = lax.axis_size(axis)
        ends = count if closed else count - 1
        head = lax.slice_in_dim(cells, 0, width, axis=dim)
        tail = lax.slice_in_dim(cells, cells.shape[dim] - width, cells.shape[dim], axis=dim)
        cells = jnp.concatenate(
            [
                lax.ppermute(tail, axis, [(i, (i + 1) % count) for i in range(ends)]),
                cells,
                lax.ppermute(head, axis, [((i + 1) % count, i) for i in range(ends)]),
            ],
            axis=dim,
        )
    return cells


def on_device(
    initial_temp,
    land_mask,
    pert_table,
    pert_index,
    base_kh,
    member_mix,
    base_mix,
    owner,
    column,
    interp_w,
    obs_inv_var,
    observed,
):
    members = pert_index.shape[0]
    levels = initial_temp.shape[0]
    width_lon = initial_temp.shape[1]
    width_lat = initial_temp.shape[2]
    table_rows = pert_table.shape[0]
    chooser = (pert_index[:, None] == jnp.arange(table_rows)[None, :]).astype(jnp.float32)
    member_kh = jnp.dot(chooser, pert_table, precision=lax.Precision.HIGHEST)
    run_kh = jnp.concatenate([member_kh, base_kh[None, :]], 0)
    run_mix = jnp.concatenate([member_mix, base_mix[None]], 0)
    run_count = members + 1
    fields = jnp.broadcast_to(
        initial_temp.astype(jnp.bfloat16)[None], (run_count, levels, width_lon, width_lat)
    )
    total_lat = width_lat * lax.axis_size("lat")
    lat_start = lax.axis_index("lat") * width_lat
    ocean_open = land_mask.astype(jnp.float32)
    for step_index in range(STEPS):
        lon_padded = padded_2(fields, (("lon", 2),), 1, True)
        padded = padded_2(lon_padded, (("lat", 3),), 1, False)
        global_rows = lat_start - (1 - 1) + jnp.arange(width_lat + 2 * (1 - 1))
        has_next = (global_rows < total_lat - 1).astype(jnp.float32)
        has_prior = (global_rows > 0).astype(jnp.float32)
        widened = padded.astype(jnp.float32)
        values = widened[:, :, 1:-1, 1:-1]
        laplace = widened[:, :, 2:, 1:-1] + widened[:, :, :-2, 1:-1] - 2.0 * values
        laplace = (
            laplace
            + has_next * (widened[:, :, 1:-1, 2:] - values)
            + has_prior * (widened[:, :, 1:-1, :-2] - values)
        )
        right_side = (values + run_kh[:, :, None, None] * laplace).astype(jnp.bfloat16)
        vertical = right_side.astype(jnp.float32) + jnp.einsum(
            "rkj,rjab->rkab", run_mix, right_side, preferred_element_type=jnp.float32
        )
        fields = (values + ocean_open * (vertical - values)).astype(jnp.bfloat16)
    owners = lax.axis_size("lat") * lax.axis_size("lon")
    prof_dev = owner.shape[0]
    capacity = max(2, 2 * prof_dev // owners)
    target = owner[:, 0]
    matches = (target[:, None] == jnp.arange(owners)[None, :]).astype(jnp.int32)
    earlier = jnp.cumsum(matches, 0) - matches
    slot_rank = jnp.sum(earlier * matches, 1)
    position = target * capacity + slot_rank
    send_ids = (
        jnp.full((owners * capacity,), -1, jnp.int32)
        .at[position]
        .set(column)
        .reshape(owners, capacity)
    )
    records = jnp.stack([interp_w, obs_inv_var, observed], 1)
    send_records = (
        jnp.zeros((owners * capacity, 3, levels), jnp.float32)
        .at[position]
        .set(records)
        .reshape(owners, capacity, 3, levels)
    )
    columns_flat = fields.reshape(run_count, levels, width_lon * width_lat)
    column_ids = lax.all_to_all(send_ids, ("lat", "lon"), split_axis=0, concat_axis=0, tiled=True)
    record_rows = lax.all_to_all(
        send_records, ("lat", "lon"), split_axis=0, concat_axis=0, tiled=True
    )
    sources = column_ids.shape[0]
    slot_count = column_ids.shape[1]
    usable = (column_ids >= 0).astype(jnp.float32).reshape(-1)
    picked = jnp.take(columns_flat, jnp.maximum(column_ids, 0).reshape(-1), axis=2).astype(
        jnp.float32
    )
    deeper = jnp.concatenate([picked[:, 1:], picked[:, -1:]], 1)
    flat_records = record_rows.reshape(sources * slot_count, 3, levels)
    weight = flat_records[:, 0].T
    inv_var = flat_records[:, 1].T * usable
    measured = flat_records[:, 2].T
    modeled = weight * picked + (1.0 - weight) * deeper
    green_cols = ((modeled[:members] - modeled[members]) * usable).astype(jnp.bfloat16)
    misfit = (measured - modeled[members]) * usable
    extras = jnp.stack([inv_var, misfit], 0)
    green_cols, extras = (
        green_cols.reshape(members, levels, sources, slot_count),
        extras.reshape(2, levels, sources, slot_count),
    )
    owner_misfit = jnp.transpose(extras[1], (1, 2, 0))
    returned = lax.all_to_all(owner_misfit, ("lat", "lon"), split_axis=0, concat_axis=0, tiled=True)
    misfit_rows = jnp.take(returned.reshape(owners * capacity, levels), position, axis=0)
    green_cols = green_cols.reshape(members, levels, -1)
    extras = extras.reshape(2, levels, -1)
    normalizer = 1.0 / (prof_dev * owners * levels)
    green_all = lax.all_gather(green_cols, "mem", axis=0, tiled=True)
    green_float = green_all.astype(jnp.float32)
    weighted = green_float * extras[0]
    gram_part = (
        jnp.einsum("mks,nks->mn", weighted, green_float, precision=lax.Precision.HIGHEST)
        * normalizer
    )
    proj_part = (
        jnp.einsum("mks,ks->m", weighted, extras[1], precision=lax.Precision.HIGHEST) * normalizer
    )
    gram_part, proj_part = (gram_part, proj_part)
    gram_block, projection = lax.psum((gram_part, proj_part), ("lat", "lon"))
    return (fields[:members], fields[members], gram_block, projection, misfit_rows)


def solution(mesh):
    placed = (
        P(None, "lon", "lat"),
        P("lon", "lat"),
        P(),
        P("mem"),
        P(),
        P("mem", None, None),
        P(),
        P(("lat", "lon"), None),
        P(("lat", "lon")),
        P(("lat", "lon"), None),
        P(("lat", "lon"), None),
        P(("lat", "lon"), None),
    )
    return jax.shard_map(
        on_device,
        mesh=mesh,
        in_specs=placed,
        out_specs=(
            P("mem", None, "lon", "lat"),
            P(None, "lon", "lat"),
            P(),
            P(),
            P(("lat", "lon"), None),
        ),
        check_vma=False,
    )
```

profile of v0, /device:TPU:258, one launch (start us, length us, event | category | flops | bytes accessed | tf_op | source)
XLA Modules:
  0.0 559.3 jit_solution(4841442048766482967)
XLA Ops:
  1.6 4.6 collective-permute-start.1
  6.3 1.9 collective-permute-start
  10.8 5.7 %collective-permute-done = bf16[3,100,1,128]{3,1,2,0:T(8,128)(2,1)S(1)} collective-permute-done((bf16[3,100,1,128]{3,1,2,0:T(8,128)(2,1)S(1)}, bf16[3,100,1,128]{3,1,2,0:T(8,128)(2,1)S(1)}, u32[]{:S(2)}, u32[]{:S(2)}) %collective-permute-start) | collective-permute-done | bytes 76832 | tf_op jit(solution)/shard_map/ppermute | solution.py:17
  16.8 1.3 collective-permute-start.2
  18.1 1.3 collective-permute-start.3
  19.6 5.7 %collective-permute-done.3 = bf16[3,100,6,1]{3,1,2,0:T(8,128)(2,1)S(1)} collective-permute-done((bf16[3,100,6,1]{3,1,2,0:T(8,128)(2,1)S(1)}, bf16[3,100,6,1]{3,1,2,0:T(8,128)(2,1)S(1)}, u32[]{:S(2)}, u32[]{:S(2)}) %collective-permute-start.3) | collective-permute-done | bytes 3632 | tf_op jit(solution)/shard_map/ppermute | solution.py:19
  25.8 1.6 fusion.19
  27.4 1.9 collective-permute-start.4
  29.4 7.8 %collective-permute-start.5 = (bf16[3,100,1,128]{3,1,2,0:T(8,128)(2,1)S(1)}, bf16[3,100,1,128]{3,1,2,0:T(8,128)(2,1)S(1)}, u32[]{:S(2)}, u32[]{:S(2)}) collective-permute-start(bf16[3,100,1,128]{3,1,2,0:T(8,128)(2,1)S(1)} %get-tuple-element.41), channel_id=1, source_target_pairs={{1,0},{2,1},{3,2},{4,3},{5,4},{6,5},{7,6},{8,7},{9,8},{10,9},{11,1... | collective-permute-start | bytes 230408 | tf_op jit(solution)/shard_map/ppermute | solution.py:19
  37.7 1.6 collective-permute-done.5
  39.5 13.3 %collective-permute-start.6 = (bf16[3,100,6,1]{3,1,2,0:T(8,128)(2,1)S(1)}, bf16[3,100,6,1]{3,1,2,0:T(8,128)(2,1)S(1)}, u32[]{:S(2)}, u32[]{:S(2)}) collective-permute-start(bf16[3,100,6,1]{3,1,2,0:T(8,128)(2,1)S(1)} %get-tuple-element.30), channel_id=1, source_target_pairs={{0,32},{32,64},{64,96},{1,33},{33,65},{65,97},{2,34},{34,66},{66,9... | collective-permute-start | bytes 10808 | tf_op jit(solution)/shard_map/ppermute | solution.py:17
  52.8 1.3 collective-permute-start.7
  54.1 1.6 scatter_custom_fusion.1
  56.4 18.1 %all-to-all-start.1 = ((s32[128,1,4]{2,1,0:T(1,128)}), s32[128,1,4]{2,1,0:T(1,128)S(1)}, u32[]{:S(2)}, u32[]{:S(2)}) async-start(s32[128,1,4]{2,1,0:T(1,128)} %bitcast.22), calls=%async_computation.1 | async-start | bytes 131072 | tf_op jit(solution)/shard_map/all_to_all | solution.py:97
  75.2 1.6 fusion.20
  76.8 3.4 collective-permute-start.8
  80.2 6.4 %collective-permute-start.9 = (bf16[3,100,1,128]{3,1,2,0:T(8,128)(2,1)S(1)}, bf16[3,100,1,128]{3,1,2,0:T(8,128)(2,1)S(1)}, u32[]{:S(2)}, u32[]{:S(2)}) collective-permute-start(bf16[3,100,1,128]{3,1,2,0:T(8,128)(2,1)S(1)} %get-tuple-element.39), channel_id=1, source_target_pairs={{1,0},{2,1},{3,2},{4,3},{5,4},{6,5},{7,6},{8,7},{9,8},{10,9},{11,1... | collective-permute-start | bytes 230408 | tf_op jit(solution)/shard_map/ppermute | solution.py:19
  87.3 1.3 collective-permute-done.9
  89.8 1.3 collective-permute-start.10
  91.1 1.5 collective-permute-start.11
  93.0 7.1 %scatter_fusion = f32[512,3,100]{2,1,0:T(4,128)S(1)} fusion(f32[512,3,100]{2,1,0:T(4,128)S(1)} %broadcast_in_dim.33, s32[256]{0:T(256)S(1)} %bitcast.104, f32[256,3,100]{2,1,0:T(4,128)S(1)} %copy.45), kind=kCustom, calls=%fused_computation.2 | custom fusion | bytes 922624 | tf_op jit(solution)/shard_map/scatter | solution.py:93
  101.7 1.6 fusion.21
  103.3 1.9 collective-permute-start.12
  105.2 8.2 %collective-permute-start.13 = (bf16[3,100,1,128]{3,1,2,0:T(8,128)(2,1)S(1)}, bf16[3,100,1,128]{3,1,2,0:T(8,128)(2,1)S(1)}, u32[]{:S(2)}, u32[]{:S(2)}) collective-permute-start(bf16[3,100,1,128]{3,1,2,0:T(8,128)(2,1)S(1)} %get-tuple-element.37), channel_id=1, source_target_pairs={{1,0},{2,1},{3,2},{4,3},{5,4},{6,5},{7,6},{8,7},{9,8},{10,9},{11,1... | collective-permute-start | bytes 230408 | tf_op jit(solution)/shard_map/ppermute | solution.py:19
  113.4 21.5 %all-to-all-start = ((f32[128,4,3,100]{3,1,2,0:T(4,128)}), f32[128,4,3,100]{3,1,2,0:T(4,128)S(1)}, u32[]{:S(2)}, u32[]{:S(2)}) async-start(f32[128,4,3,100]{3,1,2,0:T(4,128)} %copy.47), calls=%async_computation | async-start | bytes 1572864 | tf_op jit(solution)/shard_map/all_to_all | solution.py:98
  135.5 2.3 collective-permute-start.14
  137.8 1.3 collective-permute-start.15
  140.1 6.5 %collective-permute-done.15 = bf16[3,100,6,1]{3,1,2,0:T(8,128)(2,1)} collective-permute-done((bf16[3,100,6,1]{3,1,2,0:T(8,128)(2,1)S(1)}, bf16[3,100,6,1]{3,1,2,0:T(8,128)(2,1)}, u32[]{:S(2)}, u32[]{:S(2)}) %collective-permute-start.15) | collective-permute-done | bytes 3632 | tf_op jit(solution)/shard_map/ppermute | solution.py:19
  146.7 1.7 maximum_convert_fusion.3
  148.4 1.6 fusion.22
  150.0 2.5 collective-permute-start.16
  152.5 7.3 %collective-permute-start.17 = (bf16[3,100,1,128]{3,1,2,0:T(8,128)(2,1)S(1)}, bf16[3,100,1,128]{3,1,2,0:T(8,128)(2,1)S(1)}, u32[]{:S(2)}, u32[]{:S(2)}) collective-permute-start(bf16[3,100,1,128]{3,1,2,0:T(8,128)(2,1)S(1)} %get-tuple-element.35), channel_id=1, source_target_pairs={{1,0},{2,1},{3,2},{4,3},{5,4},{6,5},{7,6},{8,7},{9,8},{10,9},{11,1... | collective-permute-start | bytes 230408 | tf_op jit(solution)/shard_map/ppermute | solution.py:19
  160.0 1.6 collective-permute-done.16
  162.1 23.8 %collective-permute-start.18 = (bf16[3,100,6,1]{3,1,2,0:T(8,128)(2,1)S(1)}, bf16[3,100,6,1]{3,1,2,0:T(8,128)(2,1)S(1)}, u32[]{:S(2)}, u32[]{:S(2)}) collective-permute-start(bf16[3,100,6,1]{3,1,2,0:T(8,128)(2,1)S(1)} %get-tuple-element.24), channel_id=1, source_target_pairs={{0,32},{32,64},{64,96},{1,33},{33,65},{65,97},{2,34},{34,66},{66,9... | collective-permute-start | bytes 10808 | tf_op jit(solution)/shard_map/ppermute | solution.py:17
  186.0 1.5 collective-permute-start.19
  188.5 1.7 collective-permute-done.19
  190.2 1.7 maximum_convert_fusion.4
  192.0 1.6 fusion.23
  194.3 2.1 gather_fusion
  196.4 1.8 convert_bitcast_fusion
  201.2 1.9 fusion.36
  203.4 1.5 fusion.94
  206.1 24.3 %all-to-all-start.2 = ((f32[128,4,100]{2,1,0:T(4,128)}), f32[128,4,100]{2,1,0:T(4,128)S(1)}, u32[]{:S(2)}, u32[]{:S(2)}) async-start(f32[128,4,100]{2,1,0:T(4,128)} %bitcast.35), calls=%async_computation.2 | async-start | bytes 524288 | tf_op jit(solution)/shard_map/all_to_all | solution.py:121
  230.4 1.1 copy.60
  231.5 14.8 %all_gather.3 = bf16[8,100,512]{2,1,0:T(8,128)(2,1)S(1)} all-gather(bf16[2,100,512]{2,1,0:T(8,128)(2,1)S(1)} %copy.52), channel_id=1, replica_groups=mesh['mem'=4,'lat'=4,'lon'=32] {'mem'}, dimensions={0}, use_global_device_ids=true | all-gather | bytes 1024000 | tf_op jit(solution)/shard_map/all_gather | solution.py:126
  246.6 3.9 fusion.33
  250.4 2.6 fusion.27
  253.0 304.7 %all-reduce = (f32[8,8]{1,0:T(8,128)}, f32[8]{0:T(128)}) all-reduce(f32[8,8]{1,0:T(8,128)S(1)} %fusion.27, f32[8]{0:T(128)S(1)} %fusion.33), channel_id=1, replica_groups=mesh['mem'=4,'lat'=4,'lon'=32] {'lat','lon'}, use_global_device_ids=true, to_apply=%region_5.6 | all-reduce | flops 72 | bytes 576 | tf_op jit(solution)/shard_map/psum | solution.py:137
  (110 shorter events, 20.8 us)
Async XLA Ops:
  0.6 8.6 %copy-start = (f32[16,100]{1,0:T(8,128)S(1)}, f32[16,100]{1,0:T(8,128)}, u32[]{:S(2)}) copy-start(f32[16,100]{1,0:T(8,128)} %param.14) | copy-start | bytes 19204
  1.6 9.2 %collective-permute-start.1 = (bf16[3,100,1,128]{3,1,2,0:T(8,128)(2,1)S(1)}, bf16[3,100,1,128]{3,1,2,0:T(8,128)(2,1)S(1)}, u32[]{:S(2)}, u32[]{:S(2)}) collective-permute-start(bf16[3,100,1,128]{3,1,2,0:T(8,128)(2,1)S(1)} %broadcast_in_dim.30), channel_id=1, source_target_pairs={{1,0},{2,1},{3,2},{4,3},{5,4},{6,5},{7,6},{8,7},{9,8},{10,9},{11,1... | collective-permute-start | bytes 230408 | tf_op jit(solution)/shard_map/ppermute | solution.py:19
  6.3 10.2 %collective-permute-start = (bf16[3,100,1,128]{3,1,2,0:T(8,128)(2,1)S(1)}, bf16[3,100,1,128]{3,1,2,0:T(8,128)(2,1)S(1)}, u32[]{:S(2)}, u32[]{:S(2)}) collective-permute-start(bf16[3,100,1,128]{3,1,2,0:T(8,128)(2,1)S(1)} %broadcast_in_dim.28), channel_id=1, source_target_pairs={{0,1},{1,2},{2,3},{3,4},{4,5},{5,6},{6,7},{7,8},{8,9},{9,10},{10,1... | collective-permute-start | bytes 230408 | tf_op jit(solution)/shard_map/ppermute | solution.py:17
  9.0 10.5 %copy-start.10 = (s32[4,128]{1,0:T(4,128)S(1)}, s32[4,128]{1,0:T(4,128)}, u32[]{:S(2)}) copy-start(s32[4,128]{1,0:T(4,128)} %param.13) | copy-start | bytes 6148
  9.0 10.5 %copy-start.8 = (bf16[2,100,100]{2,0,1:T(2,128)(2,1)S(1)}, bf16[2,100,100]{2,0,1:T(2,128)(2,1)}, u32[]{:S(2)}) copy-start(bf16[2,100,100]{2,0,1:T(2,128)(2,1)} %param.17) | copy-start | bytes 120004
  16.8 9.0 %copy-start.11 = (bf16[100,100]{1,0:T(8,128)(2,1)S(1)}, bf16[100,100]{1,0:T(8,128)(2,1)}, u32[]{:S(2)}) copy-start(bf16[100,100]{1,0:T(8,128)(2,1)} %param.18) | copy-start | bytes 60004
  16.8 2.8 collective-permute-start.2
  18.1 7.1 %collective-permute-start.3 = (bf16[3,100,6,1]{3,1,2,0:T(8,128)(2,1)S(1)}, bf16[3,100,6,1]{3,1,2,0:T(8,128)(2,1)S(1)}, u32[]{:S(2)}, u32[]{:S(2)}) collective-permute-start(bf16[3,100,6,1]{3,1,2,0:T(8,128)(2,1)S(1)} %get-tuple-element.33), channel_id=1, source_target_pairs={{32,0},{64,32},{96,64},{33,1},{65,33},{97,65},{34,2},{66,34},{98,6... | collective-permute-start | bytes 10808 | tf_op jit(solution)/shard_map/ppermute | solution.py:19
  25.8 11.4 %copy-start.9 = (s32[256,1]{0,1:T(1,128)S(1)}, s32[256,1]{0,1:T(1,128)}, u32[]{:S(2)}) copy-start(s32[256,1]{0,1:T(1,128)} %param.19) | copy-start | bytes 3076
  27.4 10.2 %collective-permute-start.4 = (bf16[3,100,1,128]{3,1,2,0:T(8,128)(2,1)S(1)}, bf16[3,100,1,128]{3,1,2,0:T(8,128)(2,1)S(1)}, u32[]{:S(2)}, u32[]{:S(2)}) collective-permute-start(bf16[3,100,1,128]{3,1,2,0:T(8,128)(2,1)S(1)} %get-tuple-element.40), channel_id=1, source_target_pairs={{0,1},{1,2},{2,3},{3,4},{4,5},{5,6},{6,7},{7,8},{8,9},{9,10},{10,1... | collective-permute-start | bytes 230408 | tf_op jit(solution)/shard_map/ppermute | solution.py:17
  29.4 9.9 %collective-permute-start.5 = (bf16[3,100,1,128]{3,1,2,0:T(8,128)(2,1)S(1)}, bf16[3,100,1,128]{3,1,2,0:T(8,128)(2,1)S(1)}, u32[]{:S(2)}, u32[]{:S(2)}) collective-permute-start(bf16[3,100,1,128]{3,1,2,0:T(8,128)(2,1)S(1)} %get-tuple-element.41), channel_id=1, source_target_pairs={{1,0},{2,1},{3,2},{4,3},{5,4},{6,5},{7,6},{8,7},{9,8},{10,9},{11,1... | collective-permute-start | bytes 230408 | tf_op jit(solution)/shard_map/ppermute | solution.py:19
  39.5 35.1 %collective-permute-start.6 = (bf16[3,100,6,1]{3,1,2,0:T(8,128)(2,1)S(1)}, bf16[3,100,6,1]{3,1,2,0:T(8,128)(2,1)S(1)}, u32[]{:S(2)}, u32[]{:S(2)}) collective-permute-start(bf16[3,100,6,1]{3,1,2,0:T(8,128)(2,1)S(1)} %get-tuple-element.30), channel_id=1, source_target_pairs={{0,32},{32,64},{64,96},{1,33},{33,65},{65,97},{2,34},{34,66},{66,9... | collective-permute-start | bytes 10808 | tf_op jit(solution)/shard_map/ppermute | solution.py:17
  52.8 21.8 %collective-permute-start.7 = (bf16[3,100,6,1]{3,1,2,0:T(8,128)(2,1)S(1)}, bf16[3,100,6,1]{3,1,2,0:T(8,128)(2,1)S(1)}, u32[]{:S(2)}, u32[]{:S(2)}) collective-permute-start(bf16[3,100,6,1]{3,1,2,0:T(8,128)(2,1)S(1)} %get-tuple-element.31), channel_id=1, source_target_pairs={{32,0},{64,32},{96,64},{33,1},{65,33},{97,65},{34,2},{66,34},{98,6... | collective-permute-start | bytes 10808 | tf_op jit(solution)/shard_map/ppermute | solution.py:19
  56.4 57.0 %all-to-all-start.1 = ((s32[128,1,4]{2,1,0:T(1,128)}), s32[128,1,4]{2,1,0:T(1,128)S(1)}, u32[]{:S(2)}, u32[]{:S(2)}) async-start(s32[128,1,4]{2,1,0:T(1,128)} %bitcast.22), calls=%async_computation.1 | async-start | bytes 131072 | tf_op jit(solution)/shard_map/all_to_all | solution.py:97
  75.1 11.4 %copy-start.5 = (f32[256,100]{0,1:T(8,128)S(1)}, f32[256,100]{0,1:T(8,128)}, u32[]{:S(2)}) copy-start(f32[256,100]{0,1:T(8,128)} %param.23) | copy-start | bytes 307204
  75.1 11.4 %copy-start.6 = (f32[256,100]{0,1:T(8,128)S(1)}, f32[256,100]{0,1:T(8,128)}, u32[]{:S(2)}) copy-start(f32[256,100]{0,1:T(8,128)} %param.22) | copy-start | bytes 307204
  75.1 11.4 %copy-start.7 = (f32[256,100]{0,1:T(8,128)S(1)}, f32[256,100]{0,1:T(8,128)}, u32[]{:S(2)}) copy-start(f32[256,100]{0,1:T(8,128)} %param.21) | copy-start | bytes 307204
  76.8 10.5 %collective-permute-start.8 = (bf16[3,100,1,128]{3,1,2,0:T(8,128)(2,1)S(1)}, bf16[3,100,1,128]{3,1,2,0:T(8,128)(2,1)S(1)}, u32[]{:S(2)}, u32[]{:S(2)}) collective-permute-start(bf16[3,100,1,128]{3,1,2,0:T(8,128)(2,1)S(1)} %get-tuple-element.38), channel_id=1, source_target_pairs={{0,1},{1,2},{2,3},{3,4},{4,5},{5,6},{6,7},{7,8},{8,9},{9,10},{10,1... | collective-permute-start | bytes 230408 | tf_op jit(solution)/shard_map/ppermute | solution.py:17
  80.2 8.4 %collective-permute-start.9 = (bf16[3,100,1,128]{3,1,2,0:T(8,128)(2,1)S(1)}, bf16[3,100,1,128]{3,1,2,0:T(8,128)(2,1)S(1)}, u32[]{:S(2)}, u32[]{:S(2)}) collective-permute-start(bf16[3,100,1,128]{3,1,2,0:T(8,128)(2,1)S(1)} %get-tuple-element.39), channel_id=1, source_target_pairs={{1,0},{2,1},{3,2},{4,3},{5,4},{6,5},{7,6},{8,7},{9,8},{10,9},{11,1... | collective-permute-start | bytes 230408 | tf_op jit(solution)/shard_map/ppermute | solution.py:19
  89.8 11.4 %collective-permute-start.10 = (bf16[3,100,6,1]{3,1,2,0:T(8,128)(2,1)}, bf16[3,100,6,1]{3,1,2,0:T(8,128)(2,1)S(1)}, u32[]{:S(2)}, u32[]{:S(2)}) collective-permute-start(bf16[3,100,6,1]{3,1,2,0:T(8,128)(2,1)} %get-tuple-element.28), channel_id=1, source_target_pairs={{0,32},{32,64},{64,96},{1,33},{33,65},{65,97},{2,34},{34,66},{66,9... | collective-permute-start | bytes 10808 | tf_op jit(solution)/shard_map/ppermute | solution.py:17
  91.1 10.1 %collective-permute-start.11 = (bf16[3,100,6,1]{3,1,2,0:T(8,128)(2,1)}, bf16[3,100,6,1]{3,1,2,0:T(8,128)(2,1)S(1)}, u32[]{:S(2)}, u32[]{:S(2)}) collective-permute-start(bf16[3,100,6,1]{3,1,2,0:T(8,128)(2,1)} %get-tuple-element.29), channel_id=1, source_target_pairs={{32,0},{64,32},{96,64},{33,1},{65,33},{97,65},{34,2},{66,34},{98,6... | collective-permute-start | bytes 10808 | tf_op jit(solution)/shard_map/ppermute | solution.py:19
  103.3 31.9 %collective-permute-start.12 = (bf16[3,100,1,128]{3,1,2,0:T(8,128)(2,1)S(1)}, bf16[3,100,1,128]{3,1,2,0:T(8,128)(2,1)S(1)}, u32[]{:S(2)}, u32[]{:S(2)}) collective-permute-start(bf16[3,100,1,128]{3,1,2,0:T(8,128)(2,1)S(1)} %get-tuple-element.36), channel_id=1, source_target_pairs={{0,1},{1,2},{2,3},{3,4},{4,5},{5,6},{6,7},{7,8},{8,9},{9,10},{10,1... | collective-permute-start | bytes 230408 | tf_op jit(solution)/shard_map/ppermute | solution.py:17
  105.2 30.0 %collective-permute-start.13 = (bf16[3,100,1,128]{3,1,2,0:T(8,128)(2,1)S(1)}, bf16[3,100,1,128]{3,1,2,0:T(8,128)(2,1)S(1)}, u32[]{:S(2)}, u32[]{:S(2)}) collective-permute-start(bf16[3,100,1,128]{3,1,2,0:T(8,128)(2,1)S(1)} %get-tuple-element.37), channel_id=1, source_target_pairs={{1,0},{2,1},{3,2},{4,3},{5,4},{6,5},{7,6},{8,7},{9,8},{10,9},{11,1... | collective-permute-start | bytes 230408 | tf_op jit(solution)/shard_map/ppermute | solution.py:19
  113.4 87.4 %all-to-all-start = ((f32[128,4,3,100]{3,1,2,0:T(4,128)}), f32[128,4,3,100]{3,1,2,0:T(4,128)S(1)}, u32[]{:S(2)}, u32[]{:S(2)}) async-start(f32[128,4,3,100]{3,1,2,0:T(4,128)} %copy.47), calls=%async_computation | async-start | bytes 1572864 | tf_op jit(solution)/shard_map/all_to_all | solution.py:98
  135.5 3.9 collective-permute-start.14
  137.8 8.9 %collective-permute-start.15 = (bf16[3,100,6,1]{3,1,2,0:T(8,128)(2,1)S(1)}, bf16[3,100,6,1]{3,1,2,0:T(8,128)(2,1)}, u32[]{:S(2)}, u32[]{:S(2)}) collective-permute-start(bf16[3,100,6,1]{3,1,2,0:T(8,128)(2,1)S(1)} %get-tuple-element.27), channel_id=1, source_target_pairs={{32,0},{64,32},{96,64},{33,1},{65,33},{97,65},{34,2},{66,34},{98,6... | collective-permute-start | bytes 10808 | tf_op jit(solution)/shard_map/ppermute | solution.py:19
  139.4 0.8 copy-start.4
  150.0 11.6 %collective-permute-start.16 = (bf16[3,100,1,128]{3,1,2,0:T(8,128)(2,1)S(1)}, bf16[3,100,1,128]{3,1,2,0:T(8,128)(2,1)S(1)}, u32[]{:S(2)}, u32[]{:S(2)}) collective-permute-start(bf16[3,100,1,128]{3,1,2,0:T(8,128)(2,1)S(1)} %get-tuple-element.34), channel_id=1, source_target_pairs={{0,1},{1,2},{2,3},{3,4},{4,5},{5,6},{6,7},{7,8},{8,9},{9,10},{10,1... | collective-permute-start | bytes 230408 | tf_op jit(solution)/shard_map/ppermute | solution.py:17
  152.5 9.4 %collective-permute-start.17 = (bf16[3,100,1,128]{3,1,2,0:T(8,128)(2,1)S(1)}, bf16[3,100,1,128]{3,1,2,0:T(8,128)(2,1)S(1)}, u32[]{:S(2)}, u32[]{:S(2)}) collective-permute-start(bf16[3,100,1,128]{3,1,2,0:T(8,128)(2,1)S(1)} %get-tuple-element.35), channel_id=1, source_target_pairs={{1,0},{2,1},{3,2},{4,3},{5,4},{6,5},{7,6},{8,7},{9,8},{10,9},{11,1... | collective-permute-start | bytes 230408 | tf_op jit(solution)/shard_map/ppermute | solution.py:19
  162.1 25.6 %collective-permute-start.18 = (bf16[3,100,6,1]{3,1,2,0:T(8,128)(2,1)S(1)}, bf16[3,100,6,1]{3,1,2,0:T(8,128)(2,1)S(1)}, u32[]{:S(2)}, u32[]{:S(2)}) collective-permute-start(bf16[3,100,6,1]{3,1,2,0:T(8,128)(2,1)S(1)} %get-tuple-element.24), channel_id=1, source_target_pairs={{0,32},{32,64},{64,96},{1,33},{33,65},{65,97},{2,34},{34,66},{66,9... | collective-permute-start | bytes 10808 | tf_op jit(solution)/shard_map/ppermute | solution.py:17
  186.0 4.2 collective-permute-start.19
  187.8 0.8 copy-start.3
  193.5 0.7 copy-start.1
  198.1 1.2 copy-start.2
  198.1 1.9 slice-start
  206.1 351.7 %all-to-all-start.2 = ((f32[128,4,100]{2,1,0:T(4,128)}), f32[128,4,100]{2,1,0:T(4,128)S(1)}, u32[]{:S(2)}, u32[]{:S(2)}) async-start(f32[128,4,100]{2,1,0:T(4,128)} %bitcast.35), calls=%async_computation.2 | async-start | bytes 524288 | tf_op jit(solution)/shard_map/all_to_all | solution.py:121
where the time goes:
time: 560 us; the launch traced here: 559 us
  blocking collectives  320 us (57%)
  starting transfers between devices  159 us (28%)
  local copies, waits for them, and re-layouts  25.4 us (5%)
  waiting for transfers between devices  25.4 us (5%)
  matrix products  15.2 us (3%)
  other arithmetic  13.8 us (2%)
    psum x1, blocking collectives, on_device(): gram_block, projection = lax.psum((gram_part, proj_part), ('lat', 'lon'))  305 us
    ppermute x10, starting transfers between devices, padded_2(): lax.ppermute(tail, axis, [(i, (i + 1) % count) for i in range(ends)])  53.6 us
    ppermute x10, starting transfers between devices, padded_2(): lax.ppermute(head, axis, [((i + 1) % count, i) for i in range(ends)])  41.1 us
    all_to_all x1, starting transfers between devices, on_device(): lax.all_to_all(owner_misfit, ('lat', 'lon'), split_axis=0, concat_axis=0,...  24.3 us
    all_to_all x1, starting transfers between devices, on_device(): lax.all_to_all(send_records, ('lat', 'lon'), split_axis=0, concat_axis=0,...  21.5 us
    all_to_all x1, starting transfers between devices, on_device(): lax.all_to_all(send_ids, ('lat', 'lon'), split_axis=0, concat_axis=0, til...  18.1 us
    ppermute x10, waiting for transfers between devices, padded_2(): lax.ppermute(head, axis, [((i + 1) % count, i) for i in range(ends)])  17.1 us
    all_gather x1, blocking collectives, on_device(): green_all = lax.all_gather(green_cols, 'mem', axis=0, tiled=True)  14.8 us
  transfers between devices with their start and end apart: 23, of which 10 were waited for; matrix products, arithmetic and copies ran while one was open for 7% of the time, Pallas kernels for 0%

commit v1 on v0

v1 whole, which is shorter than its diff:
```python
import functools

import jax
import jax.numpy as jnp
from jax import lax
from jax.experimental import pallas as pl
from jax.experimental.pallas import tpu as pltpu
from jax.sharding import PartitionSpec as P

STEPS = 5
K = 100
KP = 128
CX = 4
CY = 128
CAP = 4
OWN = 128
REC = 256
HALO = 8
ROWS = CY + 2 * HALO
COLS = CX * CY
MEMBERS = 8
PAIRS = [(a, b) for a in range(MEMBERS) for b in range(a, MEMBERS)]
F32 = jnp.float32
BF16 = jnp.bfloat16
NT = (((1,), (1,)), ((), ()))
NN = (((1,), (0,)), ((), ()))
TN = (((0,), (0,)), ((), ()))
SMEM = pltpu.SMEM
VMEM = pltpu.VMEM


def dot(a, b, dims):
    return lax.dot_general(a, b, dims, preferred_element_type=F32)


def ones_where(cond):
    return jnp.where(cond, 1.0, 0.0).astype(BF16)


def iota(shape, dim):
    return lax.broadcasted_iota(jnp.int32, shape, dim)


def slots_kernel(m_ref, owner_ref, column_ref, w_ref, iv_ref, ob_ref, out_ref, code_ref, pad):
    owner = owner_ref[...]
    column = column_ref[...]
    hit = iota((OWN, REC), 0) == owner
    before = ones_where(iota((REC, REC), 0) < iota((REC, REC), 1))
    earlier = dot(ones_where(hit), before, NN)
    rank = jnp.sum(jnp.where(hit, earlier, 0.0), 0, keepdims=True).astype(jnp.int32)
    code_ref[...] = rank * OWN + owner
    slot = owner * CAP + rank
    mine = jnp.where(rank == m_ref[0], owner * CAP, -CAP)
    rows = iota((OWN * CAP, REC), 0)
    sub = iota((KP, REC), 0)
    high = (column // CY + 1).astype(F32)
    low = (column % CY).astype(F32)
    ids = jnp.where(sub == K, high, jnp.where(sub == K + 1, low, 0.0)).astype(BF16)
    placed = dot(ones_where(rows == slot), ids, NT)
    pad[...] = jnp.zeros((KP, REC), F32)
    for group, ref in enumerate((w_ref, iv_ref, ob_ref)):
        pad[0:K, :] = ref[...]
        placed += dot(ones_where(rows == mine + group), pad[...].astype(BF16), NT)
    out_ref[...] = placed.astype(BF16)


def window_kernel(
    m_ref, index_ref, own_ref, left_ref, right_ref, left2_ref, right2_ref, recv_ref,
    table_ref, base_kh_ref, mix_ref, base_mix_ref,
    fields_ref, picks_ref, base_ref,
    start, ping, pong, ocean, kh_pad, mix_pad, base_pad, slots,
):
    body = pl.ds(8, ROWS)

    def fill(column, cells):
        cells = cells.astype(F32)
        start[column, body, :] = cells
        ocean[column] = jnp.broadcast_to(cells[:, K : K + 1], (ROWS, KP))

    start[0, pl.ds(16, CY), :] = left2_ref[0].astype(F32)
    start[13, pl.ds(16, CY), :] = right2_ref[0].astype(F32)
    for first, ref in ((1, left_ref), (5, own_ref), (9, right_ref)):
        for c in range(CX):
            fill(first + c, ref[c])
    kh_pad[...] = jnp.zeros((8, KP), F32)
    kh_pad[0:1, 0:K] = table_ref[pl.ds(index_ref[0], 1), :]
    kh_pad[1:2, 0:K] = table_ref[pl.ds(index_ref[1], 1), :]
    kh_pad[2:3, 0:K] = base_kh_ref[...]
    mix_pad[...] = jnp.zeros((2 * KP, 2 * KP), BF16)
    mix_pad[0:K, 0:K] = mix_ref[0]
    mix_pad[KP : KP + K, KP : KP + K] = mix_ref[1]
    base_pad[...] = jnp.zeros((KP, KP), BF16)
    base_pad[0:K, 0:K] = base_mix_ref[...]

    for step in range(STEPS):
        source, target = ((ping, pong), (pong, ping))[step % 2]
        row0, count = (8, ROWS) if step < STEPS - 1 else (16, CY)

        def advance(column, _, step=step, source=source, target=target, row0=row0, count=count):
            def at(run, lon, row):
                if step == 0:
                    return start[lon, pl.ds(row, count), :]
                return source[run, lon, pl.ds(row, count), :]

            def around(run):
                return (at(run, column + 1, row0) + at(run, column - 1, row0)) + (
                    at(run, column, row0 + 1) + at(run, column, row0 - 1)
                )

            values, rights = [], []
            shared = (at(0, column, row0), around(0)) if step == 0 else None
            for run in range(3):
                value, near = shared if step == 0 else (at(run, column, row0), around(run))
                kh = kh_pad[run : run + 1, :]
                values.append(value)
                rights.append((value * (1.0 - 4.0 * kh) + near * kh).astype(BF16))
            both = dot(jnp.concatenate(rights[:2], 1), mix_pad[...], NT)
            mixed = (both[:, :KP], both[:, KP:], dot(rights[2], base_pad[...], NT))
            open_ = ocean[column, pl.ds(row0 - 8, count), :] > 0.0
            for run in range(3):
                vertical = rights[run].astype(F32) + mixed[run]
                new = jnp.where(open_, vertical, values[run])
                target[run, column, pl.ds(row0, count), :] = new.astype(BF16).astype(F32)
            return 0

        lax.fori_loop(step + 1, 13 - step, advance, 0)

    final = pong
    flat = []
    for run in range(3):
        parts = []
        for c in range(CX):
            cells = final[run, 5 + c, pl.ds(16, CY), :]
            fields_ref[run, c] = cells.T[0:K, :].astype(BF16)
            parts.append(cells.astype(BF16))
        flat.append(jnp.concatenate(parts, 0))
    both = jnp.concatenate(flat[:2], 1)

    slots[...] = recv_ref[...].astype(F32)
    cols = iota((OWN, COLS), 1)

    def chooser(ids):
        at = ((ids[:, K : K + 1] - 1.0) * CY + ids[:, K + 1 : K + 2]).astype(jnp.int32)
        return ones_where(at == cols)

    base_all = flat[2]
    own = jnp.zeros((OWN, KP), F32)
    for rank in range(CAP):
        pick = chooser(slots[pl.ds(rank, OWN, stride=CAP), :])
        picks_ref[rank] = dot(pick, both, NN).astype(BF16)
        own = jnp.where(m_ref[0] == rank, dot(pick, base_all, NN), own)
    base_ref[...] = own.astype(BF16)


def gram_kernel(m_ref, recv_ref, base_ref, slot_ref, out_ref, slots, greens, weighted, sums, rows2, *, scale):
    lane = iota((OWN, KP), 1)

    def deeper(x):
        return jnp.where(lane == K - 1, x, pltpu.roll(x, KP - 1, 1))

    slots[...] = slot_ref[...].astype(F32)
    weight = slots[pl.ds(0, OWN, stride=CAP), :]
    inv_var = jnp.where(lane < K, slots[pl.ds(1, OWN, stride=CAP), :], 0.0)
    measured = slots[pl.ds(2, OWN, stride=CAP), :]
    base = base_ref[...].astype(F32)

    def model(x):
        return weight * x + (1.0 - weight) * deeper(x)

    base_model = model(base)
    misfit = measured - base_model
    for member in range(MEMBERS):
        half = (member % 2) * KP
        picked = recv_ref[member // 2, :, half : half + KP].astype(F32)
        green = jnp.where(lane < K, model(picked) - base_model, 0.0).astype(BF16).astype(F32)
        greens[member] = green
        weighted[member] = green * inv_var
    sums[...] = jnp.zeros((KP, KP), F32)
    for i, (a, b) in enumerate(PAIRS):
        sums[i : i + 1, :] = jnp.sum(weighted[a] * greens[b], 0, keepdims=True)
    for a in range(MEMBERS):
        sums[len(PAIRS) + a : len(PAIRS) + a + 1, :] = jnp.sum(weighted[a] * misfit, 0, keepdims=True)
    total = jnp.sum(sums[...].T, 0, keepdims=True) * scale
    high = total.astype(BF16).astype(F32)
    rest = total - high
    line = iota((1, KP), 1)
    both = jnp.where(line < 64, high, pltpu.roll(jnp.broadcast_to(rest, (8, KP)), 64, 1)[0:1])
    rows2[pl.ds(0, OWN, stride=2), :] = base
    rows2[pl.ds(1, OWN, stride=2), :] = jnp.broadcast_to(both, (OWN, KP))
    packed = rows2[...].astype(BF16)
    for copy in range(4):
        out_ref[copy] = packed


def result_kernel(recv_ref, code_ref, w_ref, ob_ref, misfit_ref, gram_ref, proj_ref):
    recv = recv_ref[...]
    count = recv.shape[0]
    pick = ones_where(iota((count, REC), 0) == 2 * code_ref[...])
    picked = dot(recv, pick, TN)
    values = picked[0:K]
    deeper = jnp.concatenate([picked[1:K], picked[K - 1 : K]], 0)
    weight = w_ref[...]
    misfit_ref[...] = ob_ref[...] - (weight * values + (1.0 - weight) * deeper)
    odd = iota((8, KP), 0) % 2 == 1
    part = jnp.sum(recv.astype(F32).reshape(count // 8, 8, KP), 0)
    total = jnp.sum(jnp.where(odd, part, 0.0), 0, keepdims=True)
    total = jnp.broadcast_to(total, (8, KP))
    total = total + pltpu.roll(total, 64, 1)
    sub, line = iota((8, KP), 0), iota((8, KP), 1)
    gram = jnp.zeros((8, KP), F32)
    for i, (a, b) in enumerate(PAIRS):
        here = ((sub == a) & (line == b)) | ((sub == b) & (line == a))
        gram = jnp.where(here, total[:, i : i + 1], gram)
    gram_ref[...] = gram[:, 0:MEMBERS]
    proj_ref[...] = pltpu.roll(total, KP - len(PAIRS), 1)[0:1, 0:MEMBERS]


def vmem(count):
    return [pl.BlockSpec(memory_space=VMEM)] * count


def smem(count):
    return [pl.BlockSpec(memory_space=SMEM)] * count


def on_device(
    initial_temp, land_mask, pert_table, pert_index, base_kh, member_mix, base_mix,
    owner, column, interp_w, obs_inv_var, observed,
):
    owners = ("lat", "lon")
    mem = lax.axis_index("mem").astype(jnp.int32).reshape(1)
    lat_at, lat_count = lax.axis_index("lat"), lax.axis_size("lat")
    lon_count = lax.axis_size("lon")
    w_t, iv_t, ob_t = interp_w.T, obs_inv_var.T, observed.T

    send, code = pl.pallas_call(
        slots_kernel,
        out_shape=(
            jax.ShapeDtypeStruct((OWN * CAP, KP), BF16),
            jax.ShapeDtypeStruct((1, REC), jnp.int32),
        ),
        in_specs=smem(1) + vmem(5),
        out_specs=tuple(vmem(2)),
        scratch_shapes=[VMEM((KP, REC), F32)],
        name="slots",
    )(mem, owner.reshape(1, REC), column.reshape(1, REC), w_t, iv_t, ob_t)

    cells = jnp.transpose(initial_temp, (1, 2, 0)).astype(BF16)
    cells = jnp.concatenate(
        [
            cells,
            land_mask.astype(BF16)[:, :, None],
            jnp.zeros((CX, CY, KP - K - 1), BF16),
        ],
        2,
    )
    up = [(i, i + 1) for i in range(lat_count - 1)]
    down = [(i + 1, i) for i in range(lat_count - 1)]
    below = lax.ppermute(cells[:, CY - HALO :], "lat", up)
    above = lax.ppermute(cells[:, :HALO], "lat", down)
    below = jnp.where(lat_at == 0, cells[:, :HALO][:, ::-1], below)
    above = jnp.where(lat_at == lat_count - 1, cells[:, CY - HALO :][:, ::-1], above)
    tall = jnp.concatenate([below, cells, above], 1)

    def shift(x, by):
        return lax.ppermute(x, "lon", [(i, (i + by) % lon_count) for i in range(lon_count)])

    left2, right2 = shift(cells[CX - 1 :], 2), shift(cells[:1], -2)
    left, right = shift(tall, 1), shift(tall, -1)
    recv = lax.all_to_all(
        send.reshape(OWN, CAP, KP), owners, split_axis=0, concat_axis=0, tiled=True
    ).reshape(OWN * CAP, KP)

    fields, picks, base_rows = pl.pallas_call(
        window_kernel,
        out_shape=(
            jax.ShapeDtypeStruct((3, CX, K, CY), BF16),
            jax.ShapeDtypeStruct((CAP, OWN, 2 * KP), BF16),
            jax.ShapeDtypeStruct((OWN, KP), BF16),
        ),
        in_specs=smem(2) + vmem(10),
        out_specs=tuple(vmem(3)),
        scratch_shapes=[
            VMEM((14, ROWS + 16, KP), F32),
            VMEM((3, 14, ROWS + 16, KP), F32),
            VMEM((3, 14, ROWS + 16, KP), F32),
            VMEM((14, ROWS, KP), F32),
            VMEM((8, KP), F32),
            VMEM((2 * KP, 2 * KP), BF16),
            VMEM((KP, KP), BF16),
            VMEM((OWN * CAP, KP), F32),
        ],
        name="window",
    )(
        mem, pert_index, tall, left, right, left2, right2, recv,
        pert_table, base_kh.reshape(1, K), member_mix, base_mix,
    )

    members = lax.all_to_all(picks, "mem", split_axis=0, concat_axis=0, tiled=True)
    back = pl.pallas_call(
        functools.partial(gram_kernel, scale=1.0 / (OWN * REC * K)),
        out_shape=jax.ShapeDtypeStruct((4, 2 * OWN, KP), BF16),
        in_specs=smem(1) + vmem(3),
        out_specs=vmem(1)[0],
        scratch_shapes=[
            VMEM((OWN * CAP, KP), F32),
            VMEM((MEMBERS, OWN, KP), F32),
            VMEM((MEMBERS, OWN, KP), F32),
            VMEM((KP, KP), F32),
            VMEM((2 * OWN, KP), F32),
        ],
        name="gram",
    )(mem, members, base_rows, recv)

    returned = lax.all_to_all(
        back.reshape(4 * OWN, 2, KP), ("mem", "lat", "lon"), split_axis=0, concat_axis=0, tiled=True
    ).reshape(8 * OWN, KP)
    misfit_t, gram, proj = pl.pallas_call(
        result_kernel,
        out_shape=(
            jax.ShapeDtypeStruct((K, REC), F32),
            jax.ShapeDtypeStruct((MEMBERS, MEMBERS), F32),
            jax.ShapeDtypeStruct((1, MEMBERS), F32),
        ),
        in_specs=vmem(4),
        out_specs=tuple(vmem(3)),
        name="result",
    )(returned, code, w_t, ob_t)

    fields = jnp.transpose(fields, (0, 2, 1, 3))
    return fields[:2], fields[2], gram, proj.reshape(MEMBERS), misfit_t.T


def solution(mesh):
    placed = (
        P(None, "lon", "lat"),
        P("lon", "lat"),
        P(),
        P("mem"),
        P(),
        P("mem", None, None),
        P(),
        P(("lat", "lon"), None),
        P(("lat", "lon")),
        P(("lat", "lon"), None),
        P(("lat", "lon"), None),
        P(("lat", "lon"), None),
    )
    return jax.shard_map(
        on_device,
        mesh=mesh,
        in_specs=placed,
        out_specs=(
            P("mem", None, "lon", "lat"),
            P(None, "lon", "lat"),
            P(),
            P(),
            P(("lat", "lon"), None),
        ),
        check_vma=False,
    )
```

time: 560 us -> 114 us (0.20)
  the two profiles are of different devices: /device:TPU:258 before, /device:TPU:1 now
where the time goes in v1:
time: 114 us; the launch traced here: 113 us
  starting transfers between devices  57.7 us (51%)
  waiting for transfers between devices  20.3 us (18%)
  Pallas kernels  18.5 us (16%)
  blocking collectives  9.65 us (8%)
  local copies, waits for them, and re-layouts  3.92 us (3%)
  other arithmetic  2.01 us (2%)
    all_to_all x1, starting transfers between devices, on_device(): lax.all_to_all(back.reshape(4 * OWN, 2, KP), ('mem', 'lat', 'lon'), split...  16.8 us
    all_to_all x1, waiting for transfers between devices, on_device(): lax.all_to_all(back.reshape(4 * OWN, 2, KP), ('mem', 'lat', 'lon'), split...  16.2 us
    ppermute x4, starting transfers between devices, shift(): lax.ppermute(x, 'lon', [(i, (i + by) % lon_count) for i in range(lon_coun...  15.6 us
    all_to_all x1, starting transfers between devices, on_device(): lax.all_to_all(send.reshape(OWN, CAP, KP), owners, split_axis=0, concat_a...  14.4 us
    pallas_call x1, Pallas kernels, on_device(): pl.pallas_call(window_kernel, out_shape=(jax.ShapeDtypeStruct((3, CX, K,...  11.8 us
    all_to_all x1, blocking collectives, on_device(): lax.all_to_all(picks, 'mem', split_axis=0, concat_axis=0, tiled=True)  9.65 us
    ppermute x1, starting transfers between devices, on_device(): above = lax.ppermute(cells[:, :HALO], 'lat', down)  8.75 us
    ppermute x4, waiting for transfers between devices, shift(): lax.ppermute(x, 'lon', [(i, (i + by) % lon_count) for i in range(lon_coun...  4.16 us
  transfers between devices with their start and end apart: 8, of which 3 were waited for; matrix products, arithmetic and copies ran while one was open for 2% of the time, Pallas kernels for 2%

profile of v1, /device:TPU:1, one launch (start us, length us, event | category | flops | bytes accessed | tf_op | source)
XLA Modules:
  0.0 113.0 jit_solution(4948256464106342853)
XLA Ops:
  0.6 0.7 convert_bitcast_fusion
  1.3 1.0 convert_element_type.9
  2.3 0.2 copy.26
  2.4 0.2 copy.27
  2.7 0.1 pad_maximum_fusion.5
  2.7 8.7 %collective-permute-start.1 = (bf16[4,8,128]{2,1,0:T(8,128)(2,1)S(1)}, bf16[4,8,128]{2,1,0:T(8,128)(2,1)S(1)}, u32[]{:S(2)}, u32[]{:S(2)}) collective-permute-start(bf16[4,8,128]{2,1,0:T(8,128)(2,1)S(1)} %get-tuple-element.38), channel_id=1, source_target_pairs={{32,0},{64,32},{96,64},{33,1},{65,33},{97,65},{34,2},{66,34},{98,6... | collective-permute-start | bytes 24584 | tf_op jit(solution)/shard_map/ppermute | solution.py:260
  11.5 2.0 %collective-permute-start = (bf16[4,8,128]{2,1,0:T(8,128)(2,1)S(1)}, bf16[4,8,128]{2,1,0:T(8,128)(2,1)S(1)}, u32[]{:S(2)}, u32[]{:S(2)}) collective-permute-start(bf16[4,8,128]{2,1,0:T(8,128)(2,1)S(1)} %get-tuple-element.39), channel_id=1, source_target_pairs={{0,32},{32,64},{64,96},{1,33},{33,65},{65,97},{2,34},{34,66},{66,9... | collective-permute-start | bytes 24584 | tf_op jit(solution)/shard_map/ppermute | solution.py:259
  13.5 2.3 %slots.1 = (bf16[512,128]{1,0:T(8,128)(2,1)}, s32[1,256]{1,0:T(1,128)}) custom-call(s32[1]{0:T(128)} %bitcast.m_ref, s32[1,256]{1,0:T(1,128)} %bitcast.34, s32[1,256]{1,0:T(1,128)} %bitcast.35, f32[100,256]{1,0:T(8,128)} %bitcast.26, f32[100,256]{1,0:T(8,128)} %bitcast.33, f32[100,256]{1,0:T(8,128)} %bitcast.28), custom_call_target="tpu_custom_call" | custom-call | tf_op jit(solution)/shard_map/slots/pallas_call | solution.py:236
  15.8 14.4 %all-to-all-start = ((bf16[128,4,128]{2,1,0:T(4,128)(2,1)}), bf16[128,4,128]{2,1,0:T(4,128)(2,1)S(1)}, u32[]{:S(2)}, u32[]{:S(2)}) async-start(bf16[128,4,128]{2,1,0:T(4,128)(2,1)} %bitcast.32), calls=%async_computation | async-start | bytes 262144 | tf_op jit(solution)/shard_map/all_to_all | solution.py:270
  30.3 0.0 collective-permute-done.1
  30.3 0.0 collective-permute-done
  30.4 0.1 pad_maximum_fusion.own_ref
  30.5 0.0 copy-start.2
  30.5 0.0 copy-start.6
  30.5 7.5 %collective-permute-start.3 = (bf16[4,144,128]{2,1,0:T(8,128)(2,1)S(1)}, bf16[4,144,128]{2,1,0:T(8,128)(2,1)S(1)}, u32[]{:S(2)}, u32[]{:S(2)}) collective-permute-start(bf16[4,144,128]{2,1,0:T(8,128)(2,1)S(1)} %pad_maximum_fusion.own_ref), channel_id=1, source_target_pairs={{0,31},{1,0},{2,1},{3,2},{4,3},{5,4},{6,5},{7,6},{8,7},{9,8},{10,9... | collective-permute-start | bytes 442376 | tf_op jit(solution)/shard_map/ppermute | solution.py:266
  38.1 1.9 %collective-permute-start.2 = (bf16[4,144,128]{2,1,0:T(8,128)(2,1)S(1)}, bf16[4,144,128]{2,1,0:T(8,128)(2,1)S(1)}, u32[]{:S(2)}, u32[]{:S(2)}) collective-permute-start(bf16[4,144,128]{2,1,0:T(8,128)(2,1)S(1)} %pad_maximum_fusion.own_ref), channel_id=1, source_target_pairs={{0,1},{1,2},{2,3},{3,4},{4,5},{5,6},{6,7},{7,8},{8,9},{9,10},{10,1... | collective-permute-start | bytes 442376 | tf_op jit(solution)/shard_map/ppermute | solution.py:266
  40.0 0.1 pad_maximum_fusion.1
  40.1 0.0 copy-done.2
  40.1 2.5 %collective-permute-start.5 = (bf16[1,128,128]{2,1,0:T(8,128)(2,1)S(1)}, bf16[1,128,128]{2,1,0:T(8,128)(2,1)S(1)}, u32[]{:S(2)}, u32[]{:S(2)}) collective-permute-start(bf16[1,128,128]{2,1,0:T(8,128)(2,1)S(1)} %get-tuple-element.36), channel_id=1, source_target_pairs={{0,30},{1,31},{2,0},{3,1},{4,2},{5,3},{6,4},{7,5},{8,6},{9,7},{10,... | collective-permute-start | bytes 98312 | tf_op jit(solution)/shard_map/ppermute | solution.py:266
  42.6 3.7 %collective-permute-start.4 = (bf16[1,128,128]{2,1,0:T(8,128)(2,1)S(1)}, bf16[1,128,128]{2,1,0:T(8,128)(2,1)S(1)}, u32[]{:S(2)}, u32[]{:S(2)}) collective-permute-start(bf16[1,128,128]{2,1,0:T(8,128)(2,1)S(1)} %get-tuple-element.37), channel_id=1, source_target_pairs={{0,2},{1,3},{2,4},{3,5},{4,6},{5,7},{6,8},{7,9},{8,10},{9,11},{10,... | collective-permute-start | bytes 98312 | tf_op jit(solution)/shard_map/ppermute | solution.py:266
  46.3 0.0 copy-done.6
  46.3 0.6 copy.28.mix_ref
  47.0 0.6 collective-permute-done.5.right2_ref
  47.5 0.0 copy-start.7
  47.5 3.6 %collective-permute-done.4.left2_ref = bf16[1,128,128]{2,1,0:T(8,128)(2,1)S(1)} collective-permute-done((bf16[1,128,128]{2,1,0:T(8,128)(2,1)S(1)}, bf16[1,128,128]{2,1,0:T(8,128)(2,1)S(1)}, u32[]{:S(2)}, u32[]{:S(2)}) %collective-permute-start.4) | collective-permute-done | bytes 32800 | tf_op jit(solution)/shard_map/ppermute | solution.py:266
  51.1 0.0 copy-start.8
  51.1 0.0 collective-permute-done.3.right_ref
  51.1 0.0 collective-permute-done.2.left_ref
  51.1 0.0 copy-start.5
  51.1 0.0 all-to-all-done
  51.1 0.0 copy-start
  51.2 0.0 copy-done.7
  51.2 0.6 copy-done.8
  51.7 0.0 copy-done.4
  51.8 0.1 copy-done.5
  51.8 0.0 copy-done
  51.9 11.8 %window.1 = (bf16[3,4,100,128]{3,2,1,0:T(8,128)(2,1)}, bf16[4,128,256]{2,1,0:T(8,128)(2,1)}, bf16[128,128]{1,0:T(8,128)(2,1)}) custom-call(s32[1]{0:T(128)} %bitcast.m_ref, s32[2]{0:T(128)} %index_ref.1, bf16[4,144,128]{2,1,0:T(8,128)(2,1)} %copy-done.2, bf16[4,144,128]{2,1,0:T(8,128)(2,1)} %copy-done.5, bf16[4,144,128]{2,1,0:T(8,128)(2,1)} %copy-done.4, ...), custom_call_target="tpu_custom_call" | custom-call | tf_op jit(solution)/shard_map/window/pallas_call | solution.py:274
  63.7 9.6 %all_to_all.15.recv_ref = bf16[4,128,256]{2,1,0:T(8,128)(2,1)} all-to-all(bf16[4,128,256]{2,1,0:T(8,128)(2,1)} %get-tuple-element.15), channel_id=1, replica_groups=mesh['mem'=4,'lat'=4,'lon'=32] {'mem'}, dimensions={0} | all-to-all | bytes 524288 | tf_op jit(solution)/shard_map/all_to_all | solution.py:299
  73.3 2.4 %gram.1 = bf16[4,256,128]{2,1,0:T(8,128)(2,1)} custom-call(s32[1]{0:T(128)} %bitcast.m_ref, bf16[4,128,256]{2,1,0:T(8,128)(2,1)} %all_to_all.15.recv_ref, bf16[128,128]{1,0:T(8,128)(2,1)} %get-tuple-element.16.base_ref, bf16[512,128]{1,0:T(8,128)(2,1)} %bitcast.23), custom_call_target="tpu_custom_call" | custom-call | tf_op jit(solution)/shard_map/gram/pallas_call | solution.py:300
  75.7 0.0 copy-start.3
  75.7 16.8 %all-to-all-start.2 = ((bf16[512,2,128]{2,1,0:T(2,128)(2,1)}), bf16[512,2,128]{2,1,0:T(2,128)(2,1)S(1)}, u32[]{:S(2)}, u32[]{:S(2)}) async-start(bf16[512,2,128]{2,1,0:T(2,128)(2,1)} %bitcast.25), calls=%async_computation.2 | async-start | bytes 524288 | tf_op jit(solution)/shard_map/all_to_all | solution.py:315
  92.6 0.0 copy-done.3
  92.6 0.8 copy.29
  93.4 0.7 copy.30
  94.0 16.2 %all-to-all-done.2 = bf16[512,2,128]{2,1,0:T(2,128)(2,1)S(1)} async-done(((bf16[512,2,128]{2,1,0:T(2,128)(2,1)}), bf16[512,2,128]{2,1,0:T(2,128)(2,1)S(1)}, u32[]{:S(2)}, u32[]{:S(2)}) %all-to-all-start.2) | async-done | bytes 262176 | tf_op jit(solution)/shard_map/all_to_all | solution.py:315
  110.2 0.0 copy-start.1
  110.2 0.7 copy-done.1
  110.9 2.0 %result.1 = (f32[100,256]{1,0:T(8,128)}, f32[8,8]{1,0:T(8,128)}, f32[1,8]{1,0:T(1,128)}) custom-call(bf16[1024,128]{1,0:T(8,128)(2,1)} %bitcast.24, s32[1,256]{1,0:T(1,128)} %get-tuple-element.17.code_ref, f32[100,256]{1,0:T(8,128)} %bitcast.27, f32[100,256]{1,0:T(8,128)} %bitcast.29), custom_call_target="tpu_custom_call" | custom-call | tf_op jit(solution)/shard_map/result/pallas_call | solution.py:318
  (8 shorter events, 0.1 us)
Async XLA Ops:
  2.7 27.6 %collective-permute-start.1 = (bf16[4,8,128]{2,1,0:T(8,128)(2,1)S(1)}, bf16[4,8,128]{2,1,0:T(8,128)(2,1)S(1)}, u32[]{:S(2)}, u32[]{:S(2)}) collective-permute-start(bf16[4,8,128]{2,1,0:T(8,128)(2,1)S(1)} %get-tuple-element.38), channel_id=1, source_target_pairs={{32,0},{64,32},{96,64},{33,1},{65,33},{97,65},{34,2},{66,34},{98,6... | collective-permute-start | bytes 24584 | tf_op jit(solution)/shard_map/ppermute | solution.py:260
  11.5 18.9 %collective-permute-start = (bf16[4,8,128]{2,1,0:T(8,128)(2,1)S(1)}, bf16[4,8,128]{2,1,0:T(8,128)(2,1)S(1)}, u32[]{:S(2)}, u32[]{:S(2)}) collective-permute-start(bf16[4,8,128]{2,1,0:T(8,128)(2,1)S(1)} %get-tuple-element.39), channel_id=1, source_target_pairs={{0,32},{32,64},{64,96},{1,33},{33,65},{65,97},{2,34},{34,66},{66,9... | collective-permute-start | bytes 24584 | tf_op jit(solution)/shard_map/ppermute | solution.py:259
  15.8 35.3 %all-to-all-start = ((bf16[128,4,128]{2,1,0:T(4,128)(2,1)}), bf16[128,4,128]{2,1,0:T(4,128)(2,1)S(1)}, u32[]{:S(2)}, u32[]{:S(2)}) async-start(bf16[128,4,128]{2,1,0:T(4,128)(2,1)} %bitcast.32), calls=%async_computation | async-start | bytes 262144 | tf_op jit(solution)/shard_map/all_to_all | solution.py:270
  30.5 9.6 %copy-start.2 = (bf16[4,144,128]{2,1,0:T(8,128)(2,1)}, bf16[4,144,128]{2,1,0:T(8,128)(2,1)S(1)}, u32[]{:S(2)}) copy-start(bf16[4,144,128]{2,1,0:T(8,128)(2,1)S(1)} %pad_maximum_fusion.own_ref) | copy-start | bytes 442372
  30.5 15.8 %copy-start.6 = (bf16[2,100,100]{2,0,1:T(2,128)(2,1)S(1)}, bf16[2,100,100]{2,0,1:T(2,128)(2,1)}, u32[]{:S(2)}) copy-start(bf16[2,100,100]{2,0,1:T(2,128)(2,1)} %param.17) | copy-start | bytes 120004
  30.5 20.6 %collective-permute-start.3 = (bf16[4,144,128]{2,1,0:T(8,128)(2,1)S(1)}, bf16[4,144,128]{2,1,0:T(8,128)(2,1)S(1)}, u32[]{:S(2)}, u32[]{:S(2)}) collective-permute-start(bf16[4,144,128]{2,1,0:T(8,128)(2,1)S(1)} %pad_maximum_fusion.own_ref), channel_id=1, source_target_pairs={{0,31},{1,0},{2,1},{3,2},{4,3},{5,4},{6,5},{7,6},{8,7},{9,8},{10,9... | collective-permute-start | bytes 442376 | tf_op jit(solution)/shard_map/ppermute | solution.py:266
  38.1 13.1 %collective-permute-start.2 = (bf16[4,144,128]{2,1,0:T(8,128)(2,1)S(1)}, bf16[4,144,128]{2,1,0:T(8,128)(2,1)S(1)}, u32[]{:S(2)}, u32[]{:S(2)}) collective-permute-start(bf16[4,144,128]{2,1,0:T(8,128)(2,1)S(1)} %pad_maximum_fusion.own_ref), channel_id=1, source_target_pairs={{0,1},{1,2},{2,3},{3,4},{4,5},{5,6},{6,7},{7,8},{8,9},{9,10},{10,1... | collective-permute-start | bytes 442376 | tf_op jit(solution)/shard_map/ppermute | solution.py:266
  40.1 7.4 %collective-permute-start.5 = (bf16[1,128,128]{2,1,0:T(8,128)(2,1)S(1)}, bf16[1,128,128]{2,1,0:T(8,128)(2,1)S(1)}, u32[]{:S(2)}, u32[]{:S(2)}) collective-permute-start(bf16[1,128,128]{2,1,0:T(8,128)(2,1)S(1)} %get-tuple-element.36), channel_id=1, source_target_pairs={{0,30},{1,31},{2,0},{3,1},{4,2},{5,3},{6,4},{7,5},{8,6},{9,7},{10,... | collective-permute-start | bytes 98312 | tf_op jit(solution)/shard_map/ppermute | solution.py:266
  42.6 8.5 %collective-permute-start.4 = (bf16[1,128,128]{2,1,0:T(8,128)(2,1)S(1)}, bf16[1,128,128]{2,1,0:T(8,128)(2,1)S(1)}, u32[]{:S(2)}, u32[]{:S(2)}) collective-permute-start(bf16[1,128,128]{2,1,0:T(8,128)(2,1)S(1)} %get-tuple-element.37), channel_id=1, source_target_pairs={{0,2},{1,3},{2,4},{3,5},{4,6},{5,7},{6,8},{7,9},{8,10},{9,11},{10,... | collective-permute-start | bytes 98312 | tf_op jit(solution)/shard_map/ppermute | solution.py:266
  47.5 3.6 %copy-start.7 = (bf16[1,128,128]{2,1,0:T(8,128)(2,1)}, bf16[1,128,128]{2,1,0:T(8,128)(2,1)S(1)}, u32[]{:S(2)}) copy-start(bf16[1,128,128]{2,1,0:T(8,128)(2,1)S(1)} %collective-permute-done.5.right2_ref) | copy-start | bytes 98308
  51.1 0.6 copy-start.8
  51.1 0.7 copy-start.4
  51.1 0.7 copy-start.5
  51.1 0.7 copy-start
  75.7 16.9 %copy-start.3 = (bf16[3,4,100,128]{3,2,1,0:T(8,128)(2,1)S(1)}, bf16[3,4,100,128]{3,2,1,0:T(8,128)(2,1)}, u32[]{:S(2)}) copy-start(bf16[3,4,100,128]{3,2,1,0:T(8,128)(2,1)} %get-tuple-element.14) | copy-start | bytes 921604
  75.7 34.5 %all-to-all-start.2 = ((bf16[512,2,128]{2,1,0:T(2,128)(2,1)}), bf16[512,2,128]{2,1,0:T(2,128)(2,1)S(1)}, u32[]{:S(2)}, u32[]{:S(2)}) async-start(bf16[512,2,128]{2,1,0:T(2,128)(2,1)} %bitcast.25), calls=%async_computation.2 | async-start | bytes 524288 | tf_op jit(solution)/shard_map/all_to_all | solution.py:315
  110.2 0.7 copy-start.1

commit v2 on v1

--- a/solution.py
+++ b/solution.py
@@ -7,9 +7,12 @@
 from jax.experimental.pallas import tpu as pltpu
 from jax.sharding import PartitionSpec as P
 
+
 STEPS = 5
+BLOCK = (4, 5, 4, 6, 4)
 K = 100
 KP = 128
+SPARE = KP - K
 CX = 4
 CY = 128
 CAP = 4
@@ -48,8 +51,8 @@
     before = ones_where(iota((REC, REC), 0) < iota((REC, REC), 1))
     earlier = dot(ones_where(hit), before, NN)
     rank = jnp.sum(jnp.where(hit, earlier, 0.0), 0, keepdims=True).astype(jnp.int32)
-    code_ref[...] = rank * OWN + owner
     slot = owner * CAP + rank
+    code_ref[...] = slot
     mine = jnp.where(rank == m_ref[0], owner * CAP, -CAP)
     rows = iota((OWN * CAP, REC), 0)
     sub = iota((KP, REC), 0)
@@ -65,10 +68,10 @@
 
 
 def window_kernel(
-    m_ref, index_ref, own_ref, left_ref, right_ref, left2_ref, right2_ref, recv_ref,
+    index_ref, own_ref, left_ref, right_ref, left2_ref, right2_ref, recv_ref,
     table_ref, base_kh_ref, mix_ref, base_mix_ref,
     fields_ref, picks_ref, base_ref,
-    start, ping, pong, ocean, kh_pad, mix_pad, base_pad, slots,
+    start, ping, pong, ocean, kh_pad, mix_pad, one_pad, base_pad, first, second,
 ):
     body = pl.ds(8, ROWS)
 
@@ -79,9 +82,9 @@
 
     start[0, pl.ds(16, CY), :] = left2_ref[0].astype(F32)
     start[13, pl.ds(16, CY), :] = right2_ref[0].astype(F32)
-    for first, ref in ((1, left_ref), (5, own_ref), (9, right_ref)):
+    for place, ref in ((1, left_ref), (5, own_ref), (9, right_ref)):
         for c in range(CX):
-            fill(first + c, ref[c])
+            fill(place + c, ref[c])
     kh_pad[...] = jnp.zeros((8, KP), F32)
     kh_pad[0:1, 0:K] = table_ref[pl.ds(index_ref[0], 1), :]
     kh_pad[1:2, 0:K] = table_ref[pl.ds(index_ref[1], 1), :]
@@ -89,14 +92,19 @@
     mix_pad[...] = jnp.zeros((2 * KP, 2 * KP), BF16)
     mix_pad[0:K, 0:K] = mix_ref[0]
     mix_pad[KP : KP + K, KP : KP + K] = mix_ref[1]
-    base_pad[...] = jnp.zeros((KP, KP), BF16)
+    same = iota((KP, KP), 0) == iota((KP, KP), 1)
+    one_pad[...] = jnp.zeros((2 * KP, 2 * KP), BF16)
+    one_pad[0:KP, 0:KP] = ones_where(same)
+    one_pad[KP:, KP:] = ones_where(same)
+    base_pad[...] = jnp.zeros((KP, 2 * KP), BF16)
     base_pad[0:K, 0:K] = base_mix_ref[...]
+    base_pad[:, KP:] = ones_where(same)
 
     for step in range(STEPS):
         source, target = ((ping, pong), (pong, ping))[step % 2]
         row0, count = (8, ROWS) if step < STEPS - 1 else (16, CY)
 
-        def advance(column, _, step=step, source=source, target=target, row0=row0, count=count):
+        def advance(column, step=step, source=source, target=target, row0=row0, count=count):
             def at(run, lon, row):
                 if step == 0:
                     return start[lon, pl.ds(row, count), :]
@@ -114,16 +122,27 @@
                 kh = kh_pad[run : run + 1, :]
                 values.append(value)
                 rights.append((value * (1.0 - 4.0 * kh) + near * kh).astype(BF16))
-            both = dot(jnp.concatenate(rights[:2], 1), mix_pad[...], NT)
-            mixed = (both[:, :KP], both[:, KP:], dot(rights[2], base_pad[...], NT))
+            pair = jnp.concatenate(rights[:2], 1)
+            both = dot(pair, mix_pad[...], NT) + dot(pair, one_pad[...], NT)
+            twice = jnp.concatenate([rights[2], rights[2]], 1)
+            mixed = (both[:, :KP], both[:, KP:], dot(twice, base_pad[...], NT))
             open_ = ocean[column, pl.ds(row0 - 8, count), :] > 0.0
             for run in range(3):
-                vertical = rights[run].astype(F32) + mixed[run]
-                new = jnp.where(open_, vertical, values[run])
+                new = jnp.where(open_, mixed[run], values[run])
                 target[run, column, pl.ds(row0, count), :] = new.astype(BF16).astype(F32)
+
+        columns = 12 - 2 * step
+        block = BLOCK[step]
+
+        def several(turn, _, step=step, block=block, advance=advance):
+            for c in range(block):
+                advance(step + 1 + turn * block + c)
             return 0
 
-        lax.fori_loop(step + 1, 13 - step, advance, 0)
+        if columns == block:
+            several(0, 0)
+        else:
+            lax.fori_loop(0, columns // block, several, 0)
 
     final = pong
     flat = []
@@ -134,25 +153,19 @@
             fields_ref[run, c] = cells.T[0:K, :].astype(BF16)
             parts.append(cells.astype(BF16))
         flat.append(jnp.concatenate(parts, 0))
-    both = jnp.concatenate(flat[:2], 1)
-
-    slots[...] = recv_ref[...].astype(F32)
-    cols = iota((OWN, COLS), 1)
-
-    def chooser(ids):
-        at = ((ids[:, K : K + 1] - 1.0) * CY + ids[:, K + 1 : K + 2]).astype(jnp.int32)
-        return ones_where(at == cols)
-
-    base_all = flat[2]
-    own = jnp.zeros((OWN, KP), F32)
-    for rank in range(CAP):
-        pick = chooser(slots[pl.ds(rank, OWN, stride=CAP), :])
-        picks_ref[rank] = dot(pick, both, NN).astype(BF16)
-        own = jnp.where(m_ref[0] == rank, dot(pick, base_all, NN), own)
-    base_ref[...] = own.astype(BF16)
-
-
-def gram_kernel(m_ref, recv_ref, base_ref, slot_ref, out_ref, slots, greens, weighted, sums, rows2, *, scale):
+    ids = recv_ref[...].astype(F32)
+    at = ((ids[:, K : K + 1] - 1.0) * CY + ids[:, K + 1 : K + 2]).astype(jnp.int32)
+    pick = ones_where(at == iota((OWN * CAP, COLS), 1))
+    base_ref[...] = dot(pick, flat[2], NN).astype(BF16)
+    both = dot(pick, jnp.concatenate(flat[:2], 1), NN)
+    for half, scratch in enumerate((first, second)):
+        scratch[...] = both[:, half * KP : (half + 1) * KP]
+        for rank in range(CAP):
+            picked = scratch[pl.ds(rank, OWN, stride=CAP), :]
+            picks_ref[rank, :, half * KP : (half + 1) * KP] = picked.astype(BF16)
+
+
+def gram_kernel(m_ref, recv_ref, base_ref, slot_ref, out_ref, slots, bases, greens, weighted, sums, *, scale):
     lane = iota((OWN, KP), 1)
 
     def deeper(x):
@@ -162,7 +175,10 @@
     weight = slots[pl.ds(0, OWN, stride=CAP), :]
     inv_var = jnp.where(lane < K, slots[pl.ds(1, OWN, stride=CAP), :], 0.0)
     measured = slots[pl.ds(2, OWN, stride=CAP), :]
-    base = base_ref[...].astype(F32)
+    bases[...] = base_ref[...].astype(F32)
+    base = bases[pl.ds(0, OWN, stride=CAP), :]
+    for rank in range(1, CAP):
+        base = jnp.where(m_ref[0] == rank, bases[pl.ds(rank, OWN, stride=CAP), :], base)
 
     def model(x):
         return weight * x + (1.0 - weight) * deeper(x)
@@ -182,37 +198,50 @@
         sums[len(PAIRS) + a : len(PAIRS) + a + 1, :] = jnp.sum(weighted[a] * misfit, 0, keepdims=True)
     total = jnp.sum(sums[...].T, 0, keepdims=True) * scale
     high = total.astype(BF16).astype(F32)
-    rest = total - high
-    line = iota((1, KP), 1)
-    both = jnp.where(line < 64, high, pltpu.roll(jnp.broadcast_to(rest, (8, KP)), 64, 1)[0:1])
-    rows2[pl.ds(0, OWN, stride=2), :] = base
-    rows2[pl.ds(1, OWN, stride=2), :] = jnp.broadcast_to(both, (OWN, KP))
-    packed = rows2[...].astype(BF16)
-    for copy in range(4):
-        out_ref[copy] = packed
+    high = jnp.broadcast_to(high, (8, KP))
+    rest = jnp.broadcast_to(total, (8, KP)) - high
+    turn = iota((8, KP), 0) % CAP
+    tail = jnp.where(
+        turn == 0,
+        pltpu.roll(high, K, 1),
+        jnp.where(
+            turn == 1,
+            pltpu.roll(high, K - SPARE, 1),
+            jnp.where(turn == 2, pltpu.roll(rest, K, 1), pltpu.roll(rest, K - SPARE, 1)),
+        ),
+    )
+    rows = bases[...].reshape(OWN * CAP // 8, 8, KP)
+    rows = jnp.where(iota((1, 8, KP), 2) < K, rows, tail[None])
+    out_ref[...] = rows.reshape(OWN * CAP, KP).astype(BF16)
 
 
 def result_kernel(recv_ref, code_ref, w_ref, ob_ref, misfit_ref, gram_ref, proj_ref):
     recv = recv_ref[...]
-    count = recv.shape[0]
-    pick = ones_where(iota((count, REC), 0) == 2 * code_ref[...])
+    pick = ones_where(iota((OWN * CAP, REC), 0) == code_ref[...])
     picked = dot(recv, pick, TN)
     values = picked[0:K]
     deeper = jnp.concatenate([picked[1:K], picked[K - 1 : K]], 0)
     weight = w_ref[...]
     misfit_ref[...] = ob_ref[...] - (weight * values + (1.0 - weight) * deeper)
-    odd = iota((8, KP), 0) % 2 == 1
-    part = jnp.sum(recv.astype(F32).reshape(count // 8, 8, KP), 0)
-    total = jnp.sum(jnp.where(odd, part, 0.0), 0, keepdims=True)
-    total = jnp.broadcast_to(total, (8, KP))
-    total = total + pltpu.roll(total, 64, 1)
+    part = jnp.sum(recv.astype(F32).reshape(OWN * CAP // 8, 8, KP), 0)
+    part = part + pltpu.roll(part, 4, 0)
+    part = part + pltpu.roll(part, 6, 0)
     sub, line = iota((8, KP), 0), iota((8, KP), 1)
+    total = jnp.where(
+        line < SPARE,
+        pltpu.roll(jnp.broadcast_to(part[0:1], (8, KP)), SPARE, 1),
+        pltpu.roll(jnp.broadcast_to(part[1:2], (8, KP)), 2 * SPARE, 1),
+    )
     gram = jnp.zeros((8, KP), F32)
     for i, (a, b) in enumerate(PAIRS):
         here = ((sub == a) & (line == b)) | ((sub == b) & (line == a))
         gram = jnp.where(here, total[:, i : i + 1], gram)
     gram_ref[...] = gram[:, 0:MEMBERS]
     proj_ref[...] = pltpu.roll(total, KP - len(PAIRS), 1)[0:1, 0:MEMBERS]
+
+
+def near(x):
+    return pltpu.with_memory_space_constraint(x, VMEM)
 
 
 def vmem(count):
@@ -233,18 +262,6 @@
     lon_count = lax.axis_size("lon")
     w_t, iv_t, ob_t = interp_w.T, obs_inv_var.T, observed.T
 
-    send, code = pl.pallas_call(
-        slots_kernel,
-        out_shape=(
-            jax.ShapeDtypeStruct((OWN * CAP, KP), BF16),
-            jax.ShapeDtypeStruct((1, REC), jnp.int32),
-        ),
-        in_specs=smem(1) + vmem(5),
-        out_specs=tuple(vmem(2)),
-        scratch_shapes=[VMEM((KP, REC), F32)],
-        name="slots",
-    )(mem, owner.reshape(1, REC), column.reshape(1, REC), w_t, iv_t, ob_t)
-
     cells = jnp.transpose(initial_temp, (1, 2, 0)).astype(BF16)
     cells = jnp.concatenate(
         [
@@ -265,20 +282,35 @@
     def shift(x, by):
         return lax.ppermute(x, "lon", [(i, (i + by) % lon_count) for i in range(lon_count)])
 
-    left2, right2 = shift(cells[CX - 1 :], 2), shift(cells[:1], -2)
-    left, right = shift(tall, 1), shift(tall, -1)
+    left2 = shift(cells[CX - 1 :], 2)
+    right2 = shift(cells[:1], -2)
+    left = shift(tall, 1)
+    right = shift(tall, -1)
+
+    owner_row, column_row, tall = lax.optimization_barrier(
+        (owner.reshape(1, REC), column.reshape(1, REC), tall)
+    )
+    send, code = pl.pallas_call(
+        slots_kernel,
+        out_shape=(VMEM((OWN * CAP, KP), BF16), VMEM((1, REC), jnp.int32)),
+        in_specs=smem(1) + vmem(5),
+        out_specs=tuple(vmem(2)),
+        scratch_shapes=[VMEM((KP, REC), F32)],
+        name="slots",
+    )(mem, owner_row, column_row, w_t, iv_t, ob_t)
     recv = lax.all_to_all(
         send.reshape(OWN, CAP, KP), owners, split_axis=0, concat_axis=0, tiled=True
-    ).reshape(OWN * CAP, KP)
+    )
+    recv = recv.reshape(OWN * CAP, KP)
 
     fields, picks, base_rows = pl.pallas_call(
         window_kernel,
         out_shape=(
-            jax.ShapeDtypeStruct((3, CX, K, CY), BF16),
-            jax.ShapeDtypeStruct((CAP, OWN, 2 * KP), BF16),
-            jax.ShapeDtypeStruct((OWN, KP), BF16),
+            VMEM((3, CX, K, CY), BF16),
+            VMEM((CAP, OWN, 2 * KP), BF16),
+            VMEM((OWN * CAP, KP), BF16),
         ),
-        in_specs=smem(2) + vmem(10),
+        in_specs=smem(1) + vmem(10),
         out_specs=tuple(vmem(3)),
         scratch_shapes=[
             VMEM((14, ROWS + 16, KP), F32),
@@ -287,34 +319,36 @@
             VMEM((14, ROWS, KP), F32),
             VMEM((8, KP), F32),
             VMEM((2 * KP, 2 * KP), BF16),
-            VMEM((KP, KP), BF16),
+            VMEM((2 * KP, 2 * KP), BF16),
+            VMEM((KP, 2 * KP), BF16),
+            VMEM((OWN * CAP, KP), F32),
             VMEM((OWN * CAP, KP), F32),
         ],
         name="window",
     )(
-        mem, pert_index, tall, left, right, left2, right2, recv,
+        pert_index, near(tall), near(left), near(right), near(left2), near(right2), near(recv),
         pert_table, base_kh.reshape(1, K), member_mix, base_mix,
     )
 
     members = lax.all_to_all(picks, "mem", split_axis=0, concat_axis=0, tiled=True)
     back = pl.pallas_call(
         functools.partial(gram_kernel, scale=1.0 / (OWN * REC * K)),
-        out_shape=jax.ShapeDtypeStruct((4, 2 * OWN, KP), BF16),
+        out_shape=VMEM((OWN * CAP, KP), BF16),
         in_specs=smem(1) + vmem(3),
         out_specs=vmem(1)[0],
         scratch_shapes=[
             VMEM((OWN * CAP, KP), F32),
+            VMEM((OWN * CAP, KP), F32),
             VMEM((MEMBERS, OWN, KP), F32),
             VMEM((MEMBERS, OWN, KP), F32),
             VMEM((KP, KP), F32),
-            VMEM((2 * OWN, KP), F32),
         ],
         name="gram",
-    )(mem, members, base_rows, recv)
+    )(mem, near(members), near(base_rows), near(recv))
 
     returned = lax.all_to_all(
-        back.reshape(4 * OWN, 2, KP), ("mem", "lat", "lon"), split_axis=0, concat_axis=0, tiled=True
-    ).reshape(8 * OWN, KP)
+        back.reshape(OWN, CAP, KP), owners, split_axis=0, concat_axis=0, tiled=True
+    ).reshape(OWN * CAP, KP)
     misfit_t, gram, proj = pl.pallas_call(
         result_kernel,
         out_shape=(
@@ -325,7 +359,8 @@
         in_specs=vmem(4),
         out_specs=tuple(vmem(3)),
         name="result",
-    )(returned, code, w_t, ob_t)
+    )(near(returned), near(code), w_t, ob_t)
+    gram, proj = lax.psum((gram, proj), "mem")
 
     fields = jnp.transpose(fields, (0, 2, 1, 3))
     return fields[:2], fields[2], gram, proj.reshape(MEMBERS), misfit_t.T

time: 114 us -> 112 us (0.982)
  the two profiles are of different devices: /device:TPU:1 before, /device:TPU:2 now
where the time goes in v2:
time: 112 us; the launch traced here: 111 us
  starting transfers between devices  56.7 us (51%)
  blocking collectives  19.7 us (18%)
  waiting for transfers between devices  16.8 us (15%)
  Pallas kernels  11.9 us (11%)
  local copies, waits for them, and re-layouts  3.2 us (3%)
  other arithmetic  2.01 us (2%)
    all_to_all x1, starting transfers between devices, on_device(): lax.all_to_all(send.reshape(OWN, CAP, KP), owners, split_axis=0, concat_a...  23.5 us
    ppermute x4, starting transfers between devices, shift(): lax.ppermute(x, 'lon', [(i, (i + by) % lon_count) for i in range(lon_coun...  15.8 us
    all_to_all x1, starting transfers between devices, on_device(): lax.all_to_all(back.reshape(OWN, CAP, KP), owners, split_axis=0, concat_a...  13.1 us
    all_to_all x1, waiting for transfers between devices, on_device(): lax.all_to_all(back.reshape(OWN, CAP, KP), owners, split_axis=0, concat_a...  11.7 us
    all_to_all x1, blocking collectives, on_device(): lax.all_to_all(picks, 'mem', split_axis=0, concat_axis=0, tiled=True)  9.85 us
    psum x1, blocking collectives, on_device(): gram, proj = lax.psum((gram, proj), 'mem')  9.83 us
    pallas_call x1, Pallas kernels, on_device(): pl.pallas_call(window_kernel, out_shape=(VMEM((3, CX, K, CY), BF16), VMEM...  6.36 us
    ppermute x4, waiting for transfers between devices, shift(): lax.ppermute(x, 'lon', [(i, (i + by) % lon_count) for i in range(lon_coun...  4.45 us
  transfers between devices with their start and end apart: 8, of which 4 were waited for; matrix products, arithmetic and copies ran while one was open for 2% of the time, Pallas kernels for 0%

profile of v2, /device:TPU:2, one launch (start us, length us, event | category | flops | bytes accessed | tf_op | source)
XLA Modules:
  0.0 111.2 jit_solution(593467834502331102)
XLA Ops:
  0.6 0.7 convert_bitcast_fusion
  1.3 1.0 convert_element_type.9
  2.3 0.2 copy.26
  2.4 0.2 copy.27
  2.7 0.1 pad_maximum_fusion.5
  2.8 1.3 %collective-permute-start.1 = (bf16[4,8,128]{2,1,0:T(8,128)(2,1)S(1)}, bf16[4,8,128]{2,1,0:T(8,128)(2,1)S(1)}, u32[]{:S(2)}, u32[]{:S(2)}) collective-permute-start(bf16[4,8,128]{2,1,0:T(8,128)(2,1)S(1)} %get-tuple-element.46), channel_id=1, source_target_pairs={{32,0},{64,32},{96,64},{33,1},{65,33},{97,65},{34,2},{66,34},{98,6... | collective-permute-start | bytes 24584 | tf_op jit(solution)/shard_map/ppermute | solution.py:277
  4.1 3.0 %collective-permute-start = (bf16[4,8,128]{2,1,0:T(8,128)(2,1)S(1)}, bf16[4,8,128]{2,1,0:T(8,128)(2,1)S(1)}, u32[]{:S(2)}, u32[]{:S(2)}) collective-permute-start(bf16[4,8,128]{2,1,0:T(8,128)(2,1)S(1)} %get-tuple-element.47), channel_id=1, source_target_pairs={{0,32},{32,64},{64,96},{1,33},{33,65},{65,97},{2,34},{34,66},{66,9... | collective-permute-start | bytes 24584 | tf_op jit(solution)/shard_map/ppermute | solution.py:276
  7.1 0.0 collective-permute-done.1
  7.2 0.7 collective-permute-done
  7.9 0.1 pad_maximum_fusion.own_ref
  8.1 2.3 %slots.1 = (bf16[512,128]{1,0:T(8,128)(2,1)}, s32[1,256]{1,0:T(1,128)S(1)}) custom-call(s32[1]{0:T(128)} %bitcast.4.m_ref, s32[1,256]{1,0:T(1,128)} %bitcast.32, s32[1,256]{1,0:T(1,128)} %bitcast.33, f32[100,256]{1,0:T(8,128)} %bitcast.27, f32[100,256]{1,0:T(8,128)} %bitcast.31, f32[100,256]{1,0:T(8,128)} %bitcast.29), custom_call_target="tpu_custom_call" | custom-call | tf_op jit(solution)/shard_map/slots/pallas_call | solution.py:293
  10.4 23.5 %all-to-all-start = ((bf16[128,4,128]{2,1,0:T(4,128)(2,1)}), bf16[128,4,128]{2,1,0:T(4,128)(2,1)S(1)}, u32[]{:S(2)}, u32[]{:S(2)}) async-start(bf16[128,4,128]{2,1,0:T(4,128)(2,1)} %bitcast.8), calls=%async_computation | async-start | bytes 262144 | tf_op jit(solution)/shard_map/all_to_all | solution.py:301
  33.8 0.0 copy-start
  33.9 7.2 %collective-permute-start.3 = (bf16[4,144,128]{2,1,0:T(8,128)(2,1)S(1)}, bf16[4,144,128]{2,1,0:T(8,128)(2,1)S(1)}, u32[]{:S(2)}, u32[]{:S(2)}) collective-permute-start(bf16[4,144,128]{2,1,0:T(8,128)(2,1)S(1)} %pad_maximum_fusion.own_ref), channel_id=1, source_target_pairs={{0,31},{1,0},{2,1},{3,2},{4,3},{5,4},{6,5},{7,6},{8,7},{9,8},{10,9... | collective-permute-start | bytes 442376 | tf_op jit(solution)/shard_map/ppermute | solution.py:283
  41.0 1.9 %collective-permute-start.2 = (bf16[4,144,128]{2,1,0:T(8,128)(2,1)S(1)}, bf16[4,144,128]{2,1,0:T(8,128)(2,1)S(1)}, u32[]{:S(2)}, u32[]{:S(2)}) collective-permute-start(bf16[4,144,128]{2,1,0:T(8,128)(2,1)S(1)} %pad_maximum_fusion.own_ref), channel_id=1, source_target_pairs={{0,1},{1,2},{2,3},{3,4},{4,5},{5,6},{6,7},{7,8},{8,9},{9,10},{10,1... | collective-permute-start | bytes 442376 | tf_op jit(solution)/shard_map/ppermute | solution.py:283
  43.0 0.1 pad_maximum_fusion.1
  43.1 3.0 %collective-permute-start.5 = (bf16[1,128,128]{2,1,0:T(8,128)(2,1)S(1)}, bf16[1,128,128]{2,1,0:T(8,128)(2,1)S(1)}, u32[]{:S(2)}, u32[]{:S(2)}) collective-permute-start(bf16[1,128,128]{2,1,0:T(8,128)(2,1)S(1)} %get-tuple-element.44), channel_id=1, source_target_pairs={{0,30},{1,31},{2,0},{3,1},{4,2},{5,3},{6,4},{7,5},{8,6},{9,7},{10,... | collective-permute-start | bytes 98312 | tf_op jit(solution)/shard_map/ppermute | solution.py:283
  46.1 3.7 %collective-permute-start.4 = (bf16[1,128,128]{2,1,0:T(8,128)(2,1)S(1)}, bf16[1,128,128]{2,1,0:T(8,128)(2,1)S(1)}, u32[]{:S(2)}, u32[]{:S(2)}) collective-permute-start(bf16[1,128,128]{2,1,0:T(8,128)(2,1)S(1)} %get-tuple-element.45), channel_id=1, source_target_pairs={{0,2},{1,3},{2,4},{3,5},{4,6},{5,7},{6,8},{7,9},{8,10},{9,11},{10,... | collective-permute-start | bytes 98312 | tf_op jit(solution)/shard_map/ppermute | solution.py:283
  49.8 0.0 copy-done
  49.8 0.6 copy.28.mix_ref
  50.5 0.1 collective-permute-done.5.right2_ref
  50.6 4.3 %collective-permute-done.4.left2_ref = bf16[1,128,128]{2,1,0:T(8,128)(2,1)S(1)} collective-permute-done((bf16[1,128,128]{2,1,0:T(8,128)(2,1)S(1)}, bf16[1,128,128]{2,1,0:T(8,128)(2,1)S(1)}, u32[]{:S(2)}, u32[]{:S(2)}) %collective-permute-start.4) | collective-permute-done | bytes 32800 | tf_op jit(solution)/shard_map/ppermute | solution.py:283
  54.9 0.0 collective-permute-done.3.right_ref
  54.9 0.0 collective-permute-done.2.left_ref
  54.9 0.0 all-to-all-done
  54.9 6.4 %window.1 = (bf16[3,4,100,128]{3,2,1,0:T(8,128)(2,1)S(1)}, bf16[4,128,256]{2,1,0:T(8,128)(2,1)S(1)}, bf16[512,128]{1,0:T(8,128)(2,1)S(1)}) custom-call(s32[2]{0:T(128)} %index_ref.1, bf16[4,144,128]{2,1,0:T(8,128)(2,1)S(1)} %pad_maximum_fusion.own_ref, bf16[4,144,128]{2,1,0:T(8,128)(2,1)S(1)} %collective-permute-done.2.left_ref, ...), custom_call_target="tpu_custom_call" | custom-call | tf_op jit(solution)/shard_map/window/pallas_call | solution.py:306
  61.3 9.8 %all_to_all.15.recv_ref = bf16[4,128,256]{2,1,0:T(8,128)(2,1)S(1)} all-to-all(bf16[4,128,256]{2,1,0:T(8,128)(2,1)S(1)} %get-tuple-element.21), channel_id=1, replica_groups=mesh['mem'=4,'lat'=4,'lon'=32] {'mem'}, dimensions={0} | all-to-all | bytes 524288 | tf_op jit(solution)/shard_map/all_to_all | solution.py:333
  71.1 1.4 %gram.1 = bf16[512,128]{1,0:T(8,128)(2,1)} custom-call(s32[1]{0:T(128)} %bitcast.4.m_ref, bf16[4,128,256]{2,1,0:T(8,128)(2,1)S(1)} %all_to_all.15.recv_ref, bf16[512,128]{1,0:T(8,128)(2,1)S(1)} %get-tuple-element.22.base_ref, bf16[512,128]{1,0:T(8,128)(2,1)S(1)} %bitcast.20), custom_call_target="tpu_custom_call" | custom-call | tf_op jit(solution)/shard_map/gram/pallas_call | solution.py:334
  72.5 13.1 %all-to-all-start.2 = ((bf16[128,4,128]{2,1,0:T(4,128)(2,1)}), bf16[128,4,128]{2,1,0:T(4,128)(2,1)S(1)}, u32[]{:S(2)}, u32[]{:S(2)}) async-start(bf16[128,4,128]{2,1,0:T(4,128)(2,1)} %bitcast.13), calls=%async_computation.2 | async-start | bytes 262144 | tf_op jit(solution)/shard_map/all_to_all | solution.py:349
  85.7 0.8 copy.29
  86.5 0.7 copy.30
  87.1 11.7 %all-to-all-done.2 = bf16[128,4,128]{2,1,0:T(4,128)(2,1)S(1)} async-done(((bf16[128,4,128]{2,1,0:T(4,128)(2,1)}), bf16[128,4,128]{2,1,0:T(4,128)(2,1)S(1)}, u32[]{:S(2)}, u32[]{:S(2)}) %all-to-all-start.2) | async-done | bytes 131104 | tf_op jit(solution)/shard_map/all_to_all | solution.py:349
  98.8 1.8 %result.1 = (f32[100,256]{1,0:T(8,128)}, f32[8,8]{1,0:T(8,128)}, f32[1,8]{1,0:T(1,128)}) custom-call(bf16[512,128]{1,0:T(8,128)(2,1)S(1)} %bitcast.21, s32[1,256]{1,0:T(1,128)S(1)} %get-tuple-element.23.code_ref, f32[100,256]{1,0:T(8,128)} %bitcast.28, f32[100,256]{1,0:T(8,128)} %bitcast.30), custom_call_target="tpu_custom_call" | custom-call | tf_op jit(solution)/shard_map/result/pallas_call | solution.py:352
  100.6 0.0 copy-start.1
  100.6 0.0 copy-start.2
  100.6 0.7 copy-done.1
  101.3 0.0 copy-done.2
  101.3 9.8 %all-reduce = (f32[8,8]{1,0:T(8,128)}, f32[8]{0:T(128)}) all-reduce(f32[8,8]{1,0:T(8,128)S(1)} %copy-done.1, f32[8]{0:T(128)S(1)} %bitcast.34), channel_id=1, replica_groups=mesh['mem'=4,'lat'=4,'lon'=32] {'mem'}, use_global_device_ids=true, to_apply=%region_0.1 | all-reduce | flops 72 | bytes 576 | tf_op jit(solution)/shard_map/psum | solution.py:363
  (7 shorter events, 0.1 us)
Async XLA Ops:
  2.8 4.4 %collective-permute-start.1 = (bf16[4,8,128]{2,1,0:T(8,128)(2,1)S(1)}, bf16[4,8,128]{2,1,0:T(8,128)(2,1)S(1)}, u32[]{:S(2)}, u32[]{:S(2)}) collective-permute-start(bf16[4,8,128]{2,1,0:T(8,128)(2,1)S(1)} %get-tuple-element.46), channel_id=1, source_target_pairs={{32,0},{64,32},{96,64},{33,1},{65,33},{97,65},{34,2},{66,34},{98,6... | collective-permute-start | bytes 24584 | tf_op jit(solution)/shard_map/ppermute | solution.py:277
  4.1 3.8 %collective-permute-start = (bf16[4,8,128]{2,1,0:T(8,128)(2,1)S(1)}, bf16[4,8,128]{2,1,0:T(8,128)(2,1)S(1)}, u32[]{:S(2)}, u32[]{:S(2)}) collective-permute-start(bf16[4,8,128]{2,1,0:T(8,128)(2,1)S(1)} %get-tuple-element.47), channel_id=1, source_target_pairs={{0,32},{32,64},{64,96},{1,33},{33,65},{65,97},{2,34},{34,66},{66,9... | collective-permute-start | bytes 24584 | tf_op jit(solution)/shard_map/ppermute | solution.py:276
  10.4 44.6 %all-to-all-start = ((bf16[128,4,128]{2,1,0:T(4,128)(2,1)}), bf16[128,4,128]{2,1,0:T(4,128)(2,1)S(1)}, u32[]{:S(2)}, u32[]{:S(2)}) async-start(bf16[128,4,128]{2,1,0:T(4,128)(2,1)} %bitcast.8), calls=%async_computation | async-start | bytes 262144 | tf_op jit(solution)/shard_map/all_to_all | solution.py:301
  33.8 16.0 %copy-start = (bf16[2,100,100]{2,0,1:T(2,128)(2,1)S(1)}, bf16[2,100,100]{2,0,1:T(2,128)(2,1)}, u32[]{:S(2)}) copy-start(bf16[2,100,100]{2,0,1:T(2,128)(2,1)} %param.17) | copy-start | bytes 120004
  33.9 21.1 %collective-permute-start.3 = (bf16[4,144,128]{2,1,0:T(8,128)(2,1)S(1)}, bf16[4,144,128]{2,1,0:T(8,128)(2,1)S(1)}, u32[]{:S(2)}, u32[]{:S(2)}) collective-permute-start(bf16[4,144,128]{2,1,0:T(8,128)(2,1)S(1)} %pad_maximum_fusion.own_ref), channel_id=1, source_target_pairs={{0,31},{1,0},{2,1},{3,2},{4,3},{5,4},{6,5},{7,6},{8,7},{9,8},{10,9... | collective-permute-start | bytes 442376 | tf_op jit(solution)/shard_map/ppermute | solution.py:283
  41.0 13.9 %collective-permute-start.2 = (bf16[4,144,128]{2,1,0:T(8,128)(2,1)S(1)}, bf16[4,144,128]{2,1,0:T(8,128)(2,1)S(1)}, u32[]{:S(2)}, u32[]{:S(2)}) collective-permute-start(bf16[4,144,128]{2,1,0:T(8,128)(2,1)S(1)} %pad_maximum_fusion.own_ref), channel_id=1, source_target_pairs={{0,1},{1,2},{2,3},{3,4},{4,5},{5,6},{6,7},{7,8},{8,9},{9,10},{10,1... | collective-permute-start | bytes 442376 | tf_op jit(solution)/shard_map/ppermute | solution.py:283
  43.1 7.5 %collective-permute-start.5 = (bf16[1,128,128]{2,1,0:T(8,128)(2,1)S(1)}, bf16[1,128,128]{2,1,0:T(8,128)(2,1)S(1)}, u32[]{:S(2)}, u32[]{:S(2)}) collective-permute-start(bf16[1,128,128]{2,1,0:T(8,128)(2,1)S(1)} %get-tuple-element.44), channel_id=1, source_target_pairs={{0,30},{1,31},{2,0},{3,1},{4,2},{5,3},{6,4},{7,5},{8,6},{9,7},{10,... | collective-permute-start | bytes 98312 | tf_op jit(solution)/shard_map/ppermute | solution.py:283
  46.1 8.8 %collective-permute-start.4 = (bf16[1,128,128]{2,1,0:T(8,128)(2,1)S(1)}, bf16[1,128,128]{2,1,0:T(8,128)(2,1)S(1)}, u32[]{:S(2)}, u32[]{:S(2)}) collective-permute-start(bf16[1,128,128]{2,1,0:T(8,128)(2,1)S(1)} %get-tuple-element.45), channel_id=1, source_target_pairs={{0,2},{1,3},{2,4},{3,5},{4,6},{5,7},{6,8},{7,9},{8,10},{9,11},{10,... | collective-permute-start | bytes 98312 | tf_op jit(solution)/shard_map/ppermute | solution.py:283
  72.5 26.3 %all-to-all-start.2 = ((bf16[128,4,128]{2,1,0:T(4,128)(2,1)}), bf16[128,4,128]{2,1,0:T(4,128)(2,1)S(1)}, u32[]{:S(2)}, u32[]{:S(2)}) async-start(bf16[128,4,128]{2,1,0:T(4,128)(2,1)} %bitcast.13), calls=%async_computation.2 | async-start | bytes 262144 | tf_op jit(solution)/shard_map/all_to_all | solution.py:349
  100.6 0.7 copy-start.1
  100.6 0.7 copy-start.2

commit v3 on v2

--- a/solution.py
+++ b/solution.py
@@ -215,7 +215,7 @@
     out_ref[...] = rows.reshape(OWN * CAP, KP).astype(BF16)
 
 
-def result_kernel(recv_ref, code_ref, w_ref, ob_ref, misfit_ref, gram_ref, proj_ref):
+def result_kernel(recv_ref, code_ref, w_ref, ob_ref, misfit_ref, sums_ref):
     recv = recv_ref[...]
     pick = ones_where(iota((OWN * CAP, REC), 0) == code_ref[...])
     picked = dot(recv, pick, TN)
@@ -236,8 +236,8 @@
     for i, (a, b) in enumerate(PAIRS):
         here = ((sub == a) & (line == b)) | ((sub == b) & (line == a))
         gram = jnp.where(here, total[:, i : i + 1], gram)
-    gram_ref[...] = gram[:, 0:MEMBERS]
-    proj_ref[...] = pltpu.roll(total, KP - len(PAIRS), 1)[0:1, 0:MEMBERS]
+    sums_ref[0:MEMBERS, :] = gram
+    sums_ref[MEMBERS:, :] = pltpu.roll(total, KP - len(PAIRS), 1)
 
 
 def near(x):
@@ -287,9 +287,6 @@
     left = shift(tall, 1)
     right = shift(tall, -1)
 
-    owner_row, column_row, tall = lax.optimization_barrier(
-        (owner.reshape(1, REC), column.reshape(1, REC), tall)
-    )
     send, code = pl.pallas_call(
         slots_kernel,
         out_shape=(VMEM((OWN * CAP, KP), BF16), VMEM((1, REC), jnp.int32)),
@@ -297,7 +294,7 @@
         out_specs=tuple(vmem(2)),
         scratch_shapes=[VMEM((KP, REC), F32)],
         name="slots",
-    )(mem, owner_row, column_row, w_t, iv_t, ob_t)
+    )(mem, owner.reshape(1, REC), column.reshape(1, REC), w_t, iv_t, ob_t)
     recv = lax.all_to_all(
         send.reshape(OWN, CAP, KP), owners, split_axis=0, concat_axis=0, tiled=True
     )
@@ -349,21 +346,22 @@
     returned = lax.all_to_all(
         back.reshape(OWN, CAP, KP), owners, split_axis=0, concat_axis=0, tiled=True
     ).reshape(OWN * CAP, KP)
-    misfit_t, gram, proj = pl.pallas_call(
+    misfit_t, sums = pl.pallas_call(
         result_kernel,
         out_shape=(
             jax.ShapeDtypeStruct((K, REC), F32),
-            jax.ShapeDtypeStruct((MEMBERS, MEMBERS), F32),
-            jax.ShapeDtypeStruct((1, MEMBERS), F32),
+            VMEM((2 * MEMBERS, KP), F32),
         ),
         in_specs=vmem(4),
-        out_specs=tuple(vmem(3)),
+        out_specs=tuple(vmem(2)),
         name="result",
     )(near(returned), near(code), w_t, ob_t)
-    gram, proj = lax.psum((gram, proj), "mem")
+    for pairs in (((0, 1), (2, 3)), ((0, 3), (1, 2))):
+        sums = sums + lax.ppermute(sums, "mem", [p for a, b in pairs for p in ((a, b), (b, a))])
+    gram, proj = sums[:MEMBERS, :MEMBERS], sums[MEMBERS, :MEMBERS]
 
     fields = jnp.transpose(fields, (0, 2, 1, 3))
-    return fields[:2], fields[2], gram, proj.reshape(MEMBERS), misfit_t.T
+    return fields[:2], fields[2], gram, proj, misfit_t.T
 
 
 def solution(mesh):

time: 112 us -> 110 us (0.982)
  the two profiles are of different devices: /device:TPU:2 before, /device:TPU:8 now
where the time goes in v3:
time: 110 us; the launch traced here: 109 us
  starting transfers between devices  47.9 us (44%)
  blocking collectives  32 us (29%)
  waiting for transfers between devices  11.5 us (10%)
  Pallas kernels  11.2 us (10%)
  local copies, waits for them, and re-layouts  3.61 us (3%)
  other arithmetic  2.02 us (2%)
    all_to_all x1, blocking collectives, on_device(): lax.all_to_all(back.reshape(OWN, CAP, KP), owners, split_axis=0, concat_a...  21.2 us
    all_to_all x1, starting transfers between devices, on_device(): lax.all_to_all(send.reshape(OWN, CAP, KP), owners, split_axis=0, concat_a...  19.7 us
    ppermute x4, starting transfers between devices, shift(): lax.ppermute(x, 'lon', [(i, (i + by) % lon_count) for i in range(lon_coun...  18.3 us
    all_to_all x1, blocking collectives, on_device(): lax.all_to_all(picks, 'mem', split_axis=0, concat_axis=0, tiled=True)  10.8 us
    pallas_call x1, Pallas kernels, on_device(): pl.pallas_call(window_kernel, out_shape=(VMEM((3, CX, K, CY), BF16), VMEM...  6.36 us
    ppermute x4, waiting for transfers between devices, shift(): lax.ppermute(x, 'lon', [(i, (i + by) % lon_count) for i in range(lon_coun...  6.25 us
    ppermute x2, starting transfers between devices, on_device(): lax.ppermute(sums, 'mem', [p for a, b in pairs for p in ((a, b), (b, a))])  5.53 us
    ppermute x2, waiting for transfers between devices, on_device(): lax.ppermute(sums, 'mem', [p for a, b in pairs for p in ((a, b), (b, a))])  5.25 us
  transfers between devices with their start and end apart: 9, of which 3 were waited for; matrix products, arithmetic and copies ran while one was open for 2% of the time, Pallas kernels for 2%

profile of v3, /device:TPU:8, one launch (start us, length us, event | category | flops | bytes accessed | tf_op | source)
XLA Modules:
  0.0 109.0 jit_solution(10828489889709720060)
XLA Ops:
  0.6 0.7 convert_bitcast_fusion
  1.3 1.0 convert_element_type.9
  2.3 0.2 copy.26
  2.4 0.2 copy.27
  2.7 0.1 pad_maximum_fusion.5
  2.7 1.3 %collective-permute-start.1 = (bf16[4,8,128]{2,1,0:T(8,128)(2,1)S(1)}, bf16[4,8,128]{2,1,0:T(8,128)(2,1)S(1)}, u32[]{:S(2)}, u32[]{:S(2)}) collective-permute-start(bf16[4,8,128]{2,1,0:T(8,128)(2,1)S(1)} %get-tuple-element.36), channel_id=1, source_target_pairs={{32,0},{64,32},{96,64},{33,1},{65,33},{97,65},{34,2},{66,34},{98,6... | collective-permute-start | bytes 24584 | tf_op jit(solution)/shard_map/ppermute | solution.py:277
  4.0 3.0 %collective-permute-start = (bf16[4,8,128]{2,1,0:T(8,128)(2,1)S(1)}, bf16[4,8,128]{2,1,0:T(8,128)(2,1)S(1)}, u32[]{:S(2)}, u32[]{:S(2)}) collective-permute-start(bf16[4,8,128]{2,1,0:T(8,128)(2,1)S(1)} %get-tuple-element.37), channel_id=1, source_target_pairs={{0,32},{32,64},{64,96},{1,33},{33,65},{65,97},{2,34},{34,66},{66,9... | collective-permute-start | bytes 24584 | tf_op jit(solution)/shard_map/ppermute | solution.py:276
  7.1 2.3 %slots.1 = (bf16[512,128]{1,0:T(8,128)(2,1)}, s32[1,256]{1,0:T(1,128)S(1)}) custom-call(s32[1]{0:T(128)} %bitcast.2.m_ref, s32[1,256]{1,0:T(1,128)} %bitcast.34, s32[1,256]{1,0:T(1,128)} %bitcast.35, f32[100,256]{1,0:T(8,128)} %bitcast.29, f32[100,256]{1,0:T(8,128)} %bitcast.33, f32[100,256]{1,0:T(8,128)} %bitcast.31), custom_call_target="tpu_custom_call" | custom-call | tf_op jit(solution)/shard_map/slots/pallas_call | solution.py:290
  9.4 19.7 %all-to-all-start = ((bf16[128,4,128]{2,1,0:T(4,128)(2,1)}), bf16[128,4,128]{2,1,0:T(4,128)(2,1)S(1)}, u32[]{:S(2)}, u32[]{:S(2)}) async-start(bf16[128,4,128]{2,1,0:T(4,128)(2,1)} %bitcast.8), calls=%async_computation | async-start | bytes 262144 | tf_op jit(solution)/shard_map/all_to_all | solution.py:298
  29.2 0.0 collective-permute-done.1
  29.2 0.0 collective-permute-done
  29.2 0.1 pad_maximum_fusion.own_ref
  29.4 0.0 copy-start
  29.4 2.9 %collective-permute-start.3 = (bf16[4,144,128]{2,1,0:T(8,128)(2,1)S(1)}, bf16[4,144,128]{2,1,0:T(8,128)(2,1)S(1)}, u32[]{:S(2)}, u32[]{:S(2)}) collective-permute-start(bf16[4,144,128]{2,1,0:T(8,128)(2,1)S(1)} %pad_maximum_fusion.own_ref), channel_id=1, source_target_pairs={{0,31},{1,0},{2,1},{3,2},{4,3},{5,4},{6,5},{7,6},{8,7},{9,8},{10,9... | collective-permute-start | bytes 442376 | tf_op jit(solution)/shard_map/ppermute | solution.py:283
  32.3 3.0 %collective-permute-start.2 = (bf16[4,144,128]{2,1,0:T(8,128)(2,1)S(1)}, bf16[4,144,128]{2,1,0:T(8,128)(2,1)S(1)}, u32[]{:S(2)}, u32[]{:S(2)}) collective-permute-start(bf16[4,144,128]{2,1,0:T(8,128)(2,1)S(1)} %pad_maximum_fusion.own_ref), channel_id=1, source_target_pairs={{0,1},{1,2},{2,3},{3,4},{4,5},{5,6},{6,7},{7,8},{8,9},{9,10},{10,1... | collective-permute-start | bytes 442376 | tf_op jit(solution)/shard_map/ppermute | solution.py:283
  35.4 0.1 pad_maximum_fusion.1
  35.5 10.4 %collective-permute-start.5 = (bf16[1,128,128]{2,1,0:T(8,128)(2,1)S(1)}, bf16[1,128,128]{2,1,0:T(8,128)(2,1)S(1)}, u32[]{:S(2)}, u32[]{:S(2)}) collective-permute-start(bf16[1,128,128]{2,1,0:T(8,128)(2,1)S(1)} %get-tuple-element.34), channel_id=1, source_target_pairs={{0,30},{1,31},{2,0},{3,1},{4,2},{5,3},{6,4},{7,5},{8,6},{9,7},{10,... | collective-permute-start | bytes 98312 | tf_op jit(solution)/shard_map/ppermute | solution.py:283
  45.9 1.9 %collective-permute-start.4 = (bf16[1,128,128]{2,1,0:T(8,128)(2,1)S(1)}, bf16[1,128,128]{2,1,0:T(8,128)(2,1)S(1)}, u32[]{:S(2)}, u32[]{:S(2)}) collective-permute-start(bf16[1,128,128]{2,1,0:T(8,128)(2,1)S(1)} %get-tuple-element.35), channel_id=1, source_target_pairs={{0,2},{1,3},{2,4},{3,5},{4,6},{5,7},{6,8},{7,9},{8,10},{9,11},{10,... | collective-permute-start | bytes 98312 | tf_op jit(solution)/shard_map/ppermute | solution.py:283
  47.8 0.0 copy-done
  47.8 0.6 copy.28.mix_ref
  48.5 0.0 collective-permute-done.5.right2_ref
  48.5 6.2 %collective-permute-done.4.left2_ref = bf16[1,128,128]{2,1,0:T(8,128)(2,1)S(1)} collective-permute-done((bf16[1,128,128]{2,1,0:T(8,128)(2,1)S(1)}, bf16[1,128,128]{2,1,0:T(8,128)(2,1)S(1)}, u32[]{:S(2)}, u32[]{:S(2)}) %collective-permute-start.4) | collective-permute-done | bytes 32800 | tf_op jit(solution)/shard_map/ppermute | solution.py:283
  54.7 0.0 collective-permute-done.3.right_ref
  54.7 0.0 collective-permute-done.2.left_ref
  54.7 0.0 all-to-all-done
  54.7 6.4 %window.1 = (bf16[3,4,100,128]{3,2,1,0:T(8,128)(2,1)S(1)}, bf16[4,128,256]{2,1,0:T(8,128)(2,1)S(1)}, bf16[512,128]{1,0:T(8,128)(2,1)S(1)}) custom-call(s32[2]{0:T(128)} %index_ref.1, bf16[4,144,128]{2,1,0:T(8,128)(2,1)S(1)} %pad_maximum_fusion.own_ref, bf16[4,144,128]{2,1,0:T(8,128)(2,1)S(1)} %collective-permute-done.2.left_ref, ...), custom_call_target="tpu_custom_call" | custom-call | tf_op jit(solution)/shard_map/window/pallas_call | solution.py:303
  61.1 10.8 %all_to_all.15.recv_ref = bf16[4,128,256]{2,1,0:T(8,128)(2,1)S(1)} all-to-all(bf16[4,128,256]{2,1,0:T(8,128)(2,1)S(1)} %get-tuple-element.14), channel_id=1, replica_groups=mesh['mem'=4,'lat'=4,'lon'=32] {'mem'}, dimensions={0} | all-to-all | bytes 524288 | tf_op jit(solution)/shard_map/all_to_all | solution.py:330
  71.9 0.7 gram.1
  72.6 21.2 %all_to_all.16 = bf16[128,4,128]{2,1,0:T(4,128)(2,1)S(1)} all-to-all(bf16[128,4,128]{2,1,0:T(4,128)(2,1)S(1)} %bitcast.23), channel_id=1, replica_groups=mesh['mem'=4,'lat'=4,'lon'=32] {'lat','lon'}, dimensions={0} | all-to-all | bytes 262144 | tf_op jit(solution)/shard_map/all_to_all | solution.py:346
  93.8 1.8 %result.1 = (f32[100,256]{1,0:T(8,128)}, f32[16,128]{1,0:T(8,128)S(1)}) custom-call(bf16[512,128]{1,0:T(8,128)(2,1)S(1)} %bitcast.22, s32[1,256]{1,0:T(1,128)S(1)} %get-tuple-element.16.code_ref, f32[100,256]{1,0:T(8,128)} %bitcast.30, f32[100,256]{1,0:T(8,128)} %bitcast.32), custom_call_target="tpu_custom_call" | custom-call | tf_op jit(solution)/shard_map/result/pallas_call | solution.py:349
  95.7 2.5 %collective-permute-start.6 = (f32[16,128]{1,0:T(8,128)S(1)}, f32[16,128]{1,0:T(8,128)S(1)}, u32[]{:S(2)}, u32[]{:S(2)}) collective-permute-start(f32[16,128]{1,0:T(8,128)S(1)} %get-tuple-element.17), channel_id=1, source_target_pairs={{0,128},{128,0},{256,384},{384,256},{1,129},{129,1},{257,385},{385... | collective-permute-start | bytes 24584 | tf_op jit(solution)/shard_map/ppermute | solution.py:360
  98.1 3.1 %collective-permute-done.6 = f32[16,128]{1,0:T(8,128)S(1)} collective-permute-done((f32[16,128]{1,0:T(8,128)S(1)}, f32[16,128]{1,0:T(8,128)S(1)}, u32[]{:S(2)}, u32[]{:S(2)}) %collective-permute-start.6) | collective-permute-done | bytes 8224 | tf_op jit(solution)/shard_map/ppermute | solution.py:360
  101.2 3.1 %collective-permute-start.7 = (f32[16,128]{1,0:T(8,128)S(1)}, f32[16,128]{1,0:T(8,128)S(1)}, u32[]{:S(2)}, u32[]{:S(2)}) collective-permute-start(f32[16,128]{1,0:T(8,128)S(1)} %add.6), channel_id=1, source_target_pairs={{0,384},{384,0},{128,256},{256,128},{1,385},{385,1},{129,257},{257... | collective-permute-start | bytes 24584 | tf_op jit(solution)/shard_map/ppermute | solution.py:360
  104.3 0.8 copy.29
  105.1 0.7 copy.30
  105.7 2.2 %collective-permute-done.7 = f32[16,128]{1,0:T(8,128)S(1)} collective-permute-done((f32[16,128]{1,0:T(8,128)S(1)}, f32[16,128]{1,0:T(8,128)S(1)}, u32[]{:S(2)}, u32[]{:S(2)}) %collective-permute-start.7) | collective-permute-done | bytes 8224 | tf_op jit(solution)/shard_map/ppermute | solution.py:360
  107.9 0.5 slice_bitcast_fusion.1
  108.5 0.6 slice.36
  (9 shorter events, 0.1 us)
Async XLA Ops:
  2.7 26.4 %collective-permute-start.1 = (bf16[4,8,128]{2,1,0:T(8,128)(2,1)S(1)}, bf16[4,8,128]{2,1,0:T(8,128)(2,1)S(1)}, u32[]{:S(2)}, u32[]{:S(2)}) collective-permute-start(bf16[4,8,128]{2,1,0:T(8,128)(2,1)S(1)} %get-tuple-element.36), channel_id=1, source_target_pairs={{32,0},{64,32},{96,64},{33,1},{65,33},{97,65},{34,2},{66,34},{98,6... | collective-permute-start | bytes 24584 | tf_op jit(solution)/shard_map/ppermute | solution.py:277
  4.0 25.2 %collective-permute-start = (bf16[4,8,128]{2,1,0:T(8,128)(2,1)S(1)}, bf16[4,8,128]{2,1,0:T(8,128)(2,1)S(1)}, u32[]{:S(2)}, u32[]{:S(2)}) collective-permute-start(bf16[4,8,128]{2,1,0:T(8,128)(2,1)S(1)} %get-tuple-element.37), channel_id=1, source_target_pairs={{0,32},{32,64},{64,96},{1,33},{33,65},{65,97},{2,34},{34,66},{66,9... | collective-permute-start | bytes 24584 | tf_op jit(solution)/shard_map/ppermute | solution.py:276
  9.4 45.3 %all-to-all-start = ((bf16[128,4,128]{2,1,0:T(4,128)(2,1)}), bf16[128,4,128]{2,1,0:T(4,128)(2,1)S(1)}, u32[]{:S(2)}, u32[]{:S(2)}) async-start(bf16[128,4,128]{2,1,0:T(4,128)(2,1)} %bitcast.8), calls=%async_computation | async-start | bytes 262144 | tf_op jit(solution)/shard_map/all_to_all | solution.py:298
  29.4 18.4 %copy-start = (bf16[2,100,100]{2,0,1:T(2,128)(2,1)S(1)}, bf16[2,100,100]{2,0,1:T(2,128)(2,1)}, u32[]{:S(2)}) copy-start(bf16[2,100,100]{2,0,1:T(2,128)(2,1)} %param.17) | copy-start | bytes 120004
  29.4 25.3 %collective-permute-start.3 = (bf16[4,144,128]{2,1,0:T(8,128)(2,1)S(1)}, bf16[4,144,128]{2,1,0:T(8,128)(2,1)S(1)}, u32[]{:S(2)}, u32[]{:S(2)}) collective-permute-start(bf16[4,144,128]{2,1,0:T(8,128)(2,1)S(1)} %pad_maximum_fusion.own_ref), channel_id=1, source_target_pairs={{0,31},{1,0},{2,1},{3,2},{4,3},{5,4},{6,5},{7,6},{8,7},{9,8},{10,9... | collective-permute-start | bytes 442376 | tf_op jit(solution)/shard_map/ppermute | solution.py:283
  32.3 22.4 %collective-permute-start.2 = (bf16[4,144,128]{2,1,0:T(8,128)(2,1)S(1)}, bf16[4,144,128]{2,1,0:T(8,128)(2,1)S(1)}, u32[]{:S(2)}, u32[]{:S(2)}) collective-permute-start(bf16[4,144,128]{2,1,0:T(8,128)(2,1)S(1)} %pad_maximum_fusion.own_ref), channel_id=1, source_target_pairs={{0,1},{1,2},{2,3},{3,4},{4,5},{5,6},{6,7},{7,8},{8,9},{9,10},{10,1... | collective-permute-start | bytes 442376 | tf_op jit(solution)/shard_map/ppermute | solution.py:283
  35.5 13.0 %collective-permute-start.5 = (bf16[1,128,128]{2,1,0:T(8,128)(2,1)S(1)}, bf16[1,128,128]{2,1,0:T(8,128)(2,1)S(1)}, u32[]{:S(2)}, u32[]{:S(2)}) collective-permute-start(bf16[1,128,128]{2,1,0:T(8,128)(2,1)S(1)} %get-tuple-element.34), channel_id=1, source_target_pairs={{0,30},{1,31},{2,0},{3,1},{4,2},{5,3},{6,4},{7,5},{8,6},{9,7},{10,... | collective-permute-start | bytes 98312 | tf_op jit(solution)/shard_map/ppermute | solution.py:283
  45.9 8.8 %collective-permute-start.4 = (bf16[1,128,128]{2,1,0:T(8,128)(2,1)S(1)}, bf16[1,128,128]{2,1,0:T(8,128)(2,1)S(1)}, u32[]{:S(2)}, u32[]{:S(2)}) collective-permute-start(bf16[1,128,128]{2,1,0:T(8,128)(2,1)S(1)} %get-tuple-element.35), channel_id=1, source_target_pairs={{0,2},{1,3},{2,4},{3,5},{4,6},{5,7},{6,8},{7,9},{8,10},{9,11},{10,... | collective-permute-start | bytes 98312 | tf_op jit(solution)/shard_map/ppermute | solution.py:283
  95.7 5.5 %collective-permute-start.6 = (f32[16,128]{1,0:T(8,128)S(1)}, f32[16,128]{1,0:T(8,128)S(1)}, u32[]{:S(2)}, u32[]{:S(2)}) collective-permute-start(f32[16,128]{1,0:T(8,128)S(1)} %get-tuple-element.17), channel_id=1, source_target_pairs={{0,128},{128,0},{256,384},{384,256},{1,129},{129,1},{257,385},{385... | collective-permute-start | bytes 24584 | tf_op jit(solution)/shard_map/ppermute | solution.py:360
  101.2 6.7 %collective-permute-start.7 = (f32[16,128]{1,0:T(8,128)S(1)}, f32[16,128]{1,0:T(8,128)S(1)}, u32[]{:S(2)}, u32[]{:S(2)}) collective-permute-start(f32[16,128]{1,0:T(8,128)S(1)} %add.6), channel_id=1, source_target_pairs={{0,384},{384,0},{128,256},{256,128},{1,385},{385,1},{129,257},{257... | collective-permute-start | bytes 24584 | tf_op jit(solution)/shard_map/ppermute | solution.py:360

commit v4 on v3

--- a/solution.py
+++ b/solution.py
@@ -328,6 +328,8 @@
     )
 
     members = lax.all_to_all(picks, "mem", split_axis=0, concat_axis=0, tiled=True)
+    member_temp = jnp.transpose(fields[:2], (0, 2, 1, 3))
+    base_temp = jnp.transpose(fields[2], (1, 0, 2))
     back = pl.pallas_call(
         functools.partial(gram_kernel, scale=1.0 / (OWN * REC * K)),
         out_shape=VMEM((OWN * CAP, KP), BF16),
@@ -345,7 +347,8 @@
 
     returned = lax.all_to_all(
         back.reshape(OWN, CAP, KP), owners, split_axis=0, concat_axis=0, tiled=True
-    ).reshape(OWN * CAP, KP)
+    )
+    returned = returned.reshape(OWN * CAP, KP)
     misfit_t, sums = pl.pallas_call(
         result_kernel,
         out_shape=(
@@ -360,8 +363,7 @@
         sums = sums + lax.ppermute(sums, "mem", [p for a, b in pairs for p in ((a, b), (b, a))])
     gram, proj = sums[:MEMBERS, :MEMBERS], sums[MEMBERS, :MEMBERS]
 
-    fields = jnp.transpose(fields, (0, 2, 1, 3))
-    return fields[:2], fields[2], gram, proj, misfit_t.T
+    return member_temp, base_temp, gram, proj, misfit_t.T
 
 
 def solution(mesh):

time: 110 us -> 110 us (level)
  no operation moved by 1% of the time
where the time goes in v4:
time: 110 us; the launch traced here: 109 us
  starting transfers between devices  47.9 us (44%)
  blocking collectives  32 us (29%)
  waiting for transfers between devices  11.5 us (10%)
  Pallas kernels  11.2 us (10%)
  local copies, waits for them, and re-layouts  3.61 us (3%)
  other arithmetic  2.02 us (2%)
    all_to_all x1, blocking collectives, on_device(): lax.all_to_all(back.reshape(OWN, CAP, KP), owners, split_axis=0, concat_a...  21.2 us
    all_to_all x1, starting transfers between devices, on_device(): lax.all_to_all(send.reshape(OWN, CAP, KP), owners, split_axis=0, concat_a...  19.7 us
    ppermute x4, starting transfers between devices, shift(): lax.ppermute(x, 'lon', [(i, (i + by) % lon_count) for i in range(lon_coun...  18.3 us
    all_to_all x1, blocking collectives, on_device(): lax.all_to_all(picks, 'mem', split_axis=0, concat_axis=0, tiled=True)  10.8 us
    pallas_call x1, Pallas kernels, on_device(): pl.pallas_call(window_kernel, out_shape=(VMEM((3, CX, K, CY), BF16), VMEM...  6.36 us
    ppermute x4, waiting for transfers between devices, shift(): lax.ppermute(x, 'lon', [(i, (i + by) % lon_count) for i in range(lon_coun...  6.25 us
    ppermute x2, starting transfers between devices, on_device(): lax.ppermute(sums, 'mem', [p for a, b in pairs for p in ((a, b), (b, a))])  5.53 us
    ppermute x2, waiting for transfers between devices, on_device(): lax.ppermute(sums, 'mem', [p for a, b in pairs for p in ((a, b), (b, a))])  5.25 us
  transfers between devices with their start and end apart: 9, of which 3 were waited for; matrix products, arithmetic and copies ran while one was open for 2% of the time, Pallas kernels for 2%

profile of v4, /device:TPU:8, one launch (start us, length us, event | category | flops | bytes accessed | tf_op | source)
XLA Modules:
  0.0 109.0 jit_solution(13046507923256724355)
XLA Ops:
  0.6 0.7 convert_bitcast_fusion
  1.3 1.0 convert_element_type.9
  2.3 0.2 copy.26
  2.4 0.2 copy.27
  2.7 0.1 pad_maximum_fusion.5
  2.7 1.3 %collective-permute-start.1 = (bf16[4,8,128]{2,1,0:T(8,128)(2,1)S(1)}, bf16[4,8,128]{2,1,0:T(8,128)(2,1)S(1)}, u32[]{:S(2)}, u32[]{:S(2)}) collective-permute-start(bf16[4,8,128]{2,1,0:T(8,128)(2,1)S(1)} %get-tuple-element.36), channel_id=1, source_target_pairs={{32,0},{64,32},{96,64},{33,1},{65,33},{97,65},{34,2},{66,34},{98,6... | collective-permute-start | bytes 24584 | tf_op jit(solution)/shard_map/ppermute | solution.py:277
  4.0 3.0 %collective-permute-start = (bf16[4,8,128]{2,1,0:T(8,128)(2,1)S(1)}, bf16[4,8,128]{2,1,0:T(8,128)(2,1)S(1)}, u32[]{:S(2)}, u32[]{:S(2)}) collective-permute-start(bf16[4,8,128]{2,1,0:T(8,128)(2,1)S(1)} %get-tuple-element.37), channel_id=1, source_target_pairs={{0,32},{32,64},{64,96},{1,33},{33,65},{65,97},{2,34},{34,66},{66,9... | collective-permute-start | bytes 24584 | tf_op jit(solution)/shard_map/ppermute | solution.py:276
  7.1 2.3 %slots.1 = (bf16[512,128]{1,0:T(8,128)(2,1)}, s32[1,256]{1,0:T(1,128)S(1)}) custom-call(s32[1]{0:T(128)} %bitcast.2.m_ref, s32[1,256]{1,0:T(1,128)} %bitcast.35, s32[1,256]{1,0:T(1,128)} %bitcast.36, f32[100,256]{1,0:T(8,128)} %bitcast.30, f32[100,256]{1,0:T(8,128)} %bitcast.34, f32[100,256]{1,0:T(8,128)} %bitcast.32), custom_call_target="tpu_custom_call" | custom-call | tf_op jit(solution)/shard_map/slots/pallas_call | solution.py:290
  9.4 19.7 %all-to-all-start = ((bf16[128,4,128]{2,1,0:T(4,128)(2,1)}), bf16[128,4,128]{2,1,0:T(4,128)(2,1)S(1)}, u32[]{:S(2)}, u32[]{:S(2)}) async-start(bf16[128,4,128]{2,1,0:T(4,128)(2,1)} %bitcast.8), calls=%async_computation | async-start | bytes 262144 | tf_op jit(solution)/shard_map/all_to_all | solution.py:298
  29.2 0.0 collective-permute-done.1
  29.2 0.0 collective-permute-done
  29.2 0.1 pad_maximum_fusion.own_ref
  29.4 0.0 copy-start
  29.4 2.9 %collective-permute-start.3 = (bf16[4,144,128]{2,1,0:T(8,128)(2,1)S(1)}, bf16[4,144,128]{2,1,0:T(8,128)(2,1)S(1)}, u32[]{:S(2)}, u32[]{:S(2)}) collective-permute-start(bf16[4,144,128]{2,1,0:T(8,128)(2,1)S(1)} %pad_maximum_fusion.own_ref), channel_id=1, source_target_pairs={{0,31},{1,0},{2,1},{3,2},{4,3},{5,4},{6,5},{7,6},{8,7},{9,8},{10,9... | collective-permute-start | bytes 442376 | tf_op jit(solution)/shard_map/ppermute | solution.py:283
  32.3 3.0 %collective-permute-start.2 = (bf16[4,144,128]{2,1,0:T(8,128)(2,1)S(1)}, bf16[4,144,128]{2,1,0:T(8,128)(2,1)S(1)}, u32[]{:S(2)}, u32[]{:S(2)}) collective-permute-start(bf16[4,144,128]{2,1,0:T(8,128)(2,1)S(1)} %pad_maximum_fusion.own_ref), channel_id=1, source_target_pairs={{0,1},{1,2},{2,3},{3,4},{4,5},{5,6},{6,7},{7,8},{8,9},{9,10},{10,1... | collective-permute-start | bytes 442376 | tf_op jit(solution)/shard_map/ppermute | solution.py:283
  35.4 0.1 pad_maximum_fusion.1
  35.5 10.4 %collective-permute-start.5 = (bf16[1,128,128]{2,1,0:T(8,128)(2,1)S(1)}, bf16[1,128,128]{2,1,0:T(8,128)(2,1)S(1)}, u32[]{:S(2)}, u32[]{:S(2)}) collective-permute-start(bf16[1,128,128]{2,1,0:T(8,128)(2,1)S(1)} %get-tuple-element.34), channel_id=1, source_target_pairs={{0,30},{1,31},{2,0},{3,1},{4,2},{5,3},{6,4},{7,5},{8,6},{9,7},{10,... | collective-permute-start | bytes 98312 | tf_op jit(solution)/shard_map/ppermute | solution.py:283
  45.9 1.9 %collective-permute-start.4 = (bf16[1,128,128]{2,1,0:T(8,128)(2,1)S(1)}, bf16[1,128,128]{2,1,0:T(8,128)(2,1)S(1)}, u32[]{:S(2)}, u32[]{:S(2)}) collective-permute-start(bf16[1,128,128]{2,1,0:T(8,128)(2,1)S(1)} %get-tuple-element.35), channel_id=1, source_target_pairs={{0,2},{1,3},{2,4},{3,5},{4,6},{5,7},{6,8},{7,9},{8,10},{9,11},{10,... | collective-permute-start | bytes 98312 | tf_op jit(solution)/shard_map/ppermute | solution.py:283
  47.8 0.0 copy-done
  47.8 0.6 copy.28.mix_ref
  48.5 0.0 collective-permute-done.5.right2_ref
  48.5 6.2 %collective-permute-done.4.left2_ref = bf16[1,128,128]{2,1,0:T(8,128)(2,1)S(1)} collective-permute-done((bf16[1,128,128]{2,1,0:T(8,128)(2,1)S(1)}, bf16[1,128,128]{2,1,0:T(8,128)(2,1)S(1)}, u32[]{:S(2)}, u32[]{:S(2)}) %collective-permute-start.4) | collective-permute-done | bytes 32800 | tf_op jit(solution)/shard_map/ppermute | solution.py:283
  54.7 0.0 collective-permute-done.3.right_ref
  54.7 0.0 collective-permute-done.2.left_ref
  54.7 0.0 all-to-all-done
  54.7 6.4 %window.1 = (bf16[3,4,100,128]{3,2,1,0:T(8,128)(2,1)S(1)}, bf16[4,128,256]{2,1,0:T(8,128)(2,1)S(1)}, bf16[512,128]{1,0:T(8,128)(2,1)S(1)}) custom-call(s32[2]{0:T(128)} %index_ref.1, bf16[4,144,128]{2,1,0:T(8,128)(2,1)S(1)} %pad_maximum_fusion.own_ref, bf16[4,144,128]{2,1,0:T(8,128)(2,1)S(1)} %collective-permute-done.2.left_ref, ...), custom_call_target="tpu_custom_call" | custom-call | tf_op jit(solution)/shard_map/window/pallas_call | solution.py:303
  61.1 10.8 %all_to_all.15.recv_ref = bf16[4,128,256]{2,1,0:T(8,128)(2,1)S(1)} all-to-all(bf16[4,128,256]{2,1,0:T(8,128)(2,1)S(1)} %get-tuple-element.14), channel_id=1, replica_groups=mesh['mem'=4,'lat'=4,'lon'=32] {'mem'}, dimensions={0} | all-to-all | bytes 524288 | tf_op jit(solution)/shard_map/all_to_all | solution.py:330
  71.9 0.7 gram.1
  72.6 21.2 %all_to_all.16 = bf16[128,4,128]{2,1,0:T(4,128)(2,1)S(1)} all-to-all(bf16[128,4,128]{2,1,0:T(4,128)(2,1)S(1)} %bitcast.26), channel_id=1, replica_groups=mesh['mem'=4,'lat'=4,'lon'=32] {'lat','lon'}, dimensions={0} | all-to-all | bytes 262144 | tf_op jit(solution)/shard_map/all_to_all | solution.py:348
  93.8 1.8 %result.1 = (f32[100,256]{1,0:T(8,128)}, f32[16,128]{1,0:T(8,128)S(1)}) custom-call(bf16[512,128]{1,0:T(8,128)(2,1)S(1)} %bitcast.25, s32[1,256]{1,0:T(1,128)S(1)} %get-tuple-element.16.code_ref, f32[100,256]{1,0:T(8,128)} %bitcast.31, f32[100,256]{1,0:T(8,128)} %bitcast.33), custom_call_target="tpu_custom_call" | custom-call | tf_op jit(solution)/shard_map/result/pallas_call | solution.py:352
  95.7 2.5 %collective-permute-start.6 = (f32[16,128]{1,0:T(8,128)S(1)}, f32[16,128]{1,0:T(8,128)S(1)}, u32[]{:S(2)}, u32[]{:S(2)}) collective-permute-start(f32[16,128]{1,0:T(8,128)S(1)} %get-tuple-element.17), channel_id=1, source_target_pairs={{0,128},{128,0},{256,384},{384,256},{1,129},{129,1},{257,385},{385... | collective-permute-start | bytes 24584 | tf_op jit(solution)/shard_map/ppermute | solution.py:363
  98.1 3.0 %collective-permute-done.6 = f32[16,128]{1,0:T(8,128)S(1)} collective-permute-done((f32[16,128]{1,0:T(8,128)S(1)}, f32[16,128]{1,0:T(8,128)S(1)}, u32[]{:S(2)}, u32[]{:S(2)}) %collective-permute-start.6) | collective-permute-done | bytes 8224 | tf_op jit(solution)/shard_map/ppermute | solution.py:363
  101.2 3.1 %collective-permute-start.7 = (f32[16,128]{1,0:T(8,128)S(1)}, f32[16,128]{1,0:T(8,128)S(1)}, u32[]{:S(2)}, u32[]{:S(2)}) collective-permute-start(f32[16,128]{1,0:T(8,128)S(1)} %add.6), channel_id=1, source_target_pairs={{0,384},{384,0},{128,256},{256,128},{1,385},{385,1},{129,257},{257... | collective-permute-start | bytes 24584 | tf_op jit(solution)/shard_map/ppermute | solution.py:363
  104.3 0.8 copy.29
  105.0 0.7 copy.30
  105.7 2.2 %collective-permute-done.7 = f32[16,128]{1,0:T(8,128)S(1)} collective-permute-done((f32[16,128]{1,0:T(8,128)S(1)}, f32[16,128]{1,0:T(8,128)S(1)}, u32[]{:S(2)}, u32[]{:S(2)}) %collective-permute-start.7) | collective-permute-done | bytes 8224 | tf_op jit(solution)/shard_map/ppermute | solution.py:363
  107.9 0.5 slice_bitcast_fusion.2
  108.5 0.6 slice.34
  (9 shorter events, 0.1 us)
Async XLA Ops:
  2.7 26.4 %collective-permute-start.1 = (bf16[4,8,128]{2,1,0:T(8,128)(2,1)S(1)}, bf16[4,8,128]{2,1,0:T(8,128)(2,1)S(1)}, u32[]{:S(2)}, u32[]{:S(2)}) collective-permute-start(bf16[4,8,128]{2,1,0:T(8,128)(2,1)S(1)} %get-tuple-element.36), channel_id=1, source_target_pairs={{32,0},{64,32},{96,64},{33,1},{65,33},{97,65},{34,2},{66,34},{98,6... | collective-permute-start | bytes 24584 | tf_op jit(solution)/shard_map/ppermute | solution.py:277
  4.0 25.2 %collective-permute-start = (bf16[4,8,128]{2,1,0:T(8,128)(2,1)S(1)}, bf16[4,8,128]{2,1,0:T(8,128)(2,1)S(1)}, u32[]{:S(2)}, u32[]{:S(2)}) collective-permute-start(bf16[4,8,128]{2,1,0:T(8,128)(2,1)S(1)} %get-tuple-element.37), channel_id=1, source_target_pairs={{0,32},{32,64},{64,96},{1,33},{33,65},{65,97},{2,34},{34,66},{66,9... | collective-permute-start | bytes 24584 | tf_op jit(solution)/shard_map/ppermute | solution.py:276
  9.4 45.3 %all-to-all-start = ((bf16[128,4,128]{2,1,0:T(4,128)(2,1)}), bf16[128,4,128]{2,1,0:T(4,128)(2,1)S(1)}, u32[]{:S(2)}, u32[]{:S(2)}) async-start(bf16[128,4,128]{2,1,0:T(4,128)(2,1)} %bitcast.8), calls=%async_computation | async-start | bytes 262144 | tf_op jit(solution)/shard_map/all_to_all | solution.py:298
  29.4 18.4 %copy-start = (bf16[2,100,100]{2,0,1:T(2,128)(2,1)S(1)}, bf16[2,100,100]{2,0,1:T(2,128)(2,1)}, u32[]{:S(2)}) copy-start(bf16[2,100,100]{2,0,1:T(2,128)(2,1)} %param.17) | copy-start | bytes 120004
  29.4 25.3 %collective-permute-start.3 = (bf16[4,144,128]{2,1,0:T(8,128)(2,1)S(1)}, bf16[4,144,128]{2,1,0:T(8,128)(2,1)S(1)}, u32[]{:S(2)}, u32[]{:S(2)}) collective-permute-start(bf16[4,144,128]{2,1,0:T(8,128)(2,1)S(1)} %pad_maximum_fusion.own_ref), channel_id=1, source_target_pairs={{0,31},{1,0},{2,1},{3,2},{4,3},{5,4},{6,5},{7,6},{8,7},{9,8},{10,9... | collective-permute-start | bytes 442376 | tf_op jit(solution)/shard_map/ppermute | solution.py:283
  32.3 22.4 %collective-permute-start.2 = (bf16[4,144,128]{2,1,0:T(8,128)(2,1)S(1)}, bf16[4,144,128]{2,1,0:T(8,128)(2,1)S(1)}, u32[]{:S(2)}, u32[]{:S(2)}) collective-permute-start(bf16[4,144,128]{2,1,0:T(8,128)(2,1)S(1)} %pad_maximum_fusion.own_ref), channel_id=1, source_target_pairs={{0,1},{1,2},{2,3},{3,4},{4,5},{5,6},{6,7},{7,8},{8,9},{9,10},{10,1... | collective-permute-start | bytes 442376 | tf_op jit(solution)/shard_map/ppermute | solution.py:283
  35.5 13.0 %collective-permute-start.5 = (bf16[1,128,128]{2,1,0:T(8,128)(2,1)S(1)}, bf16[1,128,128]{2,1,0:T(8,128)(2,1)S(1)}, u32[]{:S(2)}, u32[]{:S(2)}) collective-permute-start(bf16[1,128,128]{2,1,0:T(8,128)(2,1)S(1)} %get-tuple-element.34), channel_id=1, source_target_pairs={{0,30},{1,31},{2,0},{3,1},{4,2},{5,3},{6,4},{7,5},{8,6},{9,7},{10,... | collective-permute-start | bytes 98312 | tf_op jit(solution)/shard_map/ppermute | solution.py:283
  45.9 8.8 %collective-permute-start.4 = (bf16[1,128,128]{2,1,0:T(8,128)(2,1)S(1)}, bf16[1,128,128]{2,1,0:T(8,128)(2,1)S(1)}, u32[]{:S(2)}, u32[]{:S(2)}) collective-permute-start(bf16[1,128,128]{2,1,0:T(8,128)(2,1)S(1)} %get-tuple-element.35), channel_id=1, source_target_pairs={{0,2},{1,3},{2,4},{3,5},{4,6},{5,7},{6,8},{7,9},{8,10},{9,11},{10,... | collective-permute-start | bytes 98312 | tf_op jit(solution)/shard_map/ppermute | solution.py:283
  95.7 5.5 %collective-permute-start.6 = (f32[16,128]{1,0:T(8,128)S(1)}, f32[16,128]{1,0:T(8,128)S(1)}, u32[]{:S(2)}, u32[]{:S(2)}) collective-permute-start(f32[16,128]{1,0:T(8,128)S(1)} %get-tuple-element.17), channel_id=1, source_target_pairs={{0,128},{128,0},{256,384},{384,256},{1,129},{129,1},{257,385},{385... | collective-permute-start | bytes 24584 | tf_op jit(solution)/shard_map/ppermute | solution.py:363
  101.2 6.7 %collective-permute-start.7 = (f32[16,128]{1,0:T(8,128)S(1)}, f32[16,128]{1,0:T(8,128)S(1)}, u32[]{:S(2)}, u32[]{:S(2)}) collective-permute-start(f32[16,128]{1,0:T(8,128)S(1)} %add.6), channel_id=1, source_target_pairs={{0,384},{384,0},{128,256},{256,128},{1,385},{385,1},{129,257},{257... | collective-permute-start | bytes 24584 | tf_op jit(solution)/shard_map/ppermute | solution.py:363

commit v5 on v2

v5 whole, which is shorter than its diff:
```python
import functools

import jax
import jax.numpy as jnp
from jax import lax
from jax.experimental import pallas as pl
from jax.experimental.pallas import tpu as pltpu
from jax.sharding import PartitionSpec as P


STEPS = 5
BLOCK = 2
K = 100
KP = 128
SPARE = KP - K
CX = 4
CY = 128
CAP = 4
OWN = 128
REC = 256
HALO = 8
ROWS = CY + 2 * HALO
COLS = CX * CY
MEMBERS = 8
RUNS = MEMBERS + 1
MIX = 104
PAIRS = [(a, b) for a in range(MEMBERS) for b in range(a, MEMBERS)]
F32 = jnp.float32
BF16 = jnp.bfloat16
NT = (((1,), (1,)), ((), ()))
NN = (((1,), (0,)), ((), ()))
TN = (((0,), (0,)), ((), ()))
SMEM = pltpu.SMEM
VMEM = pltpu.VMEM


def dot(a, b, dims):
    return lax.dot_general(a, b, dims, preferred_element_type=F32)


def ones_where(cond):
    return jnp.where(cond, 1.0, 0.0).astype(BF16)


def iota(shape, dim):
    return lax.broadcasted_iota(jnp.int32, shape, dim)


def slots_kernel(owner_ref, column_ref, w_ref, iv_ref, ob_ref, out_ref, code_ref, pad, rows3):
    owner = owner_ref[...]
    column = column_ref[...]
    hit = iota((OWN, REC), 0) == owner
    before = ones_where(iota((REC, REC), 0) < iota((REC, REC), 1))
    earlier = dot(ones_where(hit), before, NN)
    rank = jnp.sum(jnp.where(hit, earlier, 0.0), 0, keepdims=True).astype(jnp.int32)
    slot = owner * CAP + rank
    code_ref[...] = slot
    pad[...] = jnp.zeros((3 * KP, REC), F32)
    for group, ref in enumerate((w_ref, iv_ref, ob_ref)):
        pad[group * KP : group * KP + K, :] = ref[...]
    pad[K : K + 1, :] = (column // CY + 1).astype(F32)
    pad[K + 1 : K + 2, :] = (column % CY).astype(F32)
    place = ones_where(iota((OWN * CAP, REC), 0) == slot)
    placed = dot(place, pad[...].astype(BF16), NT)
    for group in range(3):
        rows3[pl.ds(group, OWN * CAP, stride=3), :] = placed[:, group * KP : (group + 1) * KP]
    out_ref[...] = rows3[...].astype(BF16)


def mixes_kernel(index_ref, table_ref, mix_ref, out_ref, pad):
    for j in range(2):
        pad[...] = jnp.zeros((MIX, KP), F32)
        pad[0:K, 0:K] = mix_ref[j].astype(F32)
        kh = table_ref[pl.ds(index_ref[j], 1), :]
        high = kh.astype(BF16).astype(F32)
        pad[K : K + 1, 0:K] = high
        pad[K + 1 : K + 2, 0:K] = kh - high
        out_ref[j] = pad[...].astype(BF16)


def window_kernel(
    m_ref, own_ref, left_ref, right_ref, left2_ref, right2_ref, recv_ref,
    mixes0_ref, mixes1_ref, mixes2_ref, mixes3_ref,
    base_kh_ref, base_mix_ref,
    fields_ref, out_ref,
    start, ping, pong, ocean, kh_pad, mix_pad, one_pad, base_pad, slots, greens, weighted, sums,
    *, scale,
):
    body = pl.ds(8, ROWS)

    def fill(column, cells):
        cells = cells.astype(F32)
        start[column, body, :] = cells
        ocean[column] = jnp.broadcast_to(cells[:, K : K + 1], (ROWS, KP))

    start[0, pl.ds(16, CY), :] = left2_ref[0].astype(F32)
    start[13, pl.ds(16, CY), :] = right2_ref[0].astype(F32)
    for place, ref in ((1, left_ref), (5, own_ref), (9, right_ref)):
        for c in range(CX):
            fill(place + c, ref[c])
    kh_pad[...] = jnp.zeros((16, KP), F32)
    mix_pad[...] = jnp.zeros((MEMBERS // 2, 2 * KP, 2 * KP), BF16)
    for back, ref in enumerate((mixes0_ref, mixes1_ref, mixes2_ref, mixes3_ref)):
        pair = lax.rem(m_ref[0] + 4 - back, 4)
        for half in range(2):
            spot = half * KP
            mix_pad[pair, spot : spot + K, spot : spot + KP] = ref[half, 0:K, :]
            parts = ref[half, MIX - 8 : MIX, :].astype(F32)
            kh_pad[pl.ds(2 * pair + half, 1), :] = parts[4:5] + parts[5:6]
    kh_pad[MEMBERS : MEMBERS + 1, 0:K] = base_kh_ref[...]
    same = iota((KP, KP), 0) == iota((KP, KP), 1)
    one_pad[...] = jnp.zeros((2 * KP, 2 * KP), BF16)
    one_pad[0:KP, 0:KP] = ones_where(same)
    one_pad[KP:, KP:] = ones_where(same)
    base_pad[...] = jnp.zeros((KP, 2 * KP), BF16)
    base_pad[0:K, 0:K] = base_mix_ref[...]
    base_pad[:, KP:] = ones_where(same)

    for step in range(STEPS):
        source, target = ((ping, pong), (pong, ping))[step % 2]
        row0, count = (12, CY + 8) if step < STEPS - 1 else (16, CY)

        def advance(column, step=step, source=source, target=target, row0=row0, count=count):
            def at(run, lon, row):
                if step == 0:
                    return start[lon, pl.ds(row, count), :]
                return source[run, lon, pl.ds(row, count), :]

            def around(run):
                return (at(run, column + 1, row0) + at(run, column - 1, row0)) + (
                    at(run, column, row0 + 1) + at(run, column, row0 - 1)
                )

            shared = (at(0, column, row0), around(0)) if step == 0 else None
            open_ = ocean[column, pl.ds(row0 - 8, count), :] > 0.0

            def right_of(run):
                value, near = shared if step == 0 else (at(run, column, row0), around(run))
                kh = kh_pad[run : run + 1, :]
                return value, (value * (1.0 - 4.0 * kh) + near * kh).astype(BF16)

            def put(run, mixed, value):
                new = jnp.where(open_, mixed, value)
                target[run, column, pl.ds(row0, count), :] = new.astype(BF16).astype(F32)

            for pair in range(MEMBERS // 2):
                value0, right0 = right_of(2 * pair)
                value1, right1 = right_of(2 * pair + 1)
                right = jnp.concatenate([right0, right1], 1)
                both = dot(right, mix_pad[pair], NT) + dot(right, one_pad[...], NT)
                put(2 * pair, both[:, :KP], value0)
                put(2 * pair + 1, both[:, KP:], value1)
            value, right = right_of(MEMBERS)
            put(MEMBERS, dot(jnp.concatenate([right, right], 1), base_pad[...], NT), value)

        columns = 12 - 2 * step

        def several(turn, _, step=step, advance=advance):
            for c in range(BLOCK):
                advance(step + 1 + turn * BLOCK + c)
            return 0

        lax.fori_loop(0, columns // BLOCK, several, 0)

    final = pong

    def flat(run):
        return jnp.concatenate([final[run, 5 + c, pl.ds(16, CY), :].astype(BF16) for c in range(CX)], 0)

    for place, run in enumerate((2 * m_ref[0], 2 * m_ref[0] + 1, MEMBERS)):
        for c in range(CX):
            fields_ref[place, c] = final[run, 5 + c, pl.ds(16, CY), :].T[0:K, :].astype(BF16)

    count = OWN * CAP
    slots[...] = recv_ref[...].astype(F32)
    weight = slots[pl.ds(0, count, stride=3), :]
    inv_var = slots[pl.ds(1, count, stride=3), :]
    measured = slots[pl.ds(2, count, stride=3), :]
    at = ((weight[:, K : K + 1] - 1.0) * CY + weight[:, K + 1 : K + 2]).astype(jnp.int32)
    pick = ones_where(at == iota((count, COLS), 1))
    weight = jnp.where(iota((count, KP), 1) < K - 1, weight, 1.0)

    def model(x):
        below = pltpu.roll(x, KP - 1, 1)
        return below + weight * (x - below)

    base = dot(pick, flat(MEMBERS), NN)
    misfit = measured - model(base)
    for pair in range(MEMBERS // 2):
        both = dot(pick, jnp.concatenate([flat(2 * pair), flat(2 * pair + 1)], 1), NN)
        for half in range(2):
            green = model(both[:, half * KP : (half + 1) * KP] - base).astype(BF16).astype(F32)
            greens[2 * pair + half] = green
            weighted[2 * pair + half] = green * inv_var
    sums[...] = jnp.zeros((KP, KP), F32)
    for i, (a, b) in enumerate(PAIRS):
        sums[i : i + 1, :] = jnp.sum(weighted[a] * greens[b], 0, keepdims=True)
    for a in range(MEMBERS):
        sums[len(PAIRS) + a : len(PAIRS) + a + 1, :] = jnp.sum(weighted[a] * misfit, 0, keepdims=True)
    total = jnp.sum(sums[...].T, 0, keepdims=True) * scale
    high = jnp.broadcast_to(total.astype(BF16).astype(F32), (8, KP))
    rest = jnp.broadcast_to(total, (8, KP)) - high
    turn = iota((8, KP), 0) % CAP
    tail = jnp.where(
        turn == 0,
        pltpu.roll(high, K, 1),
        jnp.where(
            turn == 1,
            pltpu.roll(high, K - SPARE, 1),
            jnp.where(turn == 2, pltpu.roll(rest, K, 1), pltpu.roll(rest, K - SPARE, 1)),
        ),
    )
    rows = jnp.where(iota((1, 8, KP), 2) < K, base.reshape(count // 8, 8, KP), tail[None])
    out_ref[...] = rows.reshape(count, KP).astype(BF16)


def result_kernel(recv_ref, code_ref, w_ref, ob_ref, misfit_ref, gram_ref, proj_ref):
    recv = recv_ref[...]
    pick = ones_where(iota((OWN * CAP, REC), 0) == code_ref[...])
    picked = dot(recv, pick, TN)
    values = picked[0:K]
    deeper = jnp.concatenate([picked[1:K], picked[K - 1 : K]], 0)
    weight = w_ref[...]
    misfit_ref[...] = ob_ref[...] - (weight * values + (1.0 - weight) * deeper)
    part = jnp.sum(recv.astype(F32).reshape(OWN * CAP // 8, 8, KP), 0)
    part = part + pltpu.roll(part, 4, 0)
    part = part + pltpu.roll(part, 6, 0)
    sub, line = iota((8, KP), 0), iota((8, KP), 1)
    total = jnp.where(
        line < SPARE,
        pltpu.roll(jnp.broadcast_to(part[0:1], (8, KP)), SPARE, 1),
        pltpu.roll(jnp.broadcast_to(part[1:2], (8, KP)), 2 * SPARE, 1),
    )
    gram = jnp.zeros((8, KP), F32)
    for i, (a, b) in enumerate(PAIRS):
        here = ((sub == a) & (line == b)) | ((sub == b) & (line == a))
        gram = jnp.where(here, total[:, i : i + 1], gram)
    gram_ref[...] = gram[:, 0:MEMBERS]
    proj_ref[...] = pltpu.roll(total, KP - len(PAIRS), 1)[0:1, 0:MEMBERS]


def near(x):
    return pltpu.with_memory_space_constraint(x, VMEM)


def vmem(count):
    return [pl.BlockSpec(memory_space=VMEM)] * count


def smem(count):
    return [pl.BlockSpec(memory_space=SMEM)] * count


def on_device(
    initial_temp, land_mask, pert_table, pert_index, base_kh, member_mix, base_mix,
    owner, column, interp_w, obs_inv_var, observed,
):
    owners = ("lat", "lon")
    mem = lax.axis_index("mem").astype(jnp.int32).reshape(1)
    lat_at, lat_count = lax.axis_index("lat"), lax.axis_size("lat")
    lon_count = lax.axis_size("lon")
    w_t, iv_t, ob_t = interp_w.T, obs_inv_var.T, observed.T

    cells = jnp.transpose(initial_temp, (1, 2, 0)).astype(BF16)
    cells = jnp.concatenate(
        [
            cells,
            land_mask.astype(BF16)[:, :, None],
            jnp.zeros((CX, CY, KP - K - 1), BF16),
        ],
        2,
    )
    up = [(i, i + 1) for i in range(lat_count - 1)]
    down = [(i + 1, i) for i in range(lat_count - 1)]
    below = lax.ppermute(cells[:, CY - HALO :], "lat", up)
    above = lax.ppermute(cells[:, :HALO], "lat", down)
    below = jnp.where(lat_at == 0, cells[:, :HALO][:, ::-1], below)
    above = jnp.where(lat_at == lat_count - 1, cells[:, CY - HALO :][:, ::-1], above)
    tall = jnp.concatenate([below, cells, above], 1)

    def shift(x, by):
        return lax.ppermute(x, "lon", [(i, (i + by) % lon_count) for i in range(lon_count)])

    left2 = shift(cells[CX - 1 :], 2)
    right2 = shift(cells[:1], -2)
    left = shift(tall, 1)
    right = shift(tall, -1)

    send, code = pl.pallas_call(
        slots_kernel,
        out_shape=(VMEM((3 * OWN * CAP, KP), BF16), VMEM((1, REC), jnp.int32)),
        in_specs=vmem(5),
        out_specs=tuple(vmem(2)),
        scratch_shapes=[VMEM((3 * KP, REC), F32), VMEM((3 * OWN * CAP, KP), F32)],
        name="slots",
    )(owner.reshape(1, REC), column.reshape(1, REC), w_t, iv_t, ob_t)
    recv = lax.all_to_all(
        send.reshape(OWN, 3, CAP, KP), owners, split_axis=0, concat_axis=0, tiled=True
    )
    recv = recv.reshape(3 * OWN * CAP, KP)

    own_mixes = pl.pallas_call(
        mixes_kernel,
        out_shape=VMEM((2, MIX, KP), BF16),
        in_specs=smem(1) + vmem(2),
        out_specs=vmem(1)[0],
        scratch_shapes=[VMEM((MIX, KP), F32)],
        name="mixes",
    )(pert_index, pert_table, member_mix)
    mixes = [own_mixes]
    for back in range(1, 4):
        mixes.append(lax.ppermute(own_mixes, "mem", [(i, (i + back) % 4) for i in range(4)]))

    fields, back = pl.pallas_call(
        functools.partial(window_kernel, scale=1.0 / (OWN * REC * K)),
        out_shape=(VMEM((3, CX, K, CY), BF16), VMEM((OWN * CAP, KP), BF16)),
        in_specs=smem(1) + vmem(12),
        out_specs=tuple(vmem(2)),
        scratch_shapes=[
            VMEM((14, ROWS + 16, KP), F32),
            VMEM((RUNS, 14, ROWS + 16, KP), F32),
            VMEM((RUNS, 14, ROWS + 16, KP), F32),
            VMEM((14, ROWS, KP), F32),
            VMEM((16, KP), F32),
            VMEM((MEMBERS // 2, 2 * KP, 2 * KP), BF16),
            VMEM((2 * KP, 2 * KP), BF16),
            VMEM((KP, 2 * KP), BF16),
            VMEM((3 * OWN * CAP, KP), F32),
            VMEM((MEMBERS, OWN * CAP, KP), F32),
            VMEM((MEMBERS, OWN * CAP, KP), F32),
            VMEM((KP, KP), F32),
        ],
        name="window",
    )(
        mem, near(tall), near(left), near(right), near(left2), near(right2), near(recv),
        *map(near, mixes),
        base_kh.reshape(1, K), base_mix,
    )

    returned = lax.all_to_all(
        back.reshape(OWN, CAP, KP), owners, split_axis=0, concat_axis=0, tiled=True
    )
    returned = returned.reshape(OWN * CAP, KP)
    misfit_t, gram, proj = pl.pallas_call(
        result_kernel,
        out_shape=(
            jax.ShapeDtypeStruct((K, REC), F32),
            jax.ShapeDtypeStruct((MEMBERS, MEMBERS), F32),
            jax.ShapeDtypeStruct((1, MEMBERS), F32),
        ),
        in_specs=vmem(4),
        out_specs=tuple(vmem(3)),
        name="result",
    )(near(returned), near(code), w_t, ob_t)
    proj = proj.reshape(MEMBERS)
    fields = jnp.transpose(fields, (0, 2, 1, 3))
    member_temp, base_temp = fields[:2], fields[2]

    return member_temp, base_temp, gram, proj, misfit_t.T


def solution(mesh):
    placed = (
        P(None, "lon", "lat"),
        P("lon", "lat"),
        P(),
        P("mem"),
        P(),
        P("mem", None, None),
        P(),
        P(("lat", "lon"), None),
        P(("lat", "lon")),
        P(("lat", "lon"), None),
        P(("lat", "lon"), None),
        P(("lat", "lon"), None),
    )
    return jax.shard_map(
        on_device,
        mesh=mesh,
        in_specs=placed,
        out_specs=(
            P("mem", None, "lon", "lat"),
            P(None, "lon", "lat"),
            P(),
            P(),
            P(("lat", "lon"), None),
        ),
        check_vma=False,
    )
```

time: 112 us -> 117 us (1.045)
  the two profiles are of different devices: /device:TPU:2 before, /device:TPU:1 now
where the time goes in v5:
time: 117 us; the launch traced here: 116 us
  starting transfers between devices  66.9 us (57%)
  Pallas kernels  25.5 us (22%)
  waiting for transfers between devices  20 us (17%)
  local copies, waits for them, and re-layouts  2.51 us (2%)
    pallas_call x1, Pallas kernels, on_device(): pl.pallas_call(functools.partial(window_kernel, scale=1.0 / (OWN * REC *...  20.5 us
    all_to_all x1, starting transfers between devices, on_device(): lax.all_to_all(send.reshape(OWN, 3, CAP, KP), owners, split_axis=0, conca...  18.6 us
    all_to_all x1, starting transfers between devices, on_device(): lax.all_to_all(back.reshape(OWN, CAP, KP), owners, split_axis=0, concat_a...  16.9 us
    ppermute x4, starting transfers between devices, shift(): lax.ppermute(x, 'lon', [(i, (i + by) % lon_count) for i in range(lon_coun...  12.4 us
    all_to_all x1, waiting for transfers between devices, on_device(): lax.all_to_all(back.reshape(OWN, CAP, KP), owners, split_axis=0, concat_a...  12 us
    ppermute x3, starting transfers between devices, on_device(): lax.ppermute(own_mixes, 'mem', [(i, (i + back) % 4) for i in range(4)])  9.34 us
    ppermute x1, starting transfers between devices, on_device(): below = lax.ppermute(cells[:, CY - HALO:], 'lat', up)  6.88 us
    ppermute x1, waiting for transfers between devices, on_device(): above = lax.ppermute(cells[:, :HALO], 'lat', down)  4.38 us
  transfers between devices with their start and end apart: 11, of which 4 were waited for; matrix products, arithmetic and copies ran while one was open for 2% of the time, Pallas kernels for 1%

profile of v5, /device:TPU:1, one launch (start us, length us, event | category | flops | bytes accessed | tf_op | source)
XLA Modules:
  0.0 116.1 jit_solution(16228863693265305500)
XLA Ops:
  0.6 2.3 %slots.1 = (bf16[1536,128]{1,0:T(8,128)(2,1)}, s32[1,256]{1,0:T(1,128)S(1)}) custom-call(s32[1,256]{1,0:T(1,128)} %bitcast.31, s32[1,256]{1,0:T(1,128)} %bitcast.32, f32[100,256]{1,0:T(8,128)} %bitcast.26, f32[100,256]{1,0:T(8,128)} %bitcast.30, f32[100,256]{1,0:T(8,128)} %bitcast.28), custom_call_target="tpu_custom_call" | custom-call | tf_op jit(solution)/shard_map/slots/pallas_call | solution.py:289
  2.9 0.0 copy-start.2
  2.9 0.0 copy-start
  2.9 18.6 %all-to-all-start = ((bf16[128,3,4,128]{3,2,1,0:T(4,128)(2,1)}), bf16[128,3,4,128]{3,2,1,0:T(4,128)(2,1)S(1)}, u32[]{:S(2)}, u32[]{:S(2)}) async-start(bf16[128,3,4,128]{3,2,1,0:T(4,128)(2,1)} %bitcast.8), calls=%async_computation | async-start | bytes 786432 | tf_op jit(solution)/shard_map/all_to_all | solution.py:297
  21.6 0.0 copy-done.2
  21.6 0.0 copy-done
  21.7 0.2 copy.26
  21.8 0.2 copy.27
  22.0 0.1 pad_maximum_fusion.5
  22.1 2.7 %collective-permute-start.1 = (bf16[4,8,128]{2,1,0:T(8,128)(2,1)S(1)}, bf16[4,8,128]{2,1,0:T(8,128)(2,1)S(1)}, u32[]{:S(2)}, u32[]{:S(2)}) collective-permute-start(bf16[4,8,128]{2,1,0:T(8,128)(2,1)S(1)} %get-tuple-element.36), channel_id=1, source_target_pairs={{32,0},{64,32},{96,64},{33,1},{65,33},{97,65},{34,2},{66,34},{98,6... | collective-permute-start | bytes 24584 | tf_op jit(solution)/shard_map/ppermute | solution.py:276
  24.8 6.9 %collective-permute-start = (bf16[4,8,128]{2,1,0:T(8,128)(2,1)S(1)}, bf16[4,8,128]{2,1,0:T(8,128)(2,1)S(1)}, u32[]{:S(2)}, u32[]{:S(2)}) collective-permute-start(bf16[4,8,128]{2,1,0:T(8,128)(2,1)S(1)} %get-tuple-element.37), channel_id=1, source_target_pairs={{0,32},{32,64},{64,96},{1,33},{33,65},{65,97},{2,34},{34,66},{66,9... | collective-permute-start | bytes 24584 | tf_op jit(solution)/shard_map/ppermute | solution.py:275
  31.8 4.4 %collective-permute-done.1 = bf16[4,8,128]{2,1,0:T(8,128)(2,1)S(1)} collective-permute-done((bf16[4,8,128]{2,1,0:T(8,128)(2,1)S(1)}, bf16[4,8,128]{2,1,0:T(8,128)(2,1)S(1)}, u32[]{:S(2)}, u32[]{:S(2)}) %collective-permute-start.1) | collective-permute-done | bytes 8224 | tf_op jit(solution)/shard_map/ppermute | solution.py:276
  36.2 0.0 collective-permute-done
  36.2 0.1 pad_maximum_fusion.own_ref
  36.3 0.0 copy-start.1
  36.3 4.3 %collective-permute-start.3 = (bf16[4,144,128]{2,1,0:T(8,128)(2,1)S(1)}, bf16[4,144,128]{2,1,0:T(8,128)(2,1)S(1)}, u32[]{:S(2)}, u32[]{:S(2)}) collective-permute-start(bf16[4,144,128]{2,1,0:T(8,128)(2,1)S(1)} %pad_maximum_fusion.own_ref), channel_id=1, source_target_pairs={{0,31},{1,0},{2,1},{3,2},{4,3},{5,4},{6,5},{7,6},{8,7},{9,8},{10,9... | collective-permute-start | bytes 442376 | tf_op jit(solution)/shard_map/ppermute | solution.py:282
  40.7 1.9 %collective-permute-start.2 = (bf16[4,144,128]{2,1,0:T(8,128)(2,1)S(1)}, bf16[4,144,128]{2,1,0:T(8,128)(2,1)S(1)}, u32[]{:S(2)}, u32[]{:S(2)}) collective-permute-start(bf16[4,144,128]{2,1,0:T(8,128)(2,1)S(1)} %pad_maximum_fusion.own_ref), channel_id=1, source_target_pairs={{0,1},{1,2},{2,3},{3,4},{4,5},{5,6},{6,7},{7,8},{8,9},{9,10},{10,1... | collective-permute-start | bytes 442376 | tf_op jit(solution)/shard_map/ppermute | solution.py:282
  42.6 0.1 pad_maximum_fusion.1
  42.7 3.7 %collective-permute-start.5 = (bf16[1,128,128]{2,1,0:T(8,128)(2,1)S(1)}, bf16[1,128,128]{2,1,0:T(8,128)(2,1)S(1)}, u32[]{:S(2)}, u32[]{:S(2)}) collective-permute-start(bf16[1,128,128]{2,1,0:T(8,128)(2,1)S(1)} %get-tuple-element.34), channel_id=1, source_target_pairs={{0,30},{1,31},{2,0},{3,1},{4,2},{5,3},{6,4},{7,5},{8,6},{9,7},{10,... | collective-permute-start | bytes 98312 | tf_op jit(solution)/shard_map/ppermute | solution.py:282
  46.4 2.5 %collective-permute-start.4 = (bf16[1,128,128]{2,1,0:T(8,128)(2,1)S(1)}, bf16[1,128,128]{2,1,0:T(8,128)(2,1)S(1)}, u32[]{:S(2)}, u32[]{:S(2)}) collective-permute-start(bf16[1,128,128]{2,1,0:T(8,128)(2,1)S(1)} %get-tuple-element.35), channel_id=1, source_target_pairs={{0,2},{1,3},{2,4},{3,5},{4,6},{5,7},{6,8},{7,9},{8,10},{9,11},{10,... | collective-permute-start | bytes 98312 | tf_op jit(solution)/shard_map/ppermute | solution.py:282
  48.9 0.0 copy-done.1
  48.9 0.6 copy.28.mix_ref
  49.6 0.9 mixes.1.mixes0_ref
  50.4 4.4 %collective-permute-start.8 = (bf16[2,104,128]{2,1,0:T(8,128)(2,1)S(1)}, bf16[2,104,128]{2,1,0:T(8,128)(2,1)S(1)}, u32[]{:S(2)}, u32[]{:S(2)}) collective-permute-start(bf16[2,104,128]{2,1,0:T(8,128)(2,1)S(1)} %mixes.1.mixes0_ref), channel_id=1, source_target_pairs={{0,384},{128,0},{256,128},{384,256},{1,385},{129,1},{257,129},{385... | collective-permute-start | bytes 159752 | tf_op jit(solution)/shard_map/ppermute | solution.py:312
  54.8 0.0 collective-permute-done.5.right2_ref
  54.9 2.4 %collective-permute-start.7 = (bf16[2,104,128]{2,1,0:T(8,128)(2,1)S(1)}, bf16[2,104,128]{2,1,0:T(8,128)(2,1)S(1)}, u32[]{:S(2)}, u32[]{:S(2)}) collective-permute-start(bf16[2,104,128]{2,1,0:T(8,128)(2,1)S(1)} %mixes.1.mixes0_ref), channel_id=1, source_target_pairs={{0,256},{128,384},{256,0},{384,128},{1,257},{129,385},{257,1},{385... | collective-permute-start | bytes 159752 | tf_op jit(solution)/shard_map/ppermute | solution.py:312
  57.3 0.0 collective-permute-done.4.left2_ref
  57.3 2.5 %collective-permute-start.6 = (bf16[2,104,128]{2,1,0:T(8,128)(2,1)S(1)}, bf16[2,104,128]{2,1,0:T(8,128)(2,1)S(1)}, u32[]{:S(2)}, u32[]{:S(2)}) collective-permute-start(bf16[2,104,128]{2,1,0:T(8,128)(2,1)S(1)} %mixes.1.mixes0_ref), channel_id=1, source_target_pairs={{0,128},{128,256},{256,384},{384,0},{1,129},{129,257},{257,385},{3... | collective-permute-start | bytes 159752 | tf_op jit(solution)/shard_map/ppermute | solution.py:312
  59.8 0.0 collective-permute-done.8.mixes3_ref
  59.8 1.4 %collective-permute-done.7.mixes2_ref = bf16[2,104,128]{2,1,0:T(8,128)(2,1)S(1)} collective-permute-done((bf16[2,104,128]{2,1,0:T(8,128)(2,1)S(1)}, bf16[2,104,128]{2,1,0:T(8,128)(2,1)S(1)}, u32[]{:S(2)}, u32[]{:S(2)}) %collective-permute-start.7) | collective-permute-done | bytes 53280 | tf_op jit(solution)/shard_map/ppermute | solution.py:312
  61.2 2.1 %collective-permute-done.6.mixes1_ref = bf16[2,104,128]{2,1,0:T(8,128)(2,1)S(1)} collective-permute-done((bf16[2,104,128]{2,1,0:T(8,128)(2,1)S(1)}, bf16[2,104,128]{2,1,0:T(8,128)(2,1)S(1)}, u32[]{:S(2)}, u32[]{:S(2)}) %collective-permute-start.6) | collective-permute-done | bytes 53280 | tf_op jit(solution)/shard_map/ppermute | solution.py:312
  63.4 0.0 collective-permute-done.3.right_ref
  63.4 0.0 collective-permute-done.2.left_ref
  63.4 0.0 all-to-all-done
  63.4 20.5 %window.1 = (bf16[3,4,100,128]{3,2,1,0:T(8,128)(2,1)S(1)}, bf16[512,128]{1,0:T(8,128)(2,1)}) custom-call(s32[1]{0:T(128)} %bitcast.m_ref, bf16[4,144,128]{2,1,0:T(8,128)(2,1)S(1)} %pad_maximum_fusion.own_ref, bf16[4,144,128]{2,1,0:T(8,128)(2,1)S(1)} %collective-permute-done.2.left_ref, bf16[4,144,128]{2,1,0:T(8,128)(2,1)S(1)} %collective-permute-done.3.right_ref, ...), custom_call_target="tpu_custom_call" | custom-call | tf_op jit(solution)/shard_map/window/pallas_call | solution.py:314
  83.9 16.9 %all-to-all-start.1 = ((bf16[128,4,128]{2,1,0:T(4,128)(2,1)}), bf16[128,4,128]{2,1,0:T(4,128)(2,1)S(1)}, u32[]{:S(2)}, u32[]{:S(2)}) async-start(bf16[128,4,128]{2,1,0:T(4,128)(2,1)} %bitcast.13), calls=%async_computation.1 | async-start | bytes 262144 | tf_op jit(solution)/shard_map/all_to_all | solution.py:340
  100.8 0.8 copy.29
  101.6 0.7 copy.30
  102.3 12.0 %all-to-all-done.1 = bf16[128,4,128]{2,1,0:T(4,128)(2,1)S(1)} async-done(((bf16[128,4,128]{2,1,0:T(4,128)(2,1)}), bf16[128,4,128]{2,1,0:T(4,128)(2,1)S(1)}, u32[]{:S(2)}, u32[]{:S(2)}) %all-to-all-start.1) | async-done | bytes 131104 | tf_op jit(solution)/shard_map/all_to_all | solution.py:340
  114.3 1.8 %result.1 = (f32[100,256]{1,0:T(8,128)}, f32[8,8]{1,0:T(8,128)}, f32[1,8]{1,0:T(1,128)}) custom-call(bf16[512,128]{1,0:T(8,128)(2,1)S(1)} %bitcast.20, s32[1,256]{1,0:T(1,128)S(1)} %get-tuple-element.15.code_ref, f32[100,256]{1,0:T(8,128)} %bitcast.27, f32[100,256]{1,0:T(8,128)} %bitcast.29), custom_call_target="tpu_custom_call" | custom-call | tf_op jit(solution)/shard_map/result/pallas_call | solution.py:344
  (9 shorter events, 0.1 us)
Async XLA Ops:
  2.9 18.7 %copy-start.2 = (s32[4,128]{1,0:T(4,128)S(1)}, s32[4,128]{1,0:T(4,128)}, u32[]{:S(2)}) copy-start(s32[4,128]{1,0:T(4,128)} %param.13) | copy-start | bytes 6148
  2.9 18.7 %copy-start = (f32[100,4,128]{2,1,0:T(4,128)S(1)}, f32[100,4,128]{2,1,0:T(4,128)}, u32[]{:S(2)}) copy-start(f32[100,4,128]{2,1,0:T(4,128)} %param.12) | copy-start | bytes 614404
  2.9 60.4 %all-to-all-start = ((bf16[128,3,4,128]{3,2,1,0:T(4,128)(2,1)}), bf16[128,3,4,128]{3,2,1,0:T(4,128)(2,1)S(1)}, u32[]{:S(2)}, u32[]{:S(2)}) async-start(bf16[128,3,4,128]{3,2,1,0:T(4,128)(2,1)} %bitcast.8), calls=%async_computation | async-start | bytes 786432 | tf_op jit(solution)/shard_map/all_to_all | solution.py:297
  22.1 14.0 %collective-permute-start.1 = (bf16[4,8,128]{2,1,0:T(8,128)(2,1)S(1)}, bf16[4,8,128]{2,1,0:T(8,128)(2,1)S(1)}, u32[]{:S(2)}, u32[]{:S(2)}) collective-permute-start(bf16[4,8,128]{2,1,0:T(8,128)(2,1)S(1)} %get-tuple-element.36), channel_id=1, source_target_pairs={{32,0},{64,32},{96,64},{33,1},{65,33},{97,65},{34,2},{66,34},{98,6... | collective-permute-start | bytes 24584 | tf_op jit(solution)/shard_map/ppermute | solution.py:276
  24.8 11.3 %collective-permute-start = (bf16[4,8,128]{2,1,0:T(8,128)(2,1)S(1)}, bf16[4,8,128]{2,1,0:T(8,128)(2,1)S(1)}, u32[]{:S(2)}, u32[]{:S(2)}) collective-permute-start(bf16[4,8,128]{2,1,0:T(8,128)(2,1)S(1)} %get-tuple-element.37), channel_id=1, source_target_pairs={{0,32},{32,64},{64,96},{1,33},{33,65},{65,97},{2,34},{34,66},{66,9... | collective-permute-start | bytes 24584 | tf_op jit(solution)/shard_map/ppermute | solution.py:275
  36.3 12.6 %copy-start.1 = (bf16[2,100,100]{2,0,1:T(2,128)(2,1)S(1)}, bf16[2,100,100]{2,0,1:T(2,128)(2,1)}, u32[]{:S(2)}) copy-start(bf16[2,100,100]{2,0,1:T(2,128)(2,1)} %param.17) | copy-start | bytes 120004
  36.3 27.0 %collective-permute-start.3 = (bf16[4,144,128]{2,1,0:T(8,128)(2,1)S(1)}, bf16[4,144,128]{2,1,0:T(8,128)(2,1)S(1)}, u32[]{:S(2)}, u32[]{:S(2)}) collective-permute-start(bf16[4,144,128]{2,1,0:T(8,128)(2,1)S(1)} %pad_maximum_fusion.own_ref), channel_id=1, source_target_pairs={{0,31},{1,0},{2,1},{3,2},{4,3},{5,4},{6,5},{7,6},{8,7},{9,8},{10,9... | collective-permute-start | bytes 442376 | tf_op jit(solution)/shard_map/ppermute | solution.py:282
  40.7 22.7 %collective-permute-start.2 = (bf16[4,144,128]{2,1,0:T(8,128)(2,1)S(1)}, bf16[4,144,128]{2,1,0:T(8,128)(2,1)S(1)}, u32[]{:S(2)}, u32[]{:S(2)}) collective-permute-start(bf16[4,144,128]{2,1,0:T(8,128)(2,1)S(1)} %pad_maximum_fusion.own_ref), channel_id=1, source_target_pairs={{0,1},{1,2},{2,3},{3,4},{4,5},{5,6},{6,7},{7,8},{8,9},{9,10},{10,1... | collective-permute-start | bytes 442376 | tf_op jit(solution)/shard_map/ppermute | solution.py:282
  42.7 12.1 %collective-permute-start.5 = (bf16[1,128,128]{2,1,0:T(8,128)(2,1)S(1)}, bf16[1,128,128]{2,1,0:T(8,128)(2,1)S(1)}, u32[]{:S(2)}, u32[]{:S(2)}) collective-permute-start(bf16[1,128,128]{2,1,0:T(8,128)(2,1)S(1)} %get-tuple-element.34), channel_id=1, source_target_pairs={{0,30},{1,31},{2,0},{3,1},{4,2},{5,3},{6,4},{7,5},{8,6},{9,7},{10,... | collective-permute-start | bytes 98312 | tf_op jit(solution)/shard_map/ppermute | solution.py:282
  46.4 10.8 %collective-permute-start.4 = (bf16[1,128,128]{2,1,0:T(8,128)(2,1)S(1)}, bf16[1,128,128]{2,1,0:T(8,128)(2,1)S(1)}, u32[]{:S(2)}, u32[]{:S(2)}) collective-permute-start(bf16[1,128,128]{2,1,0:T(8,128)(2,1)S(1)} %get-tuple-element.35), channel_id=1, source_target_pairs={{0,2},{1,3},{2,4},{3,5},{4,6},{5,7},{6,8},{7,9},{8,10},{9,11},{10,... | collective-permute-start | bytes 98312 | tf_op jit(solution)/shard_map/ppermute | solution.py:282
  50.4 9.4 %collective-permute-start.8 = (bf16[2,104,128]{2,1,0:T(8,128)(2,1)S(1)}, bf16[2,104,128]{2,1,0:T(8,128)(2,1)S(1)}, u32[]{:S(2)}, u32[]{:S(2)}) collective-permute-start(bf16[2,104,128]{2,1,0:T(8,128)(2,1)S(1)} %mixes.1.mixes0_ref), channel_id=1, source_target_pairs={{0,384},{128,0},{256,128},{384,256},{1,385},{129,1},{257,129},{385... | collective-permute-start | bytes 159752 | tf_op jit(solution)/shard_map/ppermute | solution.py:312
  54.9 6.4 %collective-permute-start.7 = (bf16[2,104,128]{2,1,0:T(8,128)(2,1)S(1)}, bf16[2,104,128]{2,1,0:T(8,128)(2,1)S(1)}, u32[]{:S(2)}, u32[]{:S(2)}) collective-permute-start(bf16[2,104,128]{2,1,0:T(8,128)(2,1)S(1)} %mixes.1.mixes0_ref), channel_id=1, source_target_pairs={{0,256},{128,384},{256,0},{384,128},{1,257},{129,385},{257,1},{385... | collective-permute-start | bytes 159752 | tf_op jit(solution)/shard_map/ppermute | solution.py:312
  57.3 6.1 %collective-permute-start.6 = (bf16[2,104,128]{2,1,0:T(8,128)(2,1)S(1)}, bf16[2,104,128]{2,1,0:T(8,128)(2,1)S(1)}, u32[]{:S(2)}, u32[]{:S(2)}) collective-permute-start(bf16[2,104,128]{2,1,0:T(8,128)(2,1)S(1)} %mixes.1.mixes0_ref), channel_id=1, source_target_pairs={{0,128},{128,256},{256,384},{384,0},{1,129},{129,257},{257,385},{3... | collective-permute-start | bytes 159752 | tf_op jit(solution)/shard_map/ppermute | solution.py:312
  83.9 30.4 %all-to-all-start.1 = ((bf16[128,4,128]{2,1,0:T(4,128)(2,1)}), bf16[128,4,128]{2,1,0:T(4,128)(2,1)S(1)}, u32[]{:S(2)}, u32[]{:S(2)}) async-start(bf16[128,4,128]{2,1,0:T(4,128)(2,1)} %bitcast.13), calls=%async_computation.1 | async-start | bytes 262144 | tf_op jit(solution)/shard_map/all_to_all | solution.py:340

commit v6 on v5

--- a/solution.py
+++ b/solution.py
@@ -79,7 +79,7 @@
 
 
 def window_kernel(
-    m_ref, own_ref, left_ref, right_ref, left2_ref, right2_ref, recv_ref,
+    m_ref, lon_ref, own_ref, near0_ref, near1_ref, far0_ref, far1_ref, recv_ref,
     mixes0_ref, mixes1_ref, mixes2_ref, mixes3_ref,
     base_kh_ref, base_mix_ref,
     fields_ref, out_ref,
@@ -93,15 +93,19 @@
         start[column, body, :] = cells
         ocean[column] = jnp.broadcast_to(cells[:, K : K + 1], (ROWS, KP))
 
-    start[0, pl.ds(16, CY), :] = left2_ref[0].astype(F32)
-    start[13, pl.ds(16, CY), :] = right2_ref[0].astype(F32)
-    for place, ref in ((1, left_ref), (5, own_ref), (9, right_ref)):
-        for c in range(CX):
-            fill(place + c, ref[c])
+    near_side = 1 - lax.rem(lon_ref[0], 2)
+    far_side = 1 - lax.rem(lon_ref[0] // 2, 2)
+    start[13 * far_side, pl.ds(16, CY), :] = far0_ref[0].astype(F32)
+    start[13 * (1 - far_side), pl.ds(16, CY), :] = far1_ref[0].astype(F32)
+    for c in range(CX):
+        fill(5 + c, own_ref[c])
+        fill(1 + 8 * near_side + c, near0_ref[c])
+        fill(1 + 8 * (1 - near_side) + c, near1_ref[c])
     kh_pad[...] = jnp.zeros((16, KP), F32)
     mix_pad[...] = jnp.zeros((MEMBERS // 2, 2 * KP, 2 * KP), BF16)
-    for back, ref in enumerate((mixes0_ref, mixes1_ref, mixes2_ref, mixes3_ref)):
-        pair = lax.rem(m_ref[0] + 4 - back, 4)
+    turned = lax.rem(m_ref[0] + 2, 4)
+    sources = (m_ref[0], m_ref[0] + 1 - 2 * lax.rem(m_ref[0], 2), 3 - m_ref[0], turned)
+    for pair, ref in zip(sources, (mixes0_ref, mixes1_ref, mixes2_ref, mixes3_ref)):
         for half in range(2):
             spot = half * KP
             mix_pad[pair, spot : spot + K, spot : spot + KP] = ref[half, 0:K, :]
@@ -270,21 +274,29 @@
         ],
         2,
     )
-    up = [(i, i + 1) for i in range(lat_count - 1)]
-    down = [(i + 1, i) for i in range(lat_count - 1)]
-    below = lax.ppermute(cells[:, CY - HALO :], "lat", up)
-    above = lax.ppermute(cells[:, :HALO], "lat", down)
-    below = jnp.where(lat_at == 0, cells[:, :HALO][:, ::-1], below)
-    above = jnp.where(lat_at == lat_count - 1, cells[:, CY - HALO :][:, ::-1], above)
+    low, top = cells[:, :HALO], cells[:, CY - HALO :]
+    even = lat_at % 2 == 0
+    inner = [p for i in range(1, lat_count - 1, 2) for p in ((i, i + 1), (i + 1, i))]
+    outer = [p for i in range(0, lat_count, 2) for p in ((i, i + 1), (i + 1, i))]
+    at_inner = lax.ppermute(jnp.where(even, low, top), "lat", inner)
+    at_outer = lax.ppermute(jnp.where(even, top, low), "lat", outer)
+    at_inner = jnp.where(lat_at == 0, low[:, ::-1], at_inner)
+    at_inner = jnp.where(lat_at == lat_count - 1, top[:, ::-1], at_inner)
+    below, above = jnp.where(even, at_inner, at_outer), jnp.where(even, at_outer, at_inner)
     tall = jnp.concatenate([below, cells, above], 1)
 
-    def shift(x, by):
-        return lax.ppermute(x, "lon", [(i, (i + by) % lon_count) for i in range(lon_count)])
-
-    left2 = shift(cells[CX - 1 :], 2)
-    right2 = shift(cells[:1], -2)
-    left = shift(tall, 1)
-    right = shift(tall, -1)
+    def swap(x, first, by):
+        left = [i for i in range(lon_count) if (i // by) % 2 == first]
+        pairs = [(i, (i + by) % lon_count) for i in left]
+        return lax.ppermute(x, "lon", pairs + [(b, a) for a, b in pairs])
+
+    lon_at = lax.axis_index("lon").astype(jnp.int32).reshape(1)
+    second = lon_at[0] // 2 % 2
+    first_column, last_column = cells[:1], cells[CX - 1 :]
+    near0 = swap(tall, 0, 1)
+    near1 = swap(tall, 1, 1)
+    far0 = swap(jnp.where(second == 0, last_column, first_column), 0, 2)
+    far1 = swap(jnp.where(second == 0, first_column, last_column), 1, 2)
 
     send, code = pl.pallas_call(
         slots_kernel,
@@ -308,13 +320,13 @@
         name="mixes",
     )(pert_index, pert_table, member_mix)
     mixes = [own_mixes]
-    for back in range(1, 4):
-        mixes.append(lax.ppermute(own_mixes, "mem", [(i, (i + back) % 4) for i in range(4)]))
+    for partner in ((1, 0, 3, 2), (3, 2, 1, 0), (2, 3, 0, 1)):
+        mixes.append(lax.ppermute(own_mixes, "mem", list(enumerate(partner))))
 
     fields, back = pl.pallas_call(
         functools.partial(window_kernel, scale=1.0 / (OWN * REC * K)),
         out_shape=(VMEM((3, CX, K, CY), BF16), VMEM((OWN * CAP, KP), BF16)),
-        in_specs=smem(1) + vmem(12),
+        in_specs=smem(2) + vmem(12),
         out_specs=tuple(vmem(2)),
         scratch_shapes=[
             VMEM((14, ROWS + 16, KP), F32),
@@ -332,7 +344,7 @@
         ],
         name="window",
     )(
-        mem, near(tall), near(left), near(right), near(left2), near(right2), near(recv),
+        mem, lon_at, near(tall), near(near0), near(near1), near(far0), near(far1), near(recv),
         *map(near, mixes),
         base_kh.reshape(1, K), base_mix,
     )

time: 117 us -> 109 us (0.932)
  starting transfers between devices: 66.9 us -> 61.7 us
  waiting for transfers between devices: 20 us -> 15.3 us
    all_to_all x1, starting transfers between devices: 18.6 us -> 12.2 us  [on_device(): lax.all_to_all(send.reshape(OWN, 3, CAP, KP), owners, split_axis=0, conca...]
    ppermute x9, starting transfers between devices: 31.4 us -> 36.4 us  [the longest x4 16.4 us: swap(): return lax.ppermute(x, 'lon', pairs + [(b, a) for a, b in pairs])]
    ppermute x9, waiting for transfers between devices: 7.93 us -> 3.25 us  [the longest x3 3.23 us: on_device(): mixes.append(lax.ppermute(own_mixes, 'mem', list(enumerate(partner))))]
    all_to_all x1, starting transfers between devices: 16.9 us -> 13 us  [on_device(): lax.all_to_all(back.reshape(OWN, CAP, KP), owners, split_axis=0, concat_a...]
    unnamed x9 -> x7, local copies, waits for them, and re-layouts: 2.09 us -> 2.75 us
  transfers between devices with their start and end apart: 11 -> 11, of which waited for: 4 -> 3; matrix products, arithmetic and copies ran while one was open for 2% -> 2% of each run, Pallas kernels for 1% -> 3%
where the time goes in v6:
time: 109 us; the launch traced here: 108 us
  starting transfers between devices  61.7 us (57%)
  Pallas kernels  25.5 us (23%)
  waiting for transfers between devices  15.3 us (14%)
  local copies, waits for them, and re-layouts  3.18 us (3%)
  other arithmetic  1.35 us (1%)
    pallas_call x1, Pallas kernels, on_device(): pl.pallas_call(functools.partial(window_kernel, scale=1.0 / (OWN * REC *...  20.5 us
    ppermute x4, starting transfers between devices, swap(): return lax.ppermute(x, 'lon', pairs + [(b, a) for a, b in pairs])  16.4 us
    all_to_all x1, starting transfers between devices, on_device(): lax.all_to_all(back.reshape(OWN, CAP, KP), owners, split_axis=0, concat_a...  13 us
    all_to_all x1, starting transfers between devices, on_device(): lax.all_to_all(send.reshape(OWN, 3, CAP, KP), owners, split_axis=0, conca...  12.2 us
    all_to_all x1, waiting for transfers between devices, on_device(): lax.all_to_all(back.reshape(OWN, CAP, KP), owners, split_axis=0, concat_a...  12 us
    ppermute x3, starting transfers between devices, on_device(): mixes.append(lax.ppermute(own_mixes, 'mem', list(enumerate(partner))))  9.33 us
    ppermute x1, starting transfers between devices, on_device(): at_outer = lax.ppermute(jnp.where(even, top, low), 'lat', outer)  8.75 us
    ppermute x3, waiting for transfers between devices, on_device(): mixes.append(lax.ppermute(own_mixes, 'mem', list(enumerate(partner))))  3.23 us
  transfers between devices with their start and end apart: 11, of which 3 were waited for; matrix products, arithmetic and copies ran while one was open for 2% of the time, Pallas kernels for 3%

profile of v6, /device:TPU:1, one launch (start us, length us, event | category | flops | bytes accessed | tf_op | source)
XLA Modules:
  0.0 107.9 jit_solution(14879262526730479165)
XLA Ops:
  0.6 0.0 copy-start.1
  0.7 0.7 copy-done.1
  1.3 1.0 convert_element_type.9
  2.3 0.2 copy.26
  2.5 0.2 copy.27
  2.7 0.1 broadcast_select_fusion.5
  2.8 8.7 %collective-permute-start.1 = (bf16[4,8,128]{2,1,0:T(8,128)(2,1)S(1)}, bf16[4,8,128]{2,1,0:T(8,128)(2,1)S(1)}, u32[]{:S(2)}, u32[]{:S(2)}) collective-permute-start(bf16[4,8,128]{2,1,0:T(8,128)(2,1)S(1)} %broadcast_select_fusion.4), channel_id=1, source_target_pairs={{0,32},{32,0},{64,96},{96,64},{1,33},{33,1},{65,97},{97,65},{2,34}... | collective-permute-start | bytes 24584 | tf_op jit(solution)/shard_map/ppermute | solution.py:282
  11.5 2.0 %collective-permute-start = (bf16[4,8,128]{2,1,0:T(8,128)(2,1)S(1)}, bf16[4,8,128]{2,1,0:T(8,128)(2,1)S(1)}, u32[]{:S(2)}, u32[]{:S(2)}) collective-permute-start(bf16[4,8,128]{2,1,0:T(8,128)(2,1)S(1)} %get-tuple-element.39), channel_id=1, source_target_pairs={{32,64},{64,32},{33,65},{65,33},{34,66},{66,34},{35,67},{67,35},{3... | collective-permute-start | bytes 24584 | tf_op jit(solution)/shard_map/ppermute | solution.py:281
  13.5 2.3 %slots.1 = (bf16[1536,128]{1,0:T(8,128)(2,1)}, s32[1,256]{1,0:T(1,128)S(1)}) custom-call(s32[1,256]{1,0:T(1,128)} %bitcast.32, s32[1,256]{1,0:T(1,128)} %bitcast.33, f32[100,256]{1,0:T(8,128)} %bitcast.27, f32[100,256]{1,0:T(8,128)} %bitcast.31, f32[100,256]{1,0:T(8,128)} %bitcast.29), custom_call_target="tpu_custom_call" | custom-call | tf_op jit(solution)/shard_map/slots/pallas_call | solution.py:301
  15.9 12.2 %all-to-all-start = ((bf16[128,3,4,128]{3,2,1,0:T(4,128)(2,1)}), bf16[128,3,4,128]{3,2,1,0:T(4,128)(2,1)S(1)}, u32[]{:S(2)}, u32[]{:S(2)}) async-start(bf16[128,3,4,128]{3,2,1,0:T(4,128)(2,1)} %bitcast.9), calls=%async_computation | async-start | bytes 786432 | tf_op jit(solution)/shard_map/all_to_all | solution.py:309
  28.1 0.1 broadcast_select_fusion
  28.3 0.0 collective-permute-done.1
  28.3 0.0 collective-permute-done
  28.3 0.1 pad_maximum_fusion.own_ref
  28.5 7.4 %collective-permute-start.3 = (bf16[4,144,128]{2,1,0:T(8,128)(2,1)S(1)}, bf16[4,144,128]{2,1,0:T(8,128)(2,1)S(1)}, u32[]{:S(2)}, u32[]{:S(2)}) collective-permute-start(bf16[4,144,128]{2,1,0:T(8,128)(2,1)S(1)} %pad_maximum_fusion.own_ref), channel_id=1, source_target_pairs={{1,2},{3,4},{5,6},{7,8},{9,10},{11,12},{13,14},{15,16},{17,18},{19... | collective-permute-start | bytes 442376 | tf_op jit(solution)/shard_map/ppermute | solution.py:291
  35.9 1.9 %collective-permute-start.2 = (bf16[4,144,128]{2,1,0:T(8,128)(2,1)S(1)}, bf16[4,144,128]{2,1,0:T(8,128)(2,1)S(1)}, u32[]{:S(2)}, u32[]{:S(2)}) collective-permute-start(bf16[4,144,128]{2,1,0:T(8,128)(2,1)S(1)} %pad_maximum_fusion.own_ref), channel_id=1, source_target_pairs={{0,1},{2,3},{4,5},{6,7},{8,9},{10,11},{12,13},{14,15},{16,17},{18,... | collective-permute-start | bytes 442376 | tf_op jit(solution)/shard_map/ppermute | solution.py:291
  37.8 0.0 copy-start
  37.8 1.9 %collective-permute-start.4 = (bf16[1,128,128]{2,1,0:T(8,128)(2,1)S(1)}, bf16[1,128,128]{2,1,0:T(8,128)(2,1)S(1)}, u32[]{:S(2)}, u32[]{:S(2)}) collective-permute-start(bf16[1,128,128]{2,1,0:T(8,128)(2,1)S(1)} %broadcast_select_fusion.1), channel_id=1, source_target_pairs={{0,2},{1,3},{4,6},{5,7},{8,10},{9,11},{12,14},{13,15},{16,18},{17,... | collective-permute-start | bytes 98312 | tf_op jit(solution)/shard_map/ppermute | solution.py:291
  39.8 5.1 %collective-permute-start.5 = (bf16[1,128,128]{2,1,0:T(8,128)(2,1)S(1)}, bf16[1,128,128]{2,1,0:T(8,128)(2,1)S(1)}, u32[]{:S(2)}, u32[]{:S(2)}) collective-permute-start(bf16[1,128,128]{2,1,0:T(8,128)(2,1)S(1)} %get-tuple-element.34), channel_id=1, source_target_pairs={{2,4},{3,5},{6,8},{7,9},{10,12},{11,13},{14,16},{15,17},{18,20},{1... | collective-permute-start | bytes 98312 | tf_op jit(solution)/shard_map/ppermute | solution.py:291
  44.9 0.0 copy-done
  44.9 0.6 copy.28.mix_ref
  45.5 0.9 mixes.1.mixes0_ref
  46.4 4.6 %collective-permute-start.8 = (bf16[2,104,128]{2,1,0:T(8,128)(2,1)S(1)}, bf16[2,104,128]{2,1,0:T(8,128)(2,1)S(1)}, u32[]{:S(2)}, u32[]{:S(2)}) collective-permute-start(bf16[2,104,128]{2,1,0:T(8,128)(2,1)S(1)} %mixes.1.mixes0_ref), channel_id=1, source_target_pairs={{0,256},{128,384},{256,0},{384,128},{1,257},{129,385},{257,1},{385... | collective-permute-start | bytes 159752 | tf_op jit(solution)/shard_map/ppermute | solution.py:324
  51.0 0.0 collective-permute-done.4.far0_ref
  51.1 2.8 %collective-permute-start.7 = (bf16[2,104,128]{2,1,0:T(8,128)(2,1)S(1)}, bf16[2,104,128]{2,1,0:T(8,128)(2,1)S(1)}, u32[]{:S(2)}, u32[]{:S(2)}) collective-permute-start(bf16[2,104,128]{2,1,0:T(8,128)(2,1)S(1)} %mixes.1.mixes0_ref), channel_id=1, source_target_pairs={{0,384},{128,256},{256,128},{384,0},{1,385},{129,257},{257,129},{3... | collective-permute-start | bytes 159752 | tf_op jit(solution)/shard_map/ppermute | solution.py:324
  53.8 0.0 collective-permute-done.5.far1_ref
  53.8 1.9 %collective-permute-start.6 = (bf16[2,104,128]{2,1,0:T(8,128)(2,1)S(1)}, bf16[2,104,128]{2,1,0:T(8,128)(2,1)S(1)}, u32[]{:S(2)}, u32[]{:S(2)}) collective-permute-start(bf16[2,104,128]{2,1,0:T(8,128)(2,1)S(1)} %mixes.1.mixes0_ref), channel_id=1, source_target_pairs={{0,128},{128,0},{256,384},{384,256},{1,129},{129,1},{257,385},{385... | collective-permute-start | bytes 159752 | tf_op jit(solution)/shard_map/ppermute | solution.py:324
  55.8 0.0 collective-permute-done.8.mixes3_ref
  55.8 1.4 %collective-permute-done.7.mixes2_ref = bf16[2,104,128]{2,1,0:T(8,128)(2,1)S(1)} collective-permute-done((bf16[2,104,128]{2,1,0:T(8,128)(2,1)S(1)}, bf16[2,104,128]{2,1,0:T(8,128)(2,1)S(1)}, u32[]{:S(2)}, u32[]{:S(2)}) %collective-permute-start.7) | collective-permute-done | bytes 53280 | tf_op jit(solution)/shard_map/ppermute | solution.py:324
  57.1 1.9 %collective-permute-done.6.mixes1_ref = bf16[2,104,128]{2,1,0:T(8,128)(2,1)S(1)} collective-permute-done((bf16[2,104,128]{2,1,0:T(8,128)(2,1)S(1)}, bf16[2,104,128]{2,1,0:T(8,128)(2,1)S(1)}, u32[]{:S(2)}, u32[]{:S(2)}) %collective-permute-start.6) | collective-permute-done | bytes 53280 | tf_op jit(solution)/shard_map/ppermute | solution.py:324
  59.0 0.0 collective-permute-done.3.near1_ref
  59.0 0.0 collective-permute-done.2.near0_ref
  59.0 0.0 all-to-all-done
  59.0 20.5 %window.1 = (bf16[3,4,100,128]{3,2,1,0:T(8,128)(2,1)S(1)}, bf16[512,128]{1,0:T(8,128)(2,1)}) custom-call(s32[1]{0:T(128)} %bitcast.m_ref, s32[1]{0:T(128)} %bitcast.1.lon_ref, bf16[4,144,128]{2,1,0:T(8,128)(2,1)S(1)} %pad_maximum_fusion.own_ref, bf16[4,144,128]{2,1,0:T(8,128)(2,1)S(1)} %collective-permute-done.2.near0_ref, ...), custom_call_target="tpu_custom_call" | custom-call | tf_op jit(solution)/shard_map/window/pallas_call | solution.py:326
  79.5 13.0 %all-to-all-start.1 = ((bf16[128,4,128]{2,1,0:T(4,128)(2,1)}), bf16[128,4,128]{2,1,0:T(4,128)(2,1)S(1)}, u32[]{:S(2)}, u32[]{:S(2)}) async-start(bf16[128,4,128]{2,1,0:T(4,128)(2,1)} %bitcast.14), calls=%async_computation.1 | async-start | bytes 262144 | tf_op jit(solution)/shard_map/all_to_all | solution.py:352
  92.6 0.8 copy.29
  93.3 0.7 copy.30
  94.0 12.0 %all-to-all-done.1 = bf16[128,4,128]{2,1,0:T(4,128)(2,1)S(1)} async-done(((bf16[128,4,128]{2,1,0:T(4,128)(2,1)}), bf16[128,4,128]{2,1,0:T(4,128)(2,1)S(1)}, u32[]{:S(2)}, u32[]{:S(2)}) %all-to-all-start.1) | async-done | bytes 131104 | tf_op jit(solution)/shard_map/all_to_all | solution.py:352
  106.0 1.8 %result.1 = (f32[100,256]{1,0:T(8,128)}, f32[8,8]{1,0:T(8,128)}, f32[1,8]{1,0:T(1,128)}) custom-call(bf16[512,128]{1,0:T(8,128)(2,1)S(1)} %bitcast.21, s32[1,256]{1,0:T(1,128)S(1)} %get-tuple-element.15.code_ref, f32[100,256]{1,0:T(8,128)} %bitcast.28, f32[100,256]{1,0:T(8,128)} %bitcast.30), custom_call_target="tpu_custom_call" | custom-call | tf_op jit(solution)/shard_map/result/pallas_call | solution.py:356
  (10 shorter events, 0.1 us)
Async XLA Ops:
  0.6 0.7 copy-start.1
  2.8 25.5 %collective-permute-start.1 = (bf16[4,8,128]{2,1,0:T(8,128)(2,1)S(1)}, bf16[4,8,128]{2,1,0:T(8,128)(2,1)S(1)}, u32[]{:S(2)}, u32[]{:S(2)}) collective-permute-start(bf16[4,8,128]{2,1,0:T(8,128)(2,1)S(1)} %broadcast_select_fusion.4), channel_id=1, source_target_pairs={{0,32},{32,0},{64,96},{96,64},{1,33},{33,1},{65,97},{97,65},{2,34}... | collective-permute-start | bytes 24584 | tf_op jit(solution)/shard_map/ppermute | solution.py:282
  11.5 16.8 %collective-permute-start = (bf16[4,8,128]{2,1,0:T(8,128)(2,1)S(1)}, bf16[4,8,128]{2,1,0:T(8,128)(2,1)S(1)}, u32[]{:S(2)}, u32[]{:S(2)}) collective-permute-start(bf16[4,8,128]{2,1,0:T(8,128)(2,1)S(1)} %get-tuple-element.39), channel_id=1, source_target_pairs={{32,64},{64,32},{33,65},{65,33},{34,66},{66,34},{35,67},{67,35},{3... | collective-permute-start | bytes 24584 | tf_op jit(solution)/shard_map/ppermute | solution.py:281
  15.9 43.2 %all-to-all-start = ((bf16[128,3,4,128]{3,2,1,0:T(4,128)(2,1)}), bf16[128,3,4,128]{3,2,1,0:T(4,128)(2,1)S(1)}, u32[]{:S(2)}, u32[]{:S(2)}) async-start(bf16[128,3,4,128]{3,2,1,0:T(4,128)(2,1)} %bitcast.9), calls=%async_computation | async-start | bytes 786432 | tf_op jit(solution)/shard_map/all_to_all | solution.py:309
  28.5 30.5 %collective-permute-start.3 = (bf16[4,144,128]{2,1,0:T(8,128)(2,1)S(1)}, bf16[4,144,128]{2,1,0:T(8,128)(2,1)S(1)}, u32[]{:S(2)}, u32[]{:S(2)}) collective-permute-start(bf16[4,144,128]{2,1,0:T(8,128)(2,1)S(1)} %pad_maximum_fusion.own_ref), channel_id=1, source_target_pairs={{1,2},{3,4},{5,6},{7,8},{9,10},{11,12},{13,14},{15,16},{17,18},{19... | collective-permute-start | bytes 442376 | tf_op jit(solution)/shard_map/ppermute | solution.py:291
  35.9 23.2 %collective-permute-start.2 = (bf16[4,144,128]{2,1,0:T(8,128)(2,1)S(1)}, bf16[4,144,128]{2,1,0:T(8,128)(2,1)S(1)}, u32[]{:S(2)}, u32[]{:S(2)}) collective-permute-start(bf16[4,144,128]{2,1,0:T(8,128)(2,1)S(1)} %pad_maximum_fusion.own_ref), channel_id=1, source_target_pairs={{0,1},{2,3},{4,5},{6,7},{8,9},{10,11},{12,13},{14,15},{16,17},{18,... | collective-permute-start | bytes 442376 | tf_op jit(solution)/shard_map/ppermute | solution.py:291
  37.8 7.1 %copy-start = (bf16[2,100,100]{2,0,1:T(2,128)(2,1)S(1)}, bf16[2,100,100]{2,0,1:T(2,128)(2,1)}, u32[]{:S(2)}) copy-start(bf16[2,100,100]{2,0,1:T(2,128)(2,1)} %param.17) | copy-start | bytes 120004
  37.8 13.2 %collective-permute-start.4 = (bf16[1,128,128]{2,1,0:T(8,128)(2,1)S(1)}, bf16[1,128,128]{2,1,0:T(8,128)(2,1)S(1)}, u32[]{:S(2)}, u32[]{:S(2)}) collective-permute-start(bf16[1,128,128]{2,1,0:T(8,128)(2,1)S(1)} %broadcast_select_fusion.1), channel_id=1, source_target_pairs={{0,2},{1,3},{4,6},{5,7},{8,10},{9,11},{12,14},{13,15},{16,18},{17,... | collective-permute-start | bytes 98312 | tf_op jit(solution)/shard_map/ppermute | solution.py:291
  39.8 14.1 %collective-permute-start.5 = (bf16[1,128,128]{2,1,0:T(8,128)(2,1)S(1)}, bf16[1,128,128]{2,1,0:T(8,128)(2,1)S(1)}, u32[]{:S(2)}, u32[]{:S(2)}) collective-permute-start(bf16[1,128,128]{2,1,0:T(8,128)(2,1)S(1)} %get-tuple-element.34), channel_id=1, source_target_pairs={{2,4},{3,5},{6,8},{7,9},{10,12},{11,13},{14,16},{15,17},{18,20},{1... | collective-permute-start | bytes 98312 | tf_op jit(solution)/shard_map/ppermute | solution.py:291
  46.4 9.4 %collective-permute-start.8 = (bf16[2,104,128]{2,1,0:T(8,128)(2,1)S(1)}, bf16[2,104,128]{2,1,0:T(8,128)(2,1)S(1)}, u32[]{:S(2)}, u32[]{:S(2)}) collective-permute-start(bf16[2,104,128]{2,1,0:T(8,128)(2,1)S(1)} %mixes.1.mixes0_ref), channel_id=1, source_target_pairs={{0,256},{128,384},{256,0},{384,128},{1,257},{129,385},{257,1},{385... | collective-permute-start | bytes 159752 | tf_op jit(solution)/shard_map/ppermute | solution.py:324
  51.1 6.1 %collective-permute-start.7 = (bf16[2,104,128]{2,1,0:T(8,128)(2,1)S(1)}, bf16[2,104,128]{2,1,0:T(8,128)(2,1)S(1)}, u32[]{:S(2)}, u32[]{:S(2)}) collective-permute-start(bf16[2,104,128]{2,1,0:T(8,128)(2,1)S(1)} %mixes.1.mixes0_ref), channel_id=1, source_target_pairs={{0,384},{128,256},{256,128},{384,0},{1,385},{129,257},{257,129},{3... | collective-permute-start | bytes 159752 | tf_op jit(solution)/shard_map/ppermute | solution.py:324
  53.8 5.2 %collective-permute-start.6 = (bf16[2,104,128]{2,1,0:T(8,128)(2,1)S(1)}, bf16[2,104,128]{2,1,0:T(8,128)(2,1)S(1)}, u32[]{:S(2)}, u32[]{:S(2)}) collective-permute-start(bf16[2,104,128]{2,1,0:T(8,128)(2,1)S(1)} %mixes.1.mixes0_ref), channel_id=1, source_target_pairs={{0,128},{128,0},{256,384},{384,256},{1,129},{129,1},{257,385},{385... | collective-permute-start | bytes 159752 | tf_op jit(solution)/shard_map/ppermute | solution.py:324
  79.5 26.5 %all-to-all-start.1 = ((bf16[128,4,128]{2,1,0:T(4,128)(2,1)}), bf16[128,4,128]{2,1,0:T(4,128)(2,1)S(1)}, u32[]{:S(2)}, u32[]{:S(2)}) async-start(bf16[128,4,128]{2,1,0:T(4,128)(2,1)} %bitcast.14), calls=%async_computation.1 | async-start | bytes 262144 | tf_op jit(solution)/shard_map/all_to_all | solution.py:352
